TPU v7x, 256 devices: a whole 4x4x8 slice. The times are simulated.
256 devices in a mesh: docs: 64 (over y, z, core), mp: 4 (over x).
Axes of the slice: x: 4, y: 4, z: 8, core: 2. Of those that a mesh axis runs over, the one named last changes fastest.
Arguments:
- queries: bfloat16 [16384, 8192], P('docs', 'mp'), may hold values from -8 to 8
- keys: bfloat16 [204928, 1024], P('docs', 'mp'), may hold values from -6 to 6
- values: bfloat16 [204928, 1024], P('docs', 'mp'), may hold values from -9 to 9
- owner_of_row: int32 [16384, 1], P('docs'), may hold values from 0 to 63; in each aligned block of 256 rows (0 to 255, 256 to 511, ...) at most 6 rows name the same one
- visible: int32 [16384], P('docs'), may hold values from 1 to 2
- gain: bfloat16 [8192], P('mp'), may hold values from 0.099609375 to 1.8984375
Outputs:
- attended: bfloat16 [16384, 8192], P('docs', 'mp')
Inputs may be any that keep to these rules, and one draw needn't show every extreme that they name: `owner_of_row`: among the rows of one index of docs (aligned blocks of 256 rows), no owner is named by more than 6 rows, a bound that some block reaches.
All inputs are finite; a program needn't handle non-finite values.
Results may differ from a plain program's by a relative error of at most 0.0056.
Values may be sent and summed in bfloat16 or wider, within the bound.
A program may use at most 64 MiB of HBM per device.

v0:
```python
import math

import jax
import jax.numpy as jnp
from jax import lax
from jax.sharding import PartitionSpec as P

HD = 128
IMG_TOK = 1601
D = 8192
GROUP = 8


def rescale(context, power, gain):
    wide = context.astype(jnp.float32)
    factor = lax.rsqrt(power / D + 1e-05)
    return (wide * factor[..., None] * gain.astype(jnp.float32)).astype(jnp.bfloat16)


def squares(context):
    wide = context.astype(jnp.float32)
    return jnp.sum(wide * wide, axis=-1)


def shards(queries, keys, values, owner_of_row, visible, gain):
    docs = lax.axis_size("docs")
    rows = queries.shape[0]
    width = queries.shape[1]
    cap = max(2, 3 * rows // (2 * docs))
    kv_local = keys.shape[1] // HD
    scale = 1.0 / HD**0.5
    route = owner_of_row[:, 0]
    onehot = (route[:, None] == jnp.arange(docs, dtype=jnp.int32)[None, :]).astype(jnp.int32)
    before = jnp.cumsum(onehot, axis=0) - onehot
    rank = jnp.sum(before * onehot, axis=1)
    target = route * cap + rank
    place = (jnp.arange(docs * cap, dtype=jnp.int32)[:, None] == target[None, :]).astype(
        jnp.bfloat16
    )
    packed = jnp.dot(place, queries, preferred_element_type=jnp.float32).astype(jnp.bfloat16)
    packed = packed.reshape(docs, cap, width)
    seen_packed = jnp.dot(place, visible.astype(jnp.bfloat16), preferred_element_type=jnp.float32)
    seen_packed = seen_packed.astype(jnp.bfloat16).reshape(docs, cap)
    key_grid = keys.reshape(-1, kv_local, HD)
    value_grid = values.reshape(-1, kv_local, HD)
    token_image = (jnp.arange(keys.shape[0]) // IMG_TOK).astype(jnp.float32)

    def one_block(pieces):
        block_q, block_seen = pieces
        scores = (
            jnp.einsum("bkgd,tkd->bkgt", block_q, key_grid, preferred_element_type=jnp.float32)
            * scale
        )
        allowed = token_image[None, :] < block_seen.astype(jnp.float32)[:, None]
        scores = jnp.where(allowed[:, None, None, :], scores, jnp.float32(-1e30))
        top = jnp.max(scores, axis=-1, keepdims=True)
        weights = jnp.exp(scores - top)
        total = jnp.sum(weights, axis=-1)
        probs = weights.astype(jnp.bfloat16)
        context = jnp.einsum(
            "bkgt,tkd->bkgd", probs, value_grid, preferred_element_type=jnp.float32
        )
        context = context / total[..., None]
        return context.astype(jnp.bfloat16).reshape(block_q.shape[0], width)

    arrived, arrived_seen = (
        lax.all_to_all(packed, "docs", split_axis=0, concat_axis=0, tiled=True),
        lax.all_to_all(seen_packed, "docs", split_axis=0, concat_axis=0, tiled=True),
    )
    flat_q = arrived.reshape(-1, kv_local, GROUP, HD)
    flat_seen = arrived_seen.reshape(-1)
    count = flat_q.shape[0]
    block = math.gcd(count, 64)
    blocks = count // block
    result = lax.map(
        one_block,
        (flat_q.reshape(blocks, block, kv_local, GROUP, HD), flat_seen.reshape(blocks, block)),
    )
    context = result.reshape(arrived.shape)
    returned = lax.all_to_all(context, "docs", split_axis=0, concat_axis=0, tiled=True)
    flat_back = returned.reshape(docs * cap, width)
    mine = jnp.einsum("sr,sc->rc", place, flat_back, preferred_element_type=jnp.float32).astype(
        jnp.bfloat16
    )
    power = lax.psum(squares(mine), "mp")
    return rescale(mine, power, gain)


def solution(mesh):
    return jax.shard_map(
        shards,
        mesh=mesh,
        in_specs=(
            P("docs", "mp"),
            P("docs", "mp"),
            P("docs", "mp"),
            P("docs", None),
            P("docs"),
            P("mp"),
        ),
        out_specs=P("docs", "mp"),
        check_vma=False,
    )
```

profile of v0, /device:TPU:1, one launch (start us, length us, event | category | flops | bytes accessed | tf_op | source)
XLA Modules:
  0.0 249.5 jit_solution(762418849368403308)
XLA Ops:
  4.8 13.2 %all-to-all-start = ((bf16[64,1,6]{2,1,0:T(2,128)(2,1)}), bf16[64,1,6]{2,1,0:T(2,128)(2,1)S(1)}, u32[]{:S(2)}, u32[]{:S(2)}) async-start(bf16[64,1,6]{2,1,0:T(2,128)(2,1)} %all_to_all.16), calls=%async_computation | async-start | bytes 65536 | tf_op jit(solution)/shard_map/all_to_all | solution.py:68
  20.1 7.0 %all-to-all-done = bf16[64,1,6]{2,1,0:T(2,128)(2,1)S(1)} async-done(((bf16[64,1,6]{2,1,0:T(2,128)(2,1)}), bf16[64,1,6]{2,1,0:T(2,128)(2,1)S(1)}, u32[]{:S(2)}, u32[]{:S(2)}) %all-to-all-start) | async-done | bytes 800 | tf_op jit(solution)/shard_map/all_to_all | solution.py:68
  27.1 5.6 %all-to-all-start.1 = ((bf16[64,6,2048]{2,1,0:T(8,128)(2,1)}), bf16[64,6,2048]{2,1,0:T(8,128)(2,1)}, u32[]{:S(2)}, u32[]{:S(2)}) async-start(bf16[64,6,2048]{2,1,0:T(8,128)(2,1)} %reshape.81), calls=%async_computation.1 | async-start | bytes 4194304 | tf_op jit(solution)/shard_map/all_to_all | solution.py:67
  45.9 38.1 %all-to-all-done.1 = bf16[64,6,2048]{2,1,0:T(8,128)(2,1)} async-done(((bf16[64,6,2048]{2,1,0:T(8,128)(2,1)}), bf16[64,6,2048]{2,1,0:T(8,128)(2,1)}, u32[]{:S(2)}, u32[]{:S(2)}) %all-to-all-start.1) | async-done | bytes 1572896 | tf_op jit(solution)/shard_map/all_to_all | solution.py:67
  84.0 4.3 %reshape_reshape.7 = bf16[6,64,2,8,128]{4,3,2,1,0:T(8,128)(2,1)} reshape(bf16[64,6,2048]{2,1,0:T(8,128)(2,1)} %all-to-all-done.1) | data formatting | bytes 3145728 | tf_op jit(solution)/shard_map/reshape;reshape | solution.py:77
  88.3 86.8 %while.11 = (s32[]{:T(128)}, bf16[6,64,2048]{2,1,0:T(8,128)(2,1)}, bf16[6,64]{1,0:T(8,128)(2,1)S(1)}, bf16[6,64,2,8,128]{4,3,2,1,0:T(8,128)(2,1)}, bf16[3202,2,1...) while((s32[]{:T(128)}, bf16[6,64,2048]{2,1,0:T(8,128)(2,1)}, ...), condition=%wide.region_6.7_spmd.clone, body=%wide.region_3.6_spmd.clone.sunk | while | flops 1715331328 | bytes 52147452 | solution.py:75
  88.5 4.6 %bitcast_reduce_fusion.2 = (f32[64,2,8]{2,0,1:T(8,128)S(1)}, f32[2,64,8,3202]{3,2,1,0:T(8,128)S(1)}) fusion(pred[64,3202]{1,0:T(8,128)(4,1)S(1)} %broadcast_compare_fusion.2, bf16[3202,2,128]{2,0,1:T(8,128)(2,1)S(1)} %get-tuple-element.144, bf16[6,64,2,8,128]{4,3,2,1,0:T(8,128)(2,1)} %get-tuple-element.143, s32[]{:T(128)} %get-tuple-element.133), kind=kOutput, calls=%fused_computation.2.clone.1 | convolution fusion | flops 849220608 | bytes 15226496 | tf_op jit(solution)/shard_map/while/body/eval_jaxpr/bkgd,tkd->bkgt/dot_general | solution.py:51
  93.1 4.3 %fusion.57 = f32[64,2,8]{2,0,1:T(8,128)S(1)} fusion(f32[2,64,8,3202]{3,2,1,0:T(8,128)S(1)} %get-tuple-element.124, f32[64,2,8]{2,0,1:T(8,128)S(1)} %get-tuple-element.125, pred[64,3202]{1,0:T(8,128)(4,1)S(1)} %broadcast_compare_fusion.2), kind=kLoop, calls=%fused_computation.5.clone.1 | loop fusion | flops 13114368 | bytes 13328512 | tf_op jit(solution)/shard_map/while/body/eval_jaxpr/reduce_sum | solution.py:58
  97.4 4.5 %fusion.58 = bf16[64,2,8,128]{3,2,0,1:T(8,128)(2,1)S(1)} fusion(bf16[3202,2,128]{2,0,1:T(8,128)(2,1)S(1)} %copy-done.2, f32[2,64,8,3202]{3,2,1,0:T(8,128)S(1)} %get-tuple-element.124, f32[64,2,8]{2,0,1:T(8,128)S(1)} %get-tuple-element.125, pred[64,3202]{1,0:T(8,128)(4,1)S(1)} %broadcast_compare_fusion.2, f32[64,2,8]{2,0,1:T(8,128)S(1)} %fusion.57), kind=kOutput, calls=%fused_computation.14.clone.1 | convolution fusion | flops 852762624 | bytes 15230080 | tf_op jit(solution)/shard_map/while/body/eval_jaxpr/bkgt,tkd->bkgd/dot_general | solution.py:60
  103.0 4.6 %bitcast_reduce_fusion.2 = (f32[64,2,8]{2,0,1:T(8,128)S(1)}, f32[2,64,8,3202]{3,2,1,0:T(8,128)S(1)}) fusion(pred[64,3202]{1,0:T(8,128)(4,1)S(1)} %broadcast_compare_fusion.2, bf16[3202,2,128]{2,0,1:T(8,128)(2,1)S(1)} %get-tuple-element.144, bf16[6,64,2,8,128]{4,3,2,1,0:T(8,128)(2,1)} %get-tuple-element.143, s32[]{:T(128)} %get-tuple-element.133), kind=kOutput, calls=%fused_computation.2.clone.1 | convolution fusion | flops 849220608 | bytes 15226496 | tf_op jit(solution)/shard_map/while/body/eval_jaxpr/bkgd,tkd->bkgt/dot_general | solution.py:51
  107.6 4.3 %fusion.57 = f32[64,2,8]{2,0,1:T(8,128)S(1)} fusion(f32[2,64,8,3202]{3,2,1,0:T(8,128)S(1)} %get-tuple-element.124, f32[64,2,8]{2,0,1:T(8,128)S(1)} %get-tuple-element.125, pred[64,3202]{1,0:T(8,128)(4,1)S(1)} %broadcast_compare_fusion.2), kind=kLoop, calls=%fused_computation.5.clone.1 | loop fusion | flops 13114368 | bytes 13328512 | tf_op jit(solution)/shard_map/while/body/eval_jaxpr/reduce_sum | solution.py:58
  111.8 4.5 %fusion.58 = bf16[64,2,8,128]{3,2,0,1:T(8,128)(2,1)S(1)} fusion(bf16[3202,2,128]{2,0,1:T(8,128)(2,1)S(1)} %copy-done.2, f32[2,64,8,3202]{3,2,1,0:T(8,128)S(1)} %get-tuple-element.124, f32[64,2,8]{2,0,1:T(8,128)S(1)} %get-tuple-element.125, pred[64,3202]{1,0:T(8,128)(4,1)S(1)} %broadcast_compare_fusion.2, f32[64,2,8]{2,0,1:T(8,128)S(1)} %fusion.57), kind=kOutput, calls=%fused_computation.14.clone.1 | convolution fusion | flops 852762624 | bytes 15230080 | tf_op jit(solution)/shard_map/while/body/eval_jaxpr/bkgt,tkd->bkgd/dot_general | solution.py:60
  117.4 4.6 %bitcast_reduce_fusion.2 = (f32[64,2,8]{2,0,1:T(8,128)S(1)}, f32[2,64,8,3202]{3,2,1,0:T(8,128)S(1)}) fusion(pred[64,3202]{1,0:T(8,128)(4,1)S(1)} %broadcast_compare_fusion.2, bf16[3202,2,128]{2,0,1:T(8,128)(2,1)S(1)} %get-tuple-element.144, bf16[6,64,2,8,128]{4,3,2,1,0:T(8,128)(2,1)} %get-tuple-element.143, s32[]{:T(128)} %get-tuple-element.133), kind=kOutput, calls=%fused_computation.2.clone.1 | convolution fusion | flops 849220608 | bytes 15226496 | tf_op jit(solution)/shard_map/while/body/eval_jaxpr/bkgd,tkd->bkgt/dot_general | solution.py:51
  126.3 4.5 %fusion.58 = bf16[64,2,8,128]{3,2,0,1:T(8,128)(2,1)S(1)} fusion(bf16[3202,2,128]{2,0,1:T(8,128)(2,1)S(1)} %copy-done.2, f32[2,64,8,3202]{3,2,1,0:T(8,128)S(1)} %get-tuple-element.124, f32[64,2,8]{2,0,1:T(8,128)S(1)} %get-tuple-element.125, pred[64,3202]{1,0:T(8,128)(4,1)S(1)} %broadcast_compare_fusion.2, f32[64,2,8]{2,0,1:T(8,128)S(1)} %fusion.57), kind=kOutput, calls=%fused_computation.14.clone.1 | convolution fusion | flops 852762624 | bytes 15230080 | tf_op jit(solution)/shard_map/while/body/eval_jaxpr/bkgt,tkd->bkgd/dot_general | solution.py:60
  131.9 4.6 %bitcast_reduce_fusion.2 = (f32[64,2,8]{2,0,1:T(8,128)S(1)}, f32[2,64,8,3202]{3,2,1,0:T(8,128)S(1)}) fusion(pred[64,3202]{1,0:T(8,128)(4,1)S(1)} %broadcast_compare_fusion.2, bf16[3202,2,128]{2,0,1:T(8,128)(2,1)S(1)} %get-tuple-element.144, bf16[6,64,2,8,128]{4,3,2,1,0:T(8,128)(2,1)} %get-tuple-element.143, s32[]{:T(128)} %get-tuple-element.133), kind=kOutput, calls=%fused_computation.2.clone.1 | convolution fusion | flops 849220608 | bytes 15226496 | tf_op jit(solution)/shard_map/while/body/eval_jaxpr/bkgd,tkd->bkgt/dot_general | solution.py:51
  136.5 4.3 %fusion.57 = f32[64,2,8]{2,0,1:T(8,128)S(1)} fusion(f32[2,64,8,3202]{3,2,1,0:T(8,128)S(1)} %get-tuple-element.124, f32[64,2,8]{2,0,1:T(8,128)S(1)} %get-tuple-element.125, pred[64,3202]{1,0:T(8,128)(4,1)S(1)} %broadcast_compare_fusion.2), kind=kLoop, calls=%fused_computation.5.clone.1 | loop fusion | flops 13114368 | bytes 13328512 | tf_op jit(solution)/shard_map/while/body/eval_jaxpr/reduce_sum | solution.py:58
  140.7 4.5 %fusion.58 = bf16[64,2,8,128]{3,2,0,1:T(8,128)(2,1)S(1)} fusion(bf16[3202,2,128]{2,0,1:T(8,128)(2,1)S(1)} %copy-done.2, f32[2,64,8,3202]{3,2,1,0:T(8,128)S(1)} %get-tuple-element.124, f32[64,2,8]{2,0,1:T(8,128)S(1)} %get-tuple-element.125, pred[64,3202]{1,0:T(8,128)(4,1)S(1)} %broadcast_compare_fusion.2, f32[64,2,8]{2,0,1:T(8,128)S(1)} %fusion.57), kind=kOutput, calls=%fused_computation.14.clone.1 | convolution fusion | flops 852762624 | bytes 15230080 | tf_op jit(solution)/shard_map/while/body/eval_jaxpr/bkgt,tkd->bkgd/dot_general | solution.py:60
  146.3 4.6 %bitcast_reduce_fusion.2 = (f32[64,2,8]{2,0,1:T(8,128)S(1)}, f32[2,64,8,3202]{3,2,1,0:T(8,128)S(1)}) fusion(pred[64,3202]{1,0:T(8,128)(4,1)S(1)} %broadcast_compare_fusion.2, bf16[3202,2,128]{2,0,1:T(8,128)(2,1)S(1)} %get-tuple-element.144, bf16[6,64,2,8,128]{4,3,2,1,0:T(8,128)(2,1)} %get-tuple-element.143, s32[]{:T(128)} %get-tuple-element.133), kind=kOutput, calls=%fused_computation.2.clone.1 | convolution fusion | flops 849220608 | bytes 15226496 | tf_op jit(solution)/shard_map/while/body/eval_jaxpr/bkgd,tkd->bkgt/dot_general | solution.py:51
  155.2 4.5 %fusion.58 = bf16[64,2,8,128]{3,2,0,1:T(8,128)(2,1)S(1)} fusion(bf16[3202,2,128]{2,0,1:T(8,128)(2,1)S(1)} %copy-done.2, f32[2,64,8,3202]{3,2,1,0:T(8,128)S(1)} %get-tuple-element.124, f32[64,2,8]{2,0,1:T(8,128)S(1)} %get-tuple-element.125, pred[64,3202]{1,0:T(8,128)(4,1)S(1)} %broadcast_compare_fusion.2, f32[64,2,8]{2,0,1:T(8,128)S(1)} %fusion.57), kind=kOutput, calls=%fused_computation.14.clone.1 | convolution fusion | flops 852762624 | bytes 15230080 | tf_op jit(solution)/shard_map/while/body/eval_jaxpr/bkgt,tkd->bkgd/dot_general | solution.py:60
  160.8 4.6 %bitcast_reduce_fusion.2 = (f32[64,2,8]{2,0,1:T(8,128)S(1)}, f32[2,64,8,3202]{3,2,1,0:T(8,128)S(1)}) fusion(pred[64,3202]{1,0:T(8,128)(4,1)S(1)} %broadcast_compare_fusion.2, bf16[3202,2,128]{2,0,1:T(8,128)(2,1)S(1)} %get-tuple-element.144, bf16[6,64,2,8,128]{4,3,2,1,0:T(8,128)(2,1)} %get-tuple-element.143, s32[]{:T(128)} %get-tuple-element.133), kind=kOutput, calls=%fused_computation.2.clone.1 | convolution fusion | flops 849220608 | bytes 15226496 | tf_op jit(solution)/shard_map/while/body/eval_jaxpr/bkgd,tkd->bkgt/dot_general | solution.py:51
  169.7 4.5 %fusion.58 = bf16[64,2,8,128]{3,2,0,1:T(8,128)(2,1)S(1)} fusion(bf16[3202,2,128]{2,0,1:T(8,128)(2,1)S(1)} %copy-done.2, f32[2,64,8,3202]{3,2,1,0:T(8,128)S(1)} %get-tuple-element.124, f32[64,2,8]{2,0,1:T(8,128)S(1)} %get-tuple-element.125, pred[64,3202]{1,0:T(8,128)(4,1)S(1)} %broadcast_compare_fusion.2, f32[64,2,8]{2,0,1:T(8,128)S(1)} %fusion.57), kind=kOutput, calls=%fused_computation.14.clone.1 | convolution fusion | flops 852762624 | bytes 15230080 | tf_op jit(solution)/shard_map/while/body/eval_jaxpr/bkgt,tkd->bkgd/dot_general | solution.py:60
  178.8 5.9 %all-to-all-start.2 = ((bf16[64,6,2048]{2,1,0:T(8,128)(2,1)}), bf16[64,6,2048]{2,1,0:T(8,128)(2,1)S(1)}, u32[]{:S(2)}, u32[]{:S(2)}) async-start(bf16[64,6,2048]{2,1,0:T(8,128)(2,1)} %reshape.84), calls=%async_computation.2 | async-start | bytes 4194304 | tf_op jit(solution)/shard_map/all_to_all | solution.py:80
  184.8 51.2 %all-to-all-done.2 = bf16[64,6,2048]{2,1,0:T(8,128)(2,1)S(1)} async-done(((bf16[64,6,2048]{2,1,0:T(8,128)(2,1)}), bf16[64,6,2048]{2,1,0:T(8,128)(2,1)S(1)}, u32[]{:S(2)}, u32[]{:S(2)}) %all-to-all-start.2) | async-done | bytes 1572896 | tf_op jit(solution)/shard_map/all_to_all | solution.py:80
  239.7 8.5 %psum.7 = f32[256]{0:T(256)S(1)} all-reduce(f32[256]{0:T(256)S(1)} %get-tuple-element.83), channel_id=1, replica_groups=mesh['docs'=64,'mp'=4] {'mp'}, use_global_device_ids=true, to_apply=%region_8.9 | all-reduce | flops 256 | bytes 2048 | tf_op jit(solution)/shard_map/psum | solution.py:85
  (83 shorter events, 48.2 us)
Async XLA Ops:
  0.0 17.9 %copy-start = (bf16[256,2048]{1,0:T(8,128)(2,1)S(1)}, bf16[256,2048]{1,0:T(8,128)(2,1)}, u32[]{:S(2)}) copy-start(bf16[256,2048]{1,0:T(8,128)(2,1)} %param.8) | copy-start | bytes 3145732
  4.8 22.4 %all-to-all-start = ((bf16[64,1,6]{2,1,0:T(2,128)(2,1)}), bf16[64,1,6]{2,1,0:T(2,128)(2,1)S(1)}, u32[]{:S(2)}, u32[]{:S(2)}) async-start(bf16[64,1,6]{2,1,0:T(2,128)(2,1)} %all_to_all.16), calls=%async_computation | async-start | bytes 65536 | tf_op jit(solution)/shard_map/all_to_all | solution.py:68
  20.1 12.6 %copy-start.1 = (bf16[3202,256]{1,0:T(8,128)(2,1)S(1)}, bf16[3202,256]{1,0:T(8,128)(2,1)}, u32[]{:S(2)}) copy-start(bf16[3202,256]{1,0:T(8,128)(2,1)} %param.9) | copy-start | bytes 4918276
  27.1 56.9 %all-to-all-start.1 = ((bf16[64,6,2048]{2,1,0:T(8,128)(2,1)}), bf16[64,6,2048]{2,1,0:T(8,128)(2,1)}, u32[]{:S(2)}, u32[]{:S(2)}) async-start(bf16[64,6,2048]{2,1,0:T(8,128)(2,1)} %reshape.81), calls=%async_computation.1 | async-start | bytes 4194304 | tf_op jit(solution)/shard_map/all_to_all | solution.py:67
  93.1 4.3 %copy-start.2 = (bf16[3202,2,128]{2,0,1:T(8,128)(2,1)S(1)}, bf16[3202,2,128]{2,0,1:T(8,128)(2,1)}, u32[]{:S(2)}) copy-start(bf16[3202,2,128]{2,0,1:T(8,128)(2,1)} %get-tuple-element.145) | copy-start | bytes 4918276 | tf_op jit(solution)/shard_map/while
  107.5 4.3 %copy-start.2 = (bf16[3202,2,128]{2,0,1:T(8,128)(2,1)S(1)}, bf16[3202,2,128]{2,0,1:T(8,128)(2,1)}, u32[]{:S(2)}) copy-start(bf16[3202,2,128]{2,0,1:T(8,128)(2,1)} %get-tuple-element.145) | copy-start | bytes 4918276 | tf_op jit(solution)/shard_map/while
  122.0 4.3 %copy-start.2 = (bf16[3202,2,128]{2,0,1:T(8,128)(2,1)S(1)}, bf16[3202,2,128]{2,0,1:T(8,128)(2,1)}, u32[]{:S(2)}) copy-start(bf16[3202,2,128]{2,0,1:T(8,128)(2,1)} %get-tuple-element.145) | copy-start | bytes 4918276 | tf_op jit(solution)/shard_map/while
  136.5 4.3 %copy-start.2 = (bf16[3202,2,128]{2,0,1:T(8,128)(2,1)S(1)}, bf16[3202,2,128]{2,0,1:T(8,128)(2,1)}, u32[]{:S(2)}) copy-start(bf16[3202,2,128]{2,0,1:T(8,128)(2,1)} %get-tuple-element.145) | copy-start | bytes 4918276 | tf_op jit(solution)/shard_map/while
  150.9 4.3 %copy-start.2 = (bf16[3202,2,128]{2,0,1:T(8,128)(2,1)S(1)}, bf16[3202,2,128]{2,0,1:T(8,128)(2,1)}, u32[]{:S(2)}) copy-start(bf16[3202,2,128]{2,0,1:T(8,128)(2,1)} %get-tuple-element.145) | copy-start | bytes 4918276 | tf_op jit(solution)/shard_map/while
  165.4 4.3 %copy-start.2 = (bf16[3202,2,128]{2,0,1:T(8,128)(2,1)S(1)}, bf16[3202,2,128]{2,0,1:T(8,128)(2,1)}, u32[]{:S(2)}) copy-start(bf16[3202,2,128]{2,0,1:T(8,128)(2,1)} %get-tuple-element.145) | copy-start | bytes 4918276 | tf_op jit(solution)/shard_map/while
  178.8 6.0 %copy-start.3 = (bf16[2048]{0:T(1024)(128)(2,1)S(1)}, bf16[2048]{0:T(1024)(128)(2,1)}, u32[]{:S(2)}) copy-start(bf16[2048]{0:T(1024)(128)(2,1)} %param.13) | copy-start | bytes 12292
  178.8 57.2 %all-to-all-start.2 = ((bf16[64,6,2048]{2,1,0:T(8,128)(2,1)}), bf16[64,6,2048]{2,1,0:T(8,128)(2,1)S(1)}, u32[]{:S(2)}, u32[]{:S(2)}) async-start(bf16[64,6,2048]{2,1,0:T(8,128)(2,1)} %reshape.84), calls=%async_computation.2 | async-start | bytes 4194304 | tf_op jit(solution)/shard_map/all_to_all | solution.py:80
where the time goes:
time: 250 us; the launch traced here: 249 us
  waiting for transfers between devices  96.4 us (39%)
  matrix products  57.2 us (23%)
  other arithmetic  31.8 us (13%)
  local copies, waits for them, and re-layouts  30.5 us (12%)
  starting transfers between devices  24.7 us (10%)
  blocking collectives  8.47 us (3%)
    all_to_all x1, waiting for transfers between devices, shards(): lax.all_to_all(context, 'docs', split_axis=0, concat_axis=0, tiled=True)  51.2 us
    all_to_all x1, waiting for transfers between devices, shards(): lax.all_to_all(packed, 'docs', split_axis=0, concat_axis=0, tiled=True)  38.1 us
    dot_general x6, matrix products, one_block(): jnp.einsum('bkgd,tkd->bkgt', block_q, key_grid, preferred_element_type=jn...  27.4 us
    dot_general x6, matrix products, one_block(): jnp.einsum('bkgt,tkd->bkgd', probs, value_grid, preferred_element_type=jn...  26.8 us
    reduce_sum x6, other arithmetic, one_block(): total = jnp.sum(weights, axis=-1)  25.7 us
    all_to_all x1, starting transfers between devices, shards(): lax.all_to_all(seen_packed, 'docs', split_axis=0, concat_axis=0, tiled=True)  13.2 us
    unnamed x10, local copies, waits for them, and re-layouts  12.9 us
    psum x1, blocking collectives, shards(): power = lax.psum(squares(mine), 'mp')  8.47 us
  transfers between devices with their start and end apart: 3, of which 3 were waited for; matrix products, arithmetic and copies ran while one was open for 6% of the time, Pallas kernels for 0%

commit v1 on v0

v1 whole, which is shorter than its diff:
```python
import math

import jax
import jax.numpy as jnp
from jax import lax
from jax.experimental import pallas as pl
from jax.experimental.pallas import tpu as pltpu
from jax.sharding import PartitionSpec as P

HD = 128
IMG_TOK = 1601
D = 8192
GROUP = 8


def rescale(context, power, gain):
    wide = context.astype(jnp.float32)
    factor = lax.rsqrt(power / D + 1e-05)
    return (wide * factor[..., None] * gain.astype(jnp.float32)).astype(jnp.bfloat16)


def squares(context):
    wide = context.astype(jnp.float32)
    return jnp.sum(wide * wide, axis=-1)


def attend_kernel(seen_ref, q_ref, k_ref, v_ref, o_ref):
    tm = q_ref.shape[0]
    tp = k_ref.shape[0]
    scale = 1.0 / HD**0.5
    limit = seen_ref[...] * IMG_TOK
    allowed = lax.broadcasted_iota(jnp.int32, (tm, tp), 1) < limit
    keys = k_ref[...]
    vals = v_ref[...]
    for g in range(GROUP):
        q = q_ref[:, g * HD : (g + 1) * HD]
        s = lax.dot_general(
            q, keys, (((1,), (1,)), ((), ())), preferred_element_type=jnp.float32
        ) * scale
        s = jnp.where(allowed, s, jnp.float32(-1e30))
        top = jnp.max(s, axis=1, keepdims=True)
        w = jnp.exp(s - top)
        total = jnp.sum(w, axis=1, keepdims=True)
        ctx = jnp.dot(w.astype(jnp.bfloat16), vals, preferred_element_type=jnp.float32)
        o_ref[:, g * HD : (g + 1) * HD] = (ctx / total).astype(o_ref.dtype)


def attend(q, seen, keys, values):
    rows, width = q.shape
    tokens = keys.shape[0]
    padded = -(-tokens // 128) * 128
    kv_local = keys.shape[1] // HD
    kp = jnp.pad(keys, ((0, padded - tokens), (0, 0)))
    vp = jnp.pad(values, ((0, padded - tokens), (0, 0)))
    tm = math.gcd(rows, 128)
    return pl.pallas_call(
        attend_kernel,
        grid=(kv_local, rows // tm),
        in_specs=[
            pl.BlockSpec((tm, 1), lambda k, i: (i, 0)),
            pl.BlockSpec((tm, GROUP * HD), lambda k, i: (i, k)),
            pl.BlockSpec((padded, HD), lambda k, i: (0, k)),
            pl.BlockSpec((padded, HD), lambda k, i: (0, k)),
        ],
        out_specs=pl.BlockSpec((tm, GROUP * HD), lambda k, i: (i, k)),
        out_shape=jax.ShapeDtypeStruct((rows, width), jnp.bfloat16),
    )(seen, q, kp, vp)


def shards(queries, keys, values, owner_of_row, visible, gain):
    docs = lax.axis_size("docs")
    rows = queries.shape[0]
    width = queries.shape[1]
    cap = max(2, 3 * rows // (2 * docs))
    route = owner_of_row[:, 0]
    onehot = (route[:, None] == jnp.arange(docs, dtype=jnp.int32)[None, :]).astype(jnp.int32)
    before = jnp.cumsum(onehot, axis=0) - onehot
    rank = jnp.sum(before * onehot, axis=1)
    target = route * cap + rank
    place = (jnp.arange(docs * cap, dtype=jnp.int32)[:, None] == target[None, :]).astype(
        jnp.bfloat16
    )
    packed = jnp.dot(place, queries, preferred_element_type=jnp.float32).astype(jnp.bfloat16)
    packed = packed.reshape(docs, cap, width)
    seen_packed = jnp.dot(place, visible.astype(jnp.bfloat16), preferred_element_type=jnp.float32)
    seen_packed = seen_packed.astype(jnp.bfloat16).reshape(docs, cap)
    arrived, arrived_seen = (
        lax.all_to_all(packed, "docs", split_axis=0, concat_axis=0, tiled=True),
        lax.all_to_all(seen_packed, "docs", split_axis=0, concat_axis=0, tiled=True),
    )
    context = attend(
        arrived.reshape(-1, width),
        arrived_seen.reshape(-1, 1).astype(jnp.int32),
        keys,
        values,
    ).reshape(arrived.shape)
    returned = lax.all_to_all(context, "docs", split_axis=0, concat_axis=0, tiled=True)
    flat_back = returned.reshape(docs * cap, width)
    mine = jnp.einsum("sr,sc->rc", place, flat_back, preferred_element_type=jnp.float32).astype(
        jnp.bfloat16
    )
    power = lax.psum(squares(mine), "mp")
    return rescale(mine, power, gain)


def solution(mesh):
    return jax.shard_map(
        shards,
        mesh=mesh,
        in_specs=(
            P("docs", "mp"),
            P("docs", "mp"),
            P("docs", "mp"),
            P("docs", None),
            P("docs"),
            P("mp"),
        ),
        out_specs=P("docs", "mp"),
        check_vma=False,
    )
```

time: 250 us -> 202 us (0.81)
  matrix products: 57.2 us -> 3.03 us
  Pallas kernels: 0 us -> 42.5 us
  other arithmetic: 31.8 us -> 4.97 us
  local copies, waits for them, and re-layouts: 30.5 us -> 14.2 us
  waiting for transfers between devices: 96.4 us -> 104 us
    dot_general x12 -> x0, matrix products: 54.1 us -> none  [the longest x6 27.4 us: one_block(): jnp.einsum('bkgd,tkd->bkgt', block_q, key_grid, preferred_element_type=jn...]
    pallas_call x0 -> x1, Pallas kernels: none -> 42.5 us  [attend(): pl.pallas_call(attend_kernel, grid=(kv_local, rows // tm), in_specs=[pl.B...]
    reduce_sum x6 -> x0, other arithmetic: 25.7 us -> none  [one_block(): total = jnp.sum(weights, axis=-1)]
    unnamed x10 -> x6, local copies, waits for them, and re-layouts: 12.9 us -> 0.01 us
    all_to_all x1, waiting for transfers between devices: 38.1 us -> 46.3 us  [shards(): lax.all_to_all(packed, 'docs', split_axis=0, concat_axis=0, tiled=True)]
    another operation x3 -> x1, local copies, waits for them, and re-layouts: 4.46 us -> 0.01 us  [the longest x1 4.34 us: shards(): flat_q.reshape(blocks, block, kv_local, GROUP, HD)]
    dynamic_update_slice x6 -> x0, local copies, waits for them, and re-layouts: 4.45 us -> none  [shards(): lax.map(one_block, (flat_q.reshape(blocks, block, kv_local, GROUP, HD), f...]
    pad x0 -> x2, local copies, waits for them, and re-layouts: none -> 4.14 us  [the longest x1 2.86 us: attend(): kp = jnp.pad(keys, ((0, padded - tokens), (0, 0)))]
  transfers between devices with their start and end apart: 3 -> 3, of which waited for: 3 -> 3; matrix products, arithmetic and copies ran while one was open for 6% -> 4% of each run, Pallas kernels for 0% -> 0%
where the time goes in v1:
time: 202 us
  waiting for transfers between devices  104 us (51%)
  Pallas kernels  42.5 us (21%)
  starting transfers between devices  23.9 us (12%)
  local copies, waits for them, and re-layouts  14.2 us (7%)
  blocking collectives  8.47 us (4%)
  other arithmetic  4.97 us (2%)
  matrix products  3.03 us (2%)
    all_to_all x1, waiting for transfers between devices, shards(): lax.all_to_all(context, 'docs', split_axis=0, concat_axis=0, tiled=True)  51.2 us
    all_to_all x1, waiting for transfers between devices, shards(): lax.all_to_all(packed, 'docs', split_axis=0, concat_axis=0, tiled=True)  46.3 us
    pallas_call x1, Pallas kernels, attend(): pl.pallas_call(attend_kernel, grid=(kv_local, rows // tm), in_specs=[pl.B...  42.5 us
    all_to_all x1, starting transfers between devices, shards(): lax.all_to_all(seen_packed, 'docs', split_axis=0, concat_axis=0, tiled=True)  13.2 us
    psum x1, blocking collectives, shards(): power = lax.psum(squares(mine), 'mp')  8.47 us
    all_to_all x1, waiting for transfers between devices, shards(): lax.all_to_all(seen_packed, 'docs', split_axis=0, concat_axis=0, tiled=True)  6.97 us
    all_to_all x1, starting transfers between devices, shards(): lax.all_to_all(context, 'docs', split_axis=0, concat_axis=0, tiled=True)  5.95 us
    all_to_all x1, starting transfers between devices, shards(): lax.all_to_all(packed, 'docs', split_axis=0, concat_axis=0, tiled=True)  4.79 us
  transfers between devices with their start and end apart: 3, of which 3 were waited for; matrix products, arithmetic and copies ran while one was open for 4% of the time, Pallas kernels for 0%

profile of v1, /device:TPU:1, one launch (start us, length us, event | category | flops | bytes accessed | tf_op | source)
XLA Modules:
  0.0 201.6 jit_solution(4092737251225916050)
XLA Ops:
  0.0 0.8 fusion.9
  0.8 0.6 reduce-window.6
  1.6 0.8 fusion.8
  2.4 0.7 multiply_add_fusion
  3.1 0.7 convert_element_type.40
  4.0 0.8 all_to_all.16
  4.8 13.2 %all-to-all-start = ((bf16[64,1,6]{2,1,0:T(2,128)(2,1)}), bf16[64,1,6]{2,1,0:T(2,128)(2,1)S(1)}, u32[]{:S(2)}, u32[]{:S(2)}) async-start(bf16[64,1,6]{2,1,0:T(2,128)(2,1)} %all_to_all.16), calls=%async_computation | async-start | bytes 65536 | tf_op jit(solution)/shard_map/all_to_all | solution.py:89
  17.9 0.6 convolution_convert_fusion
  18.5 1.6 reshape.59
  20.2 7.0 %all-to-all-done = bf16[64,1,6]{2,1,0:T(2,128)(2,1)S(1)} async-done(((bf16[64,1,6]{2,1,0:T(2,128)(2,1)}), bf16[64,1,6]{2,1,0:T(2,128)(2,1)S(1)}, u32[]{:S(2)}, u32[]{:S(2)}) %all-to-all-start) | async-done | bytes 800 | tf_op jit(solution)/shard_map/all_to_all | solution.py:89
  27.1 4.8 %all-to-all-start.1 = ((bf16[64,6,2048]{2,1,0:T(8,128)(2,1)}), bf16[64,6,2048]{2,1,0:T(8,128)(2,1)S(1)}, u32[]{:S(2)}, u32[]{:S(2)}) async-start(bf16[64,6,2048]{2,1,0:T(8,128)(2,1)} %reshape.59), calls=%async_computation.1 | async-start | bytes 4194304 | tf_op jit(solution)/shard_map/all_to_all | solution.py:88
  32.0 2.9 %pad.7.k_ref = bf16[3328,256]{1,0:T(8,128)(2,1)} pad(bf16[3202,256]{1,0:T(8,128)(2,1)} %param.7, bf16[]{:T(256)} %constant.13.clone.1), padding=0_126x0_0 | pad | bytes 3343362 | tf_op jit(solution)/shard_map/jit(_pad)/pad | solution.py:53
  34.8 1.3 pad.8.v_ref
  36.2 0.8 reshape.66.seen_ref
  37.0 46.3 %all-to-all-done.1 = bf16[64,6,2048]{2,1,0:T(8,128)(2,1)S(1)} async-done(((bf16[64,6,2048]{2,1,0:T(8,128)(2,1)}), bf16[64,6,2048]{2,1,0:T(8,128)(2,1)S(1)}, u32[]{:S(2)}, u32[]{:S(2)}) %all-to-all-start.1) | async-done | bytes 1572896 | tf_op jit(solution)/shard_map/all_to_all | solution.py:88
  83.3 1.4 reshape.60.q_ref
  84.7 42.5 %shard_map.64 = bf16[384,2048]{1,0:T(8,128)(2,1)} custom-call(s32[384,1]{1,0:T(8,128)} %reshape.66.seen_ref, bf16[384,2048]{1,0:T(8,128)(2,1)} %reshape.60.q_ref, bf16[3328,256]{1,0:T(8,128)(2,1)} %pad.7.k_ref, bf16[3328,256]{1,0:T(8,128)(2,1)} %pad.8.v_ref), custom_call_target="tpu_custom_call" | custom-call | tf_op jit(solution)/shard_map/pallas_call | solution.py:56
  127.2 3.7 %reshape.61 = bf16[64,6,2048]{2,1,0:T(8,128)(2,1)} reshape(bf16[384,2048]{1,0:T(8,128)(2,1)} %shard_map.64) | data formatting | bytes 3145728 | tf_op jit(solution)/shard_map/reshape | solution.py:96
  130.9 5.9 %all-to-all-start.2 = ((bf16[64,6,2048]{2,1,0:T(8,128)(2,1)}), bf16[64,6,2048]{2,1,0:T(8,128)(2,1)S(1)}, u32[]{:S(2)}, u32[]{:S(2)}) async-start(bf16[64,6,2048]{2,1,0:T(8,128)(2,1)} %reshape.61), calls=%async_computation.2 | async-start | bytes 4194304 | tf_op jit(solution)/shard_map/all_to_all | solution.py:97
  136.9 51.2 %all-to-all-done.2 = bf16[64,6,2048]{2,1,0:T(8,128)(2,1)S(1)} async-done(((bf16[64,6,2048]{2,1,0:T(8,128)(2,1)}), bf16[64,6,2048]{2,1,0:T(8,128)(2,1)S(1)}, u32[]{:S(2)}, u32[]{:S(2)}) %all-to-all-start.2) | async-done | bytes 1572896 | tf_op jit(solution)/shard_map/all_to_all | solution.py:97
  188.1 1.4 reshape.62
  189.6 2.2 %fusion = (f32[256]{0:T(256)S(1)}, bf16[256,2048]{1,0:T(8,128)(2,1)S(1)}) fusion(bf16[384,2048]{1,0:T(8,128)(2,1)} %reshape.62, s32[256]{0:T(256)S(1)} %multiply_add_fusion), kind=kOutput, calls=%fused_computation.4 | convolution fusion | flops 404848384 | bytes 2623488 | tf_op jit(solution)/shard_map/sr,sc->rc/dot_general | solution.py:99
  191.8 8.5 %psum.7 = f32[256]{0:T(256)S(1)} all-reduce(f32[256]{0:T(256)S(1)} %get-tuple-element.5), channel_id=1, replica_groups=mesh['docs'=64,'mp'=4] {'mp'}, use_global_device_ids=true, to_apply=%region_4.5 | all-reduce | flops 256 | bytes 2048 | tf_op jit(solution)/shard_map/psum | solution.py:102
  200.3 1.3 fusion.2
  (14 shorter events, 0.6 us)
Async XLA Ops:
  0.0 17.9 %copy-start = (bf16[256,2048]{1,0:T(8,128)(2,1)S(1)}, bf16[256,2048]{1,0:T(8,128)(2,1)}, u32[]{:S(2)}) copy-start(bf16[256,2048]{1,0:T(8,128)(2,1)} %param.6) | copy-start | bytes 3145732
  4.8 22.4 %all-to-all-start = ((bf16[64,1,6]{2,1,0:T(2,128)(2,1)}), bf16[64,1,6]{2,1,0:T(2,128)(2,1)S(1)}, u32[]{:S(2)}, u32[]{:S(2)}) async-start(bf16[64,1,6]{2,1,0:T(2,128)(2,1)} %all_to_all.16), calls=%async_computation | async-start | bytes 65536 | tf_op jit(solution)/shard_map/all_to_all | solution.py:89
  27.1 56.2 %all-to-all-start.1 = ((bf16[64,6,2048]{2,1,0:T(8,128)(2,1)}), bf16[64,6,2048]{2,1,0:T(8,128)(2,1)S(1)}, u32[]{:S(2)}, u32[]{:S(2)}) async-start(bf16[64,6,2048]{2,1,0:T(8,128)(2,1)} %reshape.59), calls=%async_computation.1 | async-start | bytes 4194304 | tf_op jit(solution)/shard_map/all_to_all | solution.py:88
  31.9 2.9 %copy-start.1 = (bf16[3202,256]{1,0:T(8,128)(2,1)S(1)}, bf16[3202,256]{1,0:T(8,128)(2,1)}, u32[]{:S(2)}) copy-start(bf16[3202,256]{1,0:T(8,128)(2,1)} %param.8) | copy-start | bytes 4918276
  130.9 6.0 %copy-start.2 = (bf16[2048]{0:T(1024)(128)(2,1)S(1)}, bf16[2048]{0:T(1024)(128)(2,1)}, u32[]{:S(2)}) copy-start(bf16[2048]{0:T(1024)(128)(2,1)} %param.11) | copy-start | bytes 12292
  130.9 57.2 %all-to-all-start.2 = ((bf16[64,6,2048]{2,1,0:T(8,128)(2,1)}), bf16[64,6,2048]{2,1,0:T(8,128)(2,1)S(1)}, u32[]{:S(2)}, u32[]{:S(2)}) async-start(bf16[64,6,2048]{2,1,0:T(8,128)(2,1)} %reshape.61), calls=%async_computation.2 | async-start | bytes 4194304 | tf_op jit(solution)/shard_map/all_to_all | solution.py:97

commit v2 on v1

--- a/solution.py
+++ b/solution.py
@@ -28,8 +28,8 @@
     tm = q_ref.shape[0]
     tp = k_ref.shape[0]
     scale = 1.0 / HD**0.5
-    limit = seen_ref[...] * IMG_TOK
-    allowed = lax.broadcasted_iota(jnp.int32, (tm, tp), 1) < limit
+    limit = seen_ref[:, 0:1].astype(jnp.float32) * IMG_TOK
+    allowed = lax.broadcasted_iota(jnp.int32, (tm, tp), 1).astype(jnp.float32) < limit
     keys = k_ref[...]
     vals = v_ref[...]
     for g in range(GROUP):
@@ -45,8 +45,9 @@
         o_ref[:, g * HD : (g + 1) * HD] = (ctx / total).astype(o_ref.dtype)
 
 
-def attend(q, seen, keys, values):
-    rows, width = q.shape
+def attend(q, keys, values):
+    rows = q.shape[0]
+    width = q.shape[1] - 128
     tokens = keys.shape[0]
     padded = -(-tokens // 128) * 128
     kv_local = keys.shape[1] // HD
@@ -57,14 +58,14 @@
         attend_kernel,
         grid=(kv_local, rows // tm),
         in_specs=[
-            pl.BlockSpec((tm, 1), lambda k, i: (i, 0)),
+            pl.BlockSpec((tm, 128), lambda k, i: (i, width // 128)),
             pl.BlockSpec((tm, GROUP * HD), lambda k, i: (i, k)),
             pl.BlockSpec((padded, HD), lambda k, i: (0, k)),
             pl.BlockSpec((padded, HD), lambda k, i: (0, k)),
         ],
         out_specs=pl.BlockSpec((tm, GROUP * HD), lambda k, i: (i, k)),
         out_shape=jax.ShapeDtypeStruct((rows, width), jnp.bfloat16),
-    )(seen, q, kp, vp)
+    )(q, q, kp, vp)
 
 
 def shards(queries, keys, values, owner_of_row, visible, gain):
@@ -80,20 +81,13 @@
     place = (jnp.arange(docs * cap, dtype=jnp.int32)[:, None] == target[None, :]).astype(
         jnp.bfloat16
     )
-    packed = jnp.dot(place, queries, preferred_element_type=jnp.float32).astype(jnp.bfloat16)
-    packed = packed.reshape(docs, cap, width)
-    seen_packed = jnp.dot(place, visible.astype(jnp.bfloat16), preferred_element_type=jnp.float32)
-    seen_packed = seen_packed.astype(jnp.bfloat16).reshape(docs, cap)
-    arrived, arrived_seen = (
-        lax.all_to_all(packed, "docs", split_axis=0, concat_axis=0, tiled=True),
-        lax.all_to_all(seen_packed, "docs", split_axis=0, concat_axis=0, tiled=True),
-    )
-    context = attend(
-        arrived.reshape(-1, width),
-        arrived_seen.reshape(-1, 1).astype(jnp.int32),
-        keys,
-        values,
-    ).reshape(arrived.shape)
+    extra = jnp.broadcast_to(visible.astype(jnp.bfloat16)[:, None], (rows, 128))
+    payload = jnp.concatenate([queries, extra], axis=1)
+    packed = jnp.dot(place, payload, preferred_element_type=jnp.float32).astype(jnp.bfloat16)
+    packed = packed.reshape(docs, cap, width + 128)
+    arrived = lax.all_to_all(packed, "docs", split_axis=0, concat_axis=0, tiled=True)
+    context = attend(arrived.reshape(docs * cap, width + 128), keys, values)
+    context = context.reshape(docs, cap, width)
     returned = lax.all_to_all(context, "docs", split_axis=0, concat_axis=0, tiled=True)
     flat_back = returned.reshape(docs * cap, width)
     mine = jnp.einsum("sr,sc->rc", place, flat_back, preferred_element_type=jnp.float32).astype(

time: 202 us -> 193 us (0.955)
  starting transfers between devices: 23.9 us -> 19.3 us
  waiting for transfers between devices: 104 us -> 101 us
    all_to_all x1 -> x0, starting transfers between devices: 13.2 us -> none  [shards(): lax.all_to_all(seen_packed, 'docs', split_axis=0, concat_axis=0, tiled=True)]
    all_to_all x1, starting transfers between devices: 4.79 us -> 13.2 us  [shards(): lax.all_to_all(packed, 'docs', split_axis=0, concat_axis=0, tiled=True)]
    all_to_all x1 -> x0, waiting for transfers between devices: 6.97 us -> none  [shards(): lax.all_to_all(seen_packed, 'docs', split_axis=0, concat_axis=0, tiled=True)]
    all_to_all x1, waiting for transfers between devices: 46.3 us -> 49.7 us  [shards(): lax.all_to_all(packed, 'docs', split_axis=0, concat_axis=0, tiled=True)]
  transfers between devices with their start and end apart: 3 -> 2, of which waited for: 3 -> 2; matrix products, arithmetic and copies ran while one was open for 4% -> 2% of each run, Pallas kernels for 0% -> 0%
where the time goes in v2:
time: 193 us
  waiting for transfers between devices  101 us (52%)
  Pallas kernels  42.1 us (22%)
  starting transfers between devices  19.3 us (10%)
  local copies, waits for them, and re-layouts  12.8 us (7%)
  blocking collectives  8.47 us (4%)
  other arithmetic  4.77 us (2%)
  matrix products  4.1 us (2%)
    all_to_all x1, waiting for transfers between devices, shards(): lax.all_to_all(context, 'docs', split_axis=0, concat_axis=0, tiled=True)  51.2 us
    all_to_all x1, waiting for transfers between devices, shards(): lax.all_to_all(packed, 'docs', split_axis=0, concat_axis=0, tiled=True)  49.7 us
    pallas_call x1, Pallas kernels, attend(): pl.pallas_call(attend_kernel, grid=(kv_local, rows // tm), in_specs=[pl.B...  42.1 us
    all_to_all x1, starting transfers between devices, shards(): lax.all_to_all(packed, 'docs', split_axis=0, concat_axis=0, tiled=True)  13.2 us
    psum x1, blocking collectives, shards(): power = lax.psum(squares(mine), 'mp')  8.47 us
    all_to_all x1, starting transfers between devices, shards(): lax.all_to_all(context, 'docs', split_axis=0, concat_axis=0, tiled=True)  6.14 us
  transfers between devices with their start and end apart: 2, of which 2 were waited for; matrix products, arithmetic and copies ran while one was open for 2% of the time, Pallas kernels for 0%

profile of v2, /device:TPU:1, one launch (start us, length us, event | category | flops | bytes accessed | tf_op | source)
XLA Modules:
  0.0 192.5 jit_solution(6729499702258854551)
XLA Ops:
  0.0 0.7 fusion.11
  0.7 0.6 reduce-window.6
  1.3 0.2 slice_reduce_fusion
  1.5 0.8 fusion.10
  2.3 0.7 multiply_add_fusion
  3.0 0.7 convert_element_type.32
  3.7 0.1 broadcast_in_dim.2
  3.8 1.9 convolution_convert_fusion
  5.6 1.7 reshape.40
  7.4 13.2 %all-to-all-start = ((bf16[64,6,2176]{2,1,0:T(8,128)(2,1)}), bf16[64,6,2176]{2,1,0:T(8,128)(2,1)S(1)}, u32[]{:S(2)}, u32[]{:S(2)}) async-start(bf16[64,6,2176]{2,1,0:T(8,128)(2,1)} %reshape.40), calls=%async_computation | async-start | bytes 4456448 | tf_op jit(solution)/shard_map/all_to_all | solution.py:88
  20.5 0.0 copy-start
  20.5 2.9 %pad.7.k_ref = bf16[3328,256]{1,0:T(8,128)(2,1)} pad(bf16[3202,256]{1,0:T(8,128)(2,1)} %param.7, bf16[]{:T(256)} %constant.13.clone.1), padding=0_126x0_0 | pad | bytes 3343362 | tf_op jit(solution)/shard_map/jit(_pad)/pad | solution.py:54
  23.4 0.0 copy-done
  23.4 1.3 pad.8.v_ref
  24.7 49.7 %all-to-all-done = bf16[64,6,2176]{2,1,0:T(8,128)(2,1)S(1)} async-done(((bf16[64,6,2176]{2,1,0:T(8,128)(2,1)}), bf16[64,6,2176]{2,1,0:T(8,128)(2,1)S(1)}, u32[]{:S(2)}, u32[]{:S(2)}) %all-to-all-start) | async-done | bytes 1671200 | tf_op jit(solution)/shard_map/all_to_all | solution.py:88
  74.4 1.5 reshape.41.seen_ref.q_ref
  75.9 42.1 %shard_map.64 = bf16[384,2048]{1,0:T(8,128)(2,1)} custom-call(bf16[384,2176]{1,0:T(8,128)(2,1)} %reshape.41.seen_ref.q_ref, bf16[384,2176]{1,0:T(8,128)(2,1)} %reshape.41.seen_ref.q_ref, bf16[3328,256]{1,0:T(8,128)(2,1)} %pad.7.k_ref, bf16[3328,256]{1,0:T(8,128)(2,1)} %pad.8.v_ref), custom_call_target="tpu_custom_call" | custom-call | tf_op jit(solution)/shard_map/pallas_call | solution.py:57
  118.0 3.7 %reshape.42 = bf16[64,6,2048]{2,1,0:T(8,128)(2,1)} reshape(bf16[384,2048]{1,0:T(8,128)(2,1)} %shard_map.64) | data formatting | bytes 3145728 | tf_op jit(solution)/shard_map/reshape | solution.py:90
  121.7 6.1 %all-to-all-start.1 = ((bf16[64,6,2048]{2,1,0:T(8,128)(2,1)}), bf16[64,6,2048]{2,1,0:T(8,128)(2,1)S(1)}, u32[]{:S(2)}, u32[]{:S(2)}) async-start(bf16[64,6,2048]{2,1,0:T(8,128)(2,1)} %reshape.42), calls=%async_computation.1 | async-start | bytes 4194304 | tf_op jit(solution)/shard_map/all_to_all | solution.py:91
  127.9 51.2 %all-to-all-done.1 = bf16[64,6,2048]{2,1,0:T(8,128)(2,1)S(1)} async-done(((bf16[64,6,2048]{2,1,0:T(8,128)(2,1)}), bf16[64,6,2048]{2,1,0:T(8,128)(2,1)S(1)}, u32[]{:S(2)}, u32[]{:S(2)}) %all-to-all-start.1) | async-done | bytes 1572896 | tf_op jit(solution)/shard_map/all_to_all | solution.py:91
  179.1 1.4 reshape.43
  180.5 2.2 %fusion = (f32[256]{0:T(256)S(1)}, bf16[256,2048]{1,0:T(8,128)(2,1)S(1)}) fusion(bf16[384,2048]{1,0:T(8,128)(2,1)} %reshape.43, s32[256]{0:T(256)S(1)} %multiply_add_fusion), kind=kOutput, calls=%fused_computation.4 | convolution fusion | flops 404848384 | bytes 2623488 | tf_op jit(solution)/shard_map/sr,sc->rc/dot_general | solution.py:93
  182.8 8.5 %psum.7 = f32[256]{0:T(256)S(1)} all-reduce(f32[256]{0:T(256)S(1)} %get-tuple-element.5), channel_id=1, replica_groups=mesh['docs'=64,'mp'=4] {'mp'}, use_global_device_ids=true, to_apply=%region_4.5 | all-reduce | flops 256 | bytes 2048 | tf_op jit(solution)/shard_map/psum | solution.py:96
  191.3 1.3 fusion.2
  (6 shorter events, 0.1 us)
Async XLA Ops:
  7.4 67.0 %all-to-all-start = ((bf16[64,6,2176]{2,1,0:T(8,128)(2,1)}), bf16[64,6,2176]{2,1,0:T(8,128)(2,1)S(1)}, u32[]{:S(2)}, u32[]{:S(2)}) async-start(bf16[64,6,2176]{2,1,0:T(8,128)(2,1)} %reshape.40), calls=%async_computation | async-start | bytes 4456448 | tf_op jit(solution)/shard_map/all_to_all | solution.py:88
  20.5 2.9 %copy-start = (bf16[3202,256]{1,0:T(8,128)(2,1)S(1)}, bf16[3202,256]{1,0:T(8,128)(2,1)}, u32[]{:S(2)}) copy-start(bf16[3202,256]{1,0:T(8,128)(2,1)} %param.8) | copy-start | bytes 4918276
  121.7 6.2 %copy-start.1 = (bf16[2048]{0:T(1024)(128)(2,1)S(1)}, bf16[2048]{0:T(1024)(128)(2,1)}, u32[]{:S(2)}) copy-start(bf16[2048]{0:T(1024)(128)(2,1)} %param.11) | copy-start | bytes 12292
  121.7 57.4 %all-to-all-start.1 = ((bf16[64,6,2048]{2,1,0:T(8,128)(2,1)}), bf16[64,6,2048]{2,1,0:T(8,128)(2,1)S(1)}, u32[]{:S(2)}, u32[]{:S(2)}) async-start(bf16[64,6,2048]{2,1,0:T(8,128)(2,1)} %reshape.42), calls=%async_computation.1 | async-start | bytes 4194304 | tf_op jit(solution)/shard_map/all_to_all | solution.py:91

commit v3 on v2

--- a/solution.py
+++ b/solution.py
@@ -68,6 +68,41 @@
     )(q, q, kp, vp)
 
 
+def exchange_kernel(x_ref, o_ref, send_sem, recv_sem):
+    me = lax.axis_index("docs")
+    col = lax.axis_index("mp")
+    docs = x_ref.shape[0]
+    own = pltpu.make_async_copy(x_ref.at[me], o_ref.at[me], recv_sem)
+    own.start()
+
+    def send(d, carry):
+        peer = lax.rem(me + d, docs)
+        pltpu.make_async_remote_copy(
+            src_ref=x_ref.at[peer],
+            dst_ref=o_ref.at[me],
+            send_sem=send_sem,
+            recv_sem=recv_sem,
+            device_id=(peer, col),
+            device_id_type=pl.DeviceIdType.MESH,
+        ).start()
+        return carry
+
+    lax.fori_loop(1, docs, send, 0)
+    pltpu.make_async_copy(x_ref.at[pl.ds(1, docs - 1)], o_ref.at[pl.ds(1, docs - 1)], send_sem).wait()
+    pltpu.make_async_copy(x_ref, o_ref, recv_sem).wait()
+
+
+def exchange(x):
+    return pl.pallas_call(
+        exchange_kernel,
+        in_specs=[pl.BlockSpec(memory_space=pl.ANY)],
+        out_specs=pl.BlockSpec(memory_space=pl.ANY),
+        out_shape=jax.ShapeDtypeStruct(x.shape, x.dtype),
+        scratch_shapes=[pltpu.SemaphoreType.DMA(()), pltpu.SemaphoreType.DMA(())],
+        compiler_params=pltpu.CompilerParams(has_side_effects=True),
+    )(x)
+
+
 def shards(queries, keys, values, owner_of_row, visible, gain):
     docs = lax.axis_size("docs")
     rows = queries.shape[0]
@@ -85,10 +120,10 @@
     payload = jnp.concatenate([queries, extra], axis=1)
     packed = jnp.dot(place, payload, preferred_element_type=jnp.float32).astype(jnp.bfloat16)
     packed = packed.reshape(docs, cap, width + 128)
-    arrived = lax.all_to_all(packed, "docs", split_axis=0, concat_axis=0, tiled=True)
+    arrived = exchange(packed)
     context = attend(arrived.reshape(docs * cap, width + 128), keys, values)
     context = context.reshape(docs, cap, width)
-    returned = lax.all_to_all(context, "docs", split_axis=0, concat_axis=0, tiled=True)
+    returned = exchange(context)
     flat_back = returned.reshape(docs * cap, width)
     mine = jnp.einsum("sr,sc->rc", place, flat_back, preferred_element_type=jnp.float32).astype(
         jnp.bfloat16

time: 193 us -> 206 us (1.067)
  Pallas kernels: 42.1 us -> 174 us
  waiting for transfers between devices: 101 us -> 0 us
  starting transfers between devices: 19.3 us -> 0 us
  local copies, waits for them, and re-layouts: 12.8 us -> 15.5 us
    pallas_call x0 -> x2, Pallas kernels: none -> 131 us  [exchange(): pl.pallas_call(exchange_kernel, in_specs=[pl.BlockSpec(memory_space=pl.AN...]
    all_to_all x2 -> x0, waiting for transfers between devices: 101 us -> none  [the longest x1 51.2 us: shards(): lax.all_to_all(context, 'docs', split_axis=0, concat_axis=0, tiled=True)]
    all_to_all x2 -> x0, starting transfers between devices: 19.3 us -> none  [the longest x1 13.2 us: shards(): lax.all_to_all(packed, 'docs', split_axis=0, concat_axis=0, tiled=True)]
    reshape x1, local copies, waits for them, and re-layouts: 1.5 us -> 3.92 us  [shards(): context = attend(arrived.reshape(docs * cap, width + 128), keys, values)]
  transfers between devices with their start and end apart: 2 -> 0, of which waited for: 2 -> 0; matrix products, arithmetic and copies ran while one was open for 2% -> 0% of each run, Pallas kernels for 0% -> 0%
where the time goes in v3:
time: 206 us; the launch traced here: 205 us
  Pallas kernels  174 us (84%)
  local copies, waits for them, and re-layouts  15.5 us (8%)
  blocking collectives  8.44 us (4%)
  other arithmetic  4.77 us (2%)
  matrix products  2.7 us (1%)
    pallas_call x2, Pallas kernels, exchange(): pl.pallas_call(exchange_kernel, in_specs=[pl.BlockSpec(memory_space=pl.AN...  131 us
    pallas_call x1, Pallas kernels, attend(): pl.pallas_call(attend_kernel, grid=(kv_local, rows // tm), in_specs=[pl.B...  42.1 us
    psum x1, blocking collectives, shards(): power = lax.psum(squares(mine), 'mp')  8.44 us

profile of v3, /device:TPU:1, one launch (start us, length us, event | category | flops | bytes accessed | tf_op | source)
XLA Modules:
  0.0 205.1 jit_solution(11694793268725587579)
XLA Ops:
  0.0 0.7 fusion.11
  0.7 0.6 reduce-window.6
  1.3 0.2 slice_reduce_fusion
  1.5 0.8 fusion.10
  2.3 0.7 multiply_add_fusion
  3.0 0.7 convert_element_type.32
  3.7 0.1 broadcast_in_dim.2
  3.8 1.9 convolution_convert_fusion
  5.6 1.7 reshape.40.x_ref
  7.3 69.1 %shard_map.64 = bf16[64,6,2176]{2,1,0:T(8,128)(2,1)} custom-call(bf16[64,6,2176]{2,1,0:T(8,128)(2,1)} %reshape.40.x_ref), custom_call_target="tpu_custom_call" | custom-call | tf_op jit(solution)/shard_map/pallas_call | solution.py:96
  76.4 0.0 copy-start
  76.4 3.9 %reshape.41.seen_ref.q_ref = bf16[384,2176]{1,0:T(8,128)(2,1)} reshape(bf16[64,6,2176]{2,1,0:T(8,128)(2,1)} %shard_map.64) | data formatting | bytes 3342336 | tf_op jit(solution)/shard_map/reshape | solution.py:124
  80.3 0.0 copy-done
  80.3 1.3 pad.7.k_ref
  81.6 0.7 copy-done.1
  82.4 1.3 pad.8.v_ref
  83.7 42.1 %shard_map.65 = bf16[384,2048]{1,0:T(8,128)(2,1)} custom-call(bf16[384,2176]{1,0:T(8,128)(2,1)} %reshape.41.seen_ref.q_ref, bf16[384,2176]{1,0:T(8,128)(2,1)} %reshape.41.seen_ref.q_ref, bf16[3328,256]{1,0:T(8,128)(2,1)} %pad.7.k_ref, bf16[3328,256]{1,0:T(8,128)(2,1)} %pad.8.v_ref), custom_call_target="tpu_custom_call" | custom-call | tf_op jit(solution)/shard_map/pallas_call | solution.py:57
  125.8 3.7 %reshape.42.x_ref = bf16[64,6,2048]{2,1,0:T(8,128)(2,1)} reshape(bf16[384,2048]{1,0:T(8,128)(2,1)} %shard_map.65) | data formatting | bytes 3145728 | tf_op jit(solution)/shard_map/reshape | solution.py:125
  129.5 62.4 %shard_map.66 = bf16[64,6,2048]{2,1,0:T(8,128)(2,1)} custom-call(bf16[64,6,2048]{2,1,0:T(8,128)(2,1)} %reshape.42.x_ref), custom_call_target="tpu_custom_call" | custom-call | tf_op jit(solution)/shard_map/pallas_call | solution.py:96
  191.9 2.6 %reshape.43 = bf16[384,2048]{1,0:T(8,128)(2,1)S(1)} reshape(bf16[64,6,2048]{2,1,0:T(8,128)(2,1)} %shard_map.66) | data formatting | bytes 3145728 | tf_op jit(solution)/shard_map/reshape | solution.py:127
  194.5 0.0 copy-start.2
  194.5 0.8 fusion
  195.3 8.4 %psum.7 = f32[256]{0:T(256)S(1)} all-reduce(f32[256]{0:T(256)S(1)} %get-tuple-element.5), channel_id=1, replica_groups=mesh['docs'=64,'mp'=4] {'mp'}, use_global_device_ids=true, to_apply=%region_4.5 | all-reduce | flops 256 | bytes 2048 | tf_op jit(solution)/shard_map/psum | solution.py:131
  203.8 1.3 fusion.2
  (6 shorter events, 0.1 us)
Async XLA Ops:
  76.4 3.9 %copy-start = (bf16[3202,256]{1,0:T(8,128)(2,1)S(1)}, bf16[3202,256]{1,0:T(8,128)(2,1)}, u32[]{:S(2)}) copy-start(bf16[3202,256]{1,0:T(8,128)(2,1)} %param.7) | copy-start | bytes 4918276
  80.3 2.0 copy-start.1
  194.5 9.3 %copy-start.2 = (bf16[2048]{0:T(1024)(128)(2,1)S(1)}, bf16[2048]{0:T(1024)(128)(2,1)}, u32[]{:S(2)}) copy-start(bf16[2048]{0:T(1024)(128)(2,1)} %param.11) | copy-start | bytes 12292

commit v4 on v1

--- a/solution.py
+++ b/solution.py
@@ -29,7 +29,7 @@
     tp = k_ref.shape[0]
     scale = 1.0 / HD**0.5
     limit = seen_ref[...] * IMG_TOK
-    allowed = lax.broadcasted_iota(jnp.int32, (tm, tp), 1) < limit
+    allowed = lax.broadcasted_iota(jnp.int32, (tm, tp), 1).astype(jnp.float32) < limit
     keys = k_ref[...]
     vals = v_ref[...]
     for g in range(GROUP):
@@ -81,20 +81,16 @@
         jnp.bfloat16
     )
     packed = jnp.dot(place, queries, preferred_element_type=jnp.float32).astype(jnp.bfloat16)
-    packed = packed.reshape(docs, cap, width)
-    seen_packed = jnp.dot(place, visible.astype(jnp.bfloat16), preferred_element_type=jnp.float32)
-    seen_packed = seen_packed.astype(jnp.bfloat16).reshape(docs, cap)
-    arrived, arrived_seen = (
-        lax.all_to_all(packed, "docs", split_axis=0, concat_axis=0, tiled=True),
-        lax.all_to_all(seen_packed, "docs", split_axis=0, concat_axis=0, tiled=True),
-    )
-    context = attend(
-        arrived.reshape(-1, width),
-        arrived_seen.reshape(-1, 1).astype(jnp.int32),
-        keys,
-        values,
-    ).reshape(arrived.shape)
-    returned = lax.all_to_all(context, "docs", split_axis=0, concat_axis=0, tiled=True)
+    seen = jnp.dot(place, visible.astype(jnp.bfloat16), preferred_element_type=jnp.float32)
+    lanes = cap * width // 8
+    slabs = packed.reshape(docs, 8, lanes)
+    seen_tile = jnp.pad(seen.astype(jnp.bfloat16).reshape(docs, 1, cap), ((0, 0), (0, 7), (0, 128 - cap)))
+    sent = jnp.concatenate([slabs, seen_tile], axis=2)
+    arrived = lax.all_to_all(sent, "docs", split_axis=0, concat_axis=0, tiled=True)
+    arrived_q = arrived[:, :, :lanes].reshape(docs * cap, width)
+    arrived_seen = arrived[:, 0, lanes : lanes + cap].astype(jnp.float32).reshape(docs * cap, 1)
+    context = attend(arrived_q, arrived_seen, keys, values)
+    returned = lax.all_to_all(context.reshape(docs, 8, lanes), "docs", split_axis=0, concat_axis=0, tiled=True)
     flat_back = returned.reshape(docs * cap, width)
     mine = jnp.einsum("sr,sc->rc", place, flat_back, preferred_element_type=jnp.float32).astype(
         jnp.bfloat16

time: 202 us -> 178 us (0.88)
  waiting for transfers between devices: 104 us -> 78.2 us
  local copies, waits for them, and re-layouts: 14.2 us -> 19.4 us
  starting transfers between devices: 23.9 us -> 19.6 us
    all_to_all x3 -> x2, waiting for transfers between devices: 104 us -> 78.2 us  [the longest x1 39.8 us: shards(): lax.all_to_all(context.reshape(docs, 8, lanes), 'docs', split_axis=0, con...]
    all_to_all x3 -> x2, starting transfers between devices: 23.9 us -> 19.6 us  [the longest x1 13.2 us: shards(): lax.all_to_all(sent, 'docs', split_axis=0, concat_axis=0, tiled=True)]
    reshape x3 -> x4, local copies, waits for them, and re-layouts: 6.8 us -> 10.8 us  [the longest x1 3.87 us: shards(): context.reshape(docs, 8, lanes)]
  transfers between devices with their start and end apart: 3 -> 2, of which waited for: 3 -> 2; matrix products, arithmetic and copies ran while one was open for 4% -> 2% of each run, Pallas kernels for 0% -> 0%
where the time goes in v4:
time: 178 us
  waiting for transfers between devices  78.2 us (44%)
  Pallas kernels  42.1 us (24%)
  starting transfers between devices  19.6 us (11%)
  local copies, waits for them, and re-layouts  19.4 us (11%)
  blocking collectives  8.47 us (5%)
  other arithmetic  5.63 us (3%)
  matrix products  4.18 us (2%)
    pallas_call x1, Pallas kernels, attend(): pl.pallas_call(attend_kernel, grid=(kv_local, rows // tm), in_specs=[pl.B...  42.1 us
    all_to_all x1, waiting for transfers between devices, shards(): lax.all_to_all(context.reshape(docs, 8, lanes), 'docs', split_axis=0, con...  39.8 us
    all_to_all x1, waiting for transfers between devices, shards(): lax.all_to_all(sent, 'docs', split_axis=0, concat_axis=0, tiled=True)  38.4 us
    all_to_all x1, starting transfers between devices, shards(): lax.all_to_all(sent, 'docs', split_axis=0, concat_axis=0, tiled=True)  13.2 us
    psum x1, blocking collectives, shards(): power = lax.psum(squares(mine), 'mp')  8.47 us
    all_to_all x1, starting transfers between devices, shards(): lax.all_to_all(context.reshape(docs, 8, lanes), 'docs', split_axis=0, con...  6.4 us
    reshape x1, local copies, waits for them, and re-layouts, shards(): context.reshape(docs, 8, lanes)  3.87 us
    reshape x1, local copies, waits for them, and re-layouts, shards(): arrived_q = arrived[:, :, :lanes].reshape(docs * cap, width)  3.86 us
  transfers between devices with their start and end apart: 2, of which 2 were waited for; matrix products, arithmetic and copies ran while one was open for 2% of the time, Pallas kernels for 0%

profile of v4, /device:TPU:1, one launch (start us, length us, event | category | flops | bytes accessed | tf_op | source)
XLA Modules:
  0.0 177.7 jit_solution(16265040112839149929)
XLA Ops:
  0.0 0.8 fusion.11
  0.8 0.6 reduce-window.6
  1.4 0.2 slice_reduce_fusion
  1.6 0.8 fusion.10
  2.4 0.7 multiply_add_fusion
  3.1 1.7 convolution_convert_fusion
  4.8 2.9 %reshape.55 = bf16[64,8,1536]{2,1,0:T(8,128)(2,1)S(1)} reshape(bf16[384,2048]{1,0:T(8,128)(2,1)} %convolution_convert_fusion) | data formatting | bytes 3145728 | tf_op jit(solution)/shard_map/reshape | solution.py:86
  7.8 0.2 convolution_reduce_fusion
  8.1 1.4 fusion.4
  9.5 13.2 %all-to-all-start = ((bf16[64,8,1664]{2,1,0:T(8,128)(2,1)}), bf16[64,8,1664]{2,1,0:T(8,128)(2,1)S(1)}, u32[]{:S(2)}, u32[]{:S(2)}) async-start(bf16[64,8,1664]{2,1,0:T(8,128)(2,1)} %fusion.4), calls=%async_computation | async-start | bytes 3407872 | tf_op jit(solution)/shard_map/all_to_all | solution.py:89
  22.7 2.9 %pad.12.k_ref = bf16[3328,256]{1,0:T(8,128)(2,1)} pad(bf16[3202,256]{1,0:T(8,128)(2,1)} %param.7, bf16[]{:T(256)} %constant.13.clone.1), padding=0_126x0_0 | pad | bytes 3343362 | tf_op jit(solution)/shard_map/jit(_pad)/pad | solution.py:53
  25.5 1.3 pad.13.v_ref
  26.8 38.4 %all-to-all-done = bf16[64,8,1664]{2,1,0:T(8,128)(2,1)S(1)} async-done(((bf16[64,8,1664]{2,1,0:T(8,128)(2,1)}), bf16[64,8,1664]{2,1,0:T(8,128)(2,1)S(1)}, u32[]{:S(2)}, u32[]{:S(2)}) %all-to-all-start) | async-done | bytes 1703968 | tf_op jit(solution)/shard_map/all_to_all | solution.py:89
  65.3 1.3 slice.18
  66.6 3.9 %reshape.57.q_ref = bf16[384,2048]{1,0:T(8,128)(2,1)} reshape(bf16[64,8,1536]{2,1,0:T(8,128)(2,1)} %slice.18) | data formatting | bytes 3145728 | tf_op jit(solution)/shard_map/reshape | solution.py:90
  70.5 0.8 reshape.63.seen_ref
  71.3 42.1 %shard_map.64 = bf16[384,2048]{1,0:T(8,128)(2,1)} custom-call(f32[384,1]{1,0:T(8,128)} %reshape.63.seen_ref, bf16[384,2048]{1,0:T(8,128)(2,1)} %reshape.57.q_ref, bf16[3328,256]{1,0:T(8,128)(2,1)} %pad.12.k_ref, bf16[3328,256]{1,0:T(8,128)(2,1)} %pad.13.v_ref), custom_call_target="tpu_custom_call" | custom-call | tf_op jit(solution)/shard_map/pallas_call | solution.py:56
  113.4 3.9 %reshape.58 = bf16[64,8,1536]{2,1,0:T(8,128)(2,1)} reshape(bf16[384,2048]{1,0:T(8,128)(2,1)} %shard_map.64) | data formatting | bytes 3145728 | tf_op jit(solution)/shard_map/reshape | solution.py:93
  117.3 6.4 %all-to-all-start.1 = ((bf16[64,8,1536]{2,1,0:T(8,128)(2,1)}), bf16[64,8,1536]{2,1,0:T(8,128)(2,1)S(1)}, u32[]{:S(2)}, u32[]{:S(2)}) async-start(bf16[64,8,1536]{2,1,0:T(8,128)(2,1)} %reshape.58), calls=%async_computation.1 | async-start | bytes 3145728 | tf_op jit(solution)/shard_map/all_to_all | solution.py:93
  123.7 39.8 %all-to-all-done.1 = bf16[64,8,1536]{2,1,0:T(8,128)(2,1)S(1)} async-done(((bf16[64,8,1536]{2,1,0:T(8,128)(2,1)}), bf16[64,8,1536]{2,1,0:T(8,128)(2,1)S(1)}, u32[]{:S(2)}, u32[]{:S(2)}) %all-to-all-start.1) | async-done | bytes 1572896 | tf_op jit(solution)/shard_map/all_to_all | solution.py:93
  163.5 2.2 %reshape.59 = bf16[384,2048]{1,0:T(8,128)(2,1)} reshape(bf16[64,8,1536]{2,1,0:T(8,128)(2,1)S(1)} %all-to-all-done.1) | data formatting | bytes 3145728 | tf_op jit(solution)/shard_map/reshape | solution.py:94
  165.7 2.2 %fusion.1 = (f32[256]{0:T(256)S(1)}, bf16[256,2048]{1,0:T(8,128)(2,1)S(1)}) fusion(bf16[384,2048]{1,0:T(8,128)(2,1)} %reshape.59, s32[256]{0:T(256)S(1)} %multiply_add_fusion), kind=kOutput, calls=%fused_computation.6 | convolution fusion | flops 404848384 | bytes 2623488 | tf_op jit(solution)/shard_map/sr,sc->rc/dot_general | solution.py:95
  167.9 8.5 %psum.7 = f32[256]{0:T(256)S(1)} all-reduce(f32[256]{0:T(256)S(1)} %get-tuple-element.5), channel_id=1, replica_groups=mesh['docs'=64,'mp'=4] {'mp'}, use_global_device_ids=true, to_apply=%region_4.5 | all-reduce | flops 256 | bytes 2048 | tf_op jit(solution)/shard_map/psum | solution.py:98
  176.4 1.3 fusion.3
  (16 shorter events, 0.3 us)
Async XLA Ops:
  0.0 3.1 %copy-start = (bf16[256,2048]{1,0:T(8,128)(2,1)S(1)}, bf16[256,2048]{1,0:T(8,128)(2,1)}, u32[]{:S(2)}) copy-start(bf16[256,2048]{1,0:T(8,128)(2,1)} %param.6) | copy-start | bytes 3145732
  4.8 2.9 %copy-start.3 = (s32[256]{0:T(256)S(1)}, s32[256]{0:T(256)}, u32[]{:S(2)}) copy-start(s32[256]{0:T(256)} %param.10) | copy-start | bytes 3076
  9.5 55.8 %all-to-all-start = ((bf16[64,8,1664]{2,1,0:T(8,128)(2,1)}), bf16[64,8,1664]{2,1,0:T(8,128)(2,1)S(1)}, u32[]{:S(2)}, u32[]{:S(2)}) async-start(bf16[64,8,1664]{2,1,0:T(8,128)(2,1)} %fusion.4), calls=%async_computation | async-start | bytes 3407872 | tf_op jit(solution)/shard_map/all_to_all | solution.py:89
  22.7 2.9 %copy-start.1 = (bf16[3202,256]{1,0:T(8,128)(2,1)S(1)}, bf16[3202,256]{1,0:T(8,128)(2,1)}, u32[]{:S(2)}) copy-start(bf16[3202,256]{1,0:T(8,128)(2,1)} %param.8) | copy-start | bytes 4918276
  117.3 6.4 %copy-start.2 = (bf16[2048]{0:T(1024)(128)(2,1)S(1)}, bf16[2048]{0:T(1024)(128)(2,1)}, u32[]{:S(2)}) copy-start(bf16[2048]{0:T(1024)(128)(2,1)} %param.11) | copy-start | bytes 12292
  117.3 46.2 %all-to-all-start.1 = ((bf16[64,8,1536]{2,1,0:T(8,128)(2,1)}), bf16[64,8,1536]{2,1,0:T(8,128)(2,1)S(1)}, u32[]{:S(2)}, u32[]{:S(2)}) async-start(bf16[64,8,1536]{2,1,0:T(8,128)(2,1)} %reshape.58), calls=%async_computation.1 | async-start | bytes 3145728 | tf_op jit(solution)/shard_map/all_to_all | solution.py:93

commit v5 on v4

--- a/solution.py
+++ b/solution.py
@@ -64,6 +64,11 @@
         ],
         out_specs=pl.BlockSpec((tm, GROUP * HD), lambda k, i: (i, k)),
         out_shape=jax.ShapeDtypeStruct((rows, width), jnp.bfloat16),
+        cost_estimate=pl.CostEstimate(
+            flops=4 * rows * width * padded,
+            transcendentals=rows * (width // HD) * padded,
+            bytes_accessed=4 * rows * width + 4 * padded * kv_local * HD,
+        ),
     )(seen, q, kp, vp)
 
 
@@ -82,15 +87,23 @@
     )
     packed = jnp.dot(place, queries, preferred_element_type=jnp.float32).astype(jnp.bfloat16)
     seen = jnp.dot(place, visible.astype(jnp.bfloat16), preferred_element_type=jnp.float32)
-    lanes = cap * width // 8
-    slabs = packed.reshape(docs, 8, lanes)
-    seen_tile = jnp.pad(seen.astype(jnp.bfloat16).reshape(docs, 1, cap), ((0, 0), (0, 7), (0, 128 - cap)))
-    sent = jnp.concatenate([slabs, seen_tile], axis=2)
-    arrived = lax.all_to_all(sent, "docs", split_axis=0, concat_axis=0, tiled=True)
-    arrived_q = arrived[:, :, :lanes].reshape(docs * cap, width)
-    arrived_seen = arrived[:, 0, lanes : lanes + cap].astype(jnp.float32).reshape(docs * cap, 1)
-    context = attend(arrived_q, arrived_seen, keys, values)
-    returned = lax.all_to_all(context.reshape(docs, 8, lanes), "docs", split_axis=0, concat_axis=0, tiled=True)
+    packed = packed.reshape(docs, cap, width)
+    seen = seen.astype(jnp.bfloat16).reshape(docs, cap)
+    half = cap // 2
+    lanes = half * width // 8
+    pieces = []
+    for part in range(2):
+        rank_rows = slice(part * half, (part + 1) * half)
+        slabs = packed[:, rank_rows].reshape(docs, 8, lanes)
+        seen_tile = jnp.pad(seen[:, rank_rows].reshape(docs, 1, half), ((0, 0), (0, 7), (0, 128 - half)))
+        sent = jnp.concatenate([slabs, seen_tile], axis=2)
+        arrived = lax.all_to_all(sent, "docs", split_axis=0, concat_axis=0, tiled=True)
+        arrived_q = arrived[:, :, :lanes].reshape(docs * half, width)
+        arrived_seen = arrived[:, 0, lanes : lanes + half].astype(jnp.float32).reshape(docs * half, 1)
+        context = attend(arrived_q, arrived_seen, keys, values)
+        back = lax.all_to_all(context.reshape(docs, 8, lanes), "docs", split_axis=0, concat_axis=0, tiled=True)
+        pieces.append(back.reshape(docs, half, width))
+    returned = jnp.concatenate(pieces, axis=1)
     flat_back = returned.reshape(docs * cap, width)
     mine = jnp.einsum("sr,sc->rc", place, flat_back, preferred_element_type=jnp.float32).astype(
         jnp.bfloat16

time: 178 us -> 221 us (1.24)
  Pallas kernels: 42.1 us -> 67.4 us
  waiting for transfers between devices: 78.2 us -> 61.6 us
  starting transfers between devices: 19.6 us -> 35.9 us
  local copies, waits for them, and re-layouts: 19.4 us -> 30.8 us
  other arithmetic: 5.63 us -> 11.4 us
    pallas_call x1 -> x2, Pallas kernels: 42.1 us -> 67.4 us  [attend(): pl.pallas_call(attend_kernel, grid=(kv_local, rows // tm), in_specs=[pl.B...]
    all_to_all x1 -> x2, waiting for transfers between devices: 39.8 us -> 21.7 us  [shards(): lax.all_to_all(context.reshape(docs, 8, lanes), 'docs', split_axis=0, con...]
    all_to_all x1 -> x2, starting transfers between devices: 6.4 us -> 16.5 us  [shards(): lax.all_to_all(context.reshape(docs, 8, lanes), 'docs', split_axis=0, con...]
    reshape x3 -> x11, local copies, waits for them, and re-layouts: 6.92 us -> 13.9 us  [the longest x2 4.45 us: shards(): arrived_q = arrived[:, :, :lanes].reshape(docs * half, width)]
    all_to_all x1 -> x2, starting transfers between devices: 13.2 us -> 19.4 us  [shards(): lax.all_to_all(sent, 'docs', split_axis=0, concat_axis=0, tiled=True)]
    concatenate x0 -> x1, other arithmetic: none -> 2.61 us  [shards(): returned = jnp.concatenate(pieces, axis=1)]
    reshape x1 -> x2, local copies, waits for them, and re-layouts: 3.87 us -> 5.38 us  [shards(): context.reshape(docs, 8, lanes)]
    all_to_all x1 -> x2, waiting for transfers between devices: 38.4 us -> 39.9 us  [shards(): lax.all_to_all(sent, 'docs', split_axis=0, concat_axis=0, tiled=True)]
  transfers between devices with their start and end apart: 2 -> 4, of which waited for: 2 -> 3; matrix products, arithmetic and copies ran while one was open for 2% -> 9% of each run, Pallas kernels for 0% -> 15%
where the time goes in v5:
time: 221 us; the launch traced here: 220 us
  Pallas kernels  67.4 us (30%)
  waiting for transfers between devices  61.6 us (28%)
  starting transfers between devices  35.9 us (16%)
  local copies, waits for them, and re-layouts  30.8 us (14%)
  other arithmetic  11.4 us (5%)
  blocking collectives  8.47 us (4%)
  matrix products  4.19 us (2%)
    pallas_call x2, Pallas kernels, attend(): pl.pallas_call(attend_kernel, grid=(kv_local, rows // tm), in_specs=[pl.B...  67.4 us
    all_to_all x2, waiting for transfers between devices, shards(): lax.all_to_all(sent, 'docs', split_axis=0, concat_axis=0, tiled=True)  39.9 us
    all_to_all x2, waiting for transfers between devices, shards(): lax.all_to_all(context.reshape(docs, 8, lanes), 'docs', split_axis=0, con...  21.7 us
    all_to_all x2, starting transfers between devices, shards(): lax.all_to_all(sent, 'docs', split_axis=0, concat_axis=0, tiled=True)  19.4 us
    all_to_all x2, starting transfers between devices, shards(): lax.all_to_all(context.reshape(docs, 8, lanes), 'docs', split_axis=0, con...  16.5 us
    psum x1, blocking collectives, shards(): power = lax.psum(squares(mine), 'mp')  8.47 us
    reshape x2, local copies, waits for them, and re-layouts, shards(): context.reshape(docs, 8, lanes)  5.38 us
    reshape x2, local copies, waits for them, and re-layouts, shards(): arrived_q = arrived[:, :, :lanes].reshape(docs * half, width)  4.45 us
  transfers between devices with their start and end apart: 4, of which 3 were waited for; matrix products, arithmetic and copies ran while one was open for 9% of the time, Pallas kernels for 15%

profile of v5, /device:TPU:1, one launch (start us, length us, event | category | flops | bytes accessed | tf_op | source)
XLA Modules:
  0.0 219.9 jit_solution(16406427309258450812)
XLA Ops:
  4.3 1.7 convolution_convert_fusion
  6.0 2.5 %reshape.92 = bf16[64,6,2048]{2,1,0:T(8,128)(2,1)S(1)} reshape(bf16[384,2048]{1,0:T(8,128)(2,1)} %convolution_convert_fusion) | data formatting | bytes 3145728 | tf_op jit(solution)/shard_map/reshape | solution.py:90
  8.5 2.5 %fusion.16 = (bf16[64,3,2048]{2,1,0:T(4,128)(2,1)}, bf16[64,3,2048]{2,1,0:T(4,128)(2,1)}) fusion(bf16[64,6,2048]{2,1,0:T(8,128)(2,1)S(1)} %reshape.92), kind=kLoop, calls=%fused_computation.35 | loop fusion | bytes 3145728 | tf_op jit(solution)/shard_map/slice | solution.py:97
  11.0 2.5 %reshape.93 = bf16[64,8,768]{2,1,0:T(8,128)(2,1)S(1)} reshape(bf16[64,3,2048]{2,1,0:T(4,128)(2,1)} %get-tuple-element.5) | data formatting | bytes 1572864 | tf_op jit(solution)/shard_map/reshape | solution.py:97
  14.6 13.2 %all-to-all-start = ((bf16[64,8,896]{2,1,0:T(8,128)(2,1)}), bf16[64,8,896]{2,1,0:T(8,128)(2,1)S(1)}, u32[]{:S(2)}, u32[]{:S(2)}) async-start(bf16[64,8,896]{2,1,0:T(8,128)(2,1)} %fusion.5), calls=%async_computation | async-start | bytes 1835008 | tf_op jit(solution)/shard_map/all_to_all | solution.py:100
  27.8 1.6 reshape.99
  29.4 2.1 fusion.6
  31.6 21.9 %all-to-all-done = bf16[64,8,896]{2,1,0:T(8,128)(2,1)S(1)} async-done(((bf16[64,8,896]{2,1,0:T(8,128)(2,1)}), bf16[64,8,896]{2,1,0:T(8,128)(2,1)S(1)}, u32[]{:S(2)}, u32[]{:S(2)}) %all-to-all-start) | async-done | bytes 917536 | tf_op jit(solution)/shard_map/all_to_all | solution.py:100
  53.5 6.2 %all-to-all-start.2 = ((bf16[64,8,896]{2,1,0:T(8,128)(2,1)}), bf16[64,8,896]{2,1,0:T(8,128)(2,1)S(1)}, u32[]{:S(2)}, u32[]{:S(2)}) async-start(bf16[64,8,896]{2,1,0:T(8,128)(2,1)} %fusion.6), calls=%async_computation.2 | async-start | bytes 1835008 | tf_op jit(solution)/shard_map/all_to_all | solution.py:100
  59.8 2.9 %pad.17.k_ref = bf16[3328,256]{1,0:T(8,128)(2,1)} pad(bf16[3202,256]{1,0:T(8,128)(2,1)} %param.7, bf16[]{:T(256)} %constant.13.clone.1), padding=0_126x0_0 | pad | bytes 3343362 | tf_op jit(solution)/shard_map/jit(_pad)/pad | solution.py:53
  64.8 2.7 %reshape.96.q_ref = bf16[192,2048]{1,0:T(8,128)(2,1)} reshape(bf16[64,8,768]{2,1,0:T(8,128)(2,1)} %slice.44) | data formatting | bytes 1572864 | tf_op jit(solution)/shard_map/reshape | solution.py:101
  67.5 18.0 %all-to-all-done.2 = bf16[64,8,896]{2,1,0:T(8,128)(2,1)S(1)} async-done(((bf16[64,8,896]{2,1,0:T(8,128)(2,1)}), bf16[64,8,896]{2,1,0:T(8,128)(2,1)S(1)}, u32[]{:S(2)}, u32[]{:S(2)}) %all-to-all-start.2) | async-done | bytes 917536 | tf_op jit(solution)/shard_map/all_to_all | solution.py:100
  86.9 33.7 %shard_map.64 = bf16[192,2048]{1,0:T(8,128)(2,1)} custom-call(f32[192,1]{1,0:T(8,128)} %reshape.109.seen_ref, bf16[192,2048]{1,0:T(8,128)(2,1)} %reshape.96.q_ref, bf16[3328,256]{1,0:T(8,128)(2,1)} %pad.17.k_ref, bf16[3328,256]{1,0:T(8,128)(2,1)} %pad.18.v_ref), custom_call_target="tpu_custom_call" | custom-call | flops 5234491392 | bytes 4980736 | tf_op jit(solution)/shard_map/pallas_call | solution.py:56
  120.6 2.7 %reshape.97 = bf16[64,8,768]{2,1,0:T(8,128)(2,1)} reshape(bf16[192,2048]{1,0:T(8,128)(2,1)} %shard_map.64) | data formatting | bytes 1572864 | tf_op jit(solution)/shard_map/reshape | solution.py:104
  123.3 6.2 %all-to-all-start.1 = ((bf16[64,8,768]{2,1,0:T(8,128)(2,1)}), bf16[64,8,768]{2,1,0:T(8,128)(2,1)S(1)}, u32[]{:S(2)}, u32[]{:S(2)}) async-start(bf16[64,8,768]{2,1,0:T(8,128)(2,1)} %reshape.97), calls=%async_computation.1 | async-start | bytes 1572864 | tf_op jit(solution)/shard_map/all_to_all | solution.py:104
  129.6 1.8 reshape.101.q_ref
  131.4 1.5 reshape.110.seen_ref
  132.8 33.7 %shard_map.65 = bf16[192,2048]{1,0:T(8,128)(2,1)} custom-call(f32[192,1]{1,0:T(8,128)} %reshape.110.seen_ref, bf16[192,2048]{1,0:T(8,128)(2,1)} %reshape.101.q_ref, bf16[3328,256]{1,0:T(8,128)(2,1)} %pad.17.k_ref, bf16[3328,256]{1,0:T(8,128)(2,1)} %pad.18.v_ref), custom_call_target="tpu_custom_call" | custom-call | flops 5234491392 | bytes 4980736 | tf_op jit(solution)/shard_map/pallas_call | solution.py:56
  166.6 2.7 %reshape.102 = bf16[64,8,768]{2,1,0:T(8,128)(2,1)} reshape(bf16[192,2048]{1,0:T(8,128)(2,1)} %shard_map.65) | data formatting | bytes 1572864 | tf_op jit(solution)/shard_map/reshape | solution.py:104
  169.2 10.3 %all-to-all-start.3 = ((bf16[64,8,768]{2,1,0:T(8,128)(2,1)}), bf16[64,8,768]{2,1,0:T(8,128)(2,1)S(1)}, u32[]{:S(2)}, u32[]{:S(2)}) async-start(bf16[64,8,768]{2,1,0:T(8,128)(2,1)} %reshape.102), calls=%async_computation.3 | async-start | bytes 1572864 | tf_op jit(solution)/shard_map/all_to_all | solution.py:104
  180.9 21.7 %all-to-all-done.3 = bf16[64,8,768]{2,1,0:T(8,128)(2,1)S(1)} async-done(((bf16[64,8,768]{2,1,0:T(8,128)(2,1)}), bf16[64,8,768]{2,1,0:T(8,128)(2,1)S(1)}, u32[]{:S(2)}, u32[]{:S(2)}) %all-to-all-start.3) | async-done | bytes 786464 | tf_op jit(solution)/shard_map/all_to_all | solution.py:104
  203.8 2.6 %pad_maximum_fusion = bf16[64,6,2048]{2,1,0:T(8,128)(2,1)S(1)} fusion(bf16[64,3,2048]{2,1,0:T(4,128)(2,1)} %reshape.103, bf16[64,3,2048]{2,1,0:T(4,128)(2,1)} %reshape.98), kind=kLoop, calls=%fused_computation.7 | loop fusion | flops 3145728 | bytes 3145728 | tf_op jit(solution)/shard_map/concatenate | solution.py:106
  207.8 2.2 %fusion = (f32[256]{0:T(256)S(1)}, bf16[256,2048]{1,0:T(8,128)(2,1)S(1)}) fusion(bf16[384,2048]{1,0:T(8,128)(2,1)} %reshape.104, s32[256]{0:T(256)S(1)} %multiply_add_fusion), kind=kOutput, calls=%fused_computation.4 | convolution fusion | flops 404848384 | bytes 2623488 | tf_op jit(solution)/shard_map/sr,sc->rc/dot_general | solution.py:108
  210.1 8.5 %psum.7 = f32[256]{0:T(256)S(1)} all-reduce(f32[256]{0:T(256)S(1)} %get-tuple-element.9), channel_id=1, replica_groups=mesh['docs'=64,'mp'=4] {'mp'}, use_global_device_ids=true, to_apply=%region_4.5 | all-reduce | flops 256 | bytes 2048 | tf_op jit(solution)/shard_map/psum | solution.py:111
  (35 shorter events, 14.3 us)
Async XLA Ops:
  0.0 4.3 %copy-start = (bf16[256,2048]{1,0:T(8,128)(2,1)S(1)}, bf16[256,2048]{1,0:T(8,128)(2,1)}, u32[]{:S(2)}) copy-start(bf16[256,2048]{1,0:T(8,128)(2,1)} %param.6) | copy-start | bytes 3145732
  13.6 14.3 %copy-start.1 = (bf16[64,3,2048]{2,1,0:T(4,128)(2,1)S(1)}, bf16[64,3,2048]{2,1,0:T(4,128)(2,1)}, u32[]{:S(2)}) copy-start(bf16[64,3,2048]{2,1,0:T(4,128)(2,1)} %get-tuple-element.6) | copy-start | bytes 2359300
  14.6 38.9 %all-to-all-start = ((bf16[64,8,896]{2,1,0:T(8,128)(2,1)}), bf16[64,8,896]{2,1,0:T(8,128)(2,1)S(1)}, u32[]{:S(2)}, u32[]{:S(2)}) async-start(bf16[64,8,896]{2,1,0:T(8,128)(2,1)} %fusion.5), calls=%async_computation | async-start | bytes 1835008 | tf_op jit(solution)/shard_map/all_to_all | solution.py:100
  53.5 32.0 %all-to-all-start.2 = ((bf16[64,8,896]{2,1,0:T(8,128)(2,1)}), bf16[64,8,896]{2,1,0:T(8,128)(2,1)S(1)}, u32[]{:S(2)}, u32[]{:S(2)}) async-start(bf16[64,8,896]{2,1,0:T(8,128)(2,1)} %fusion.6), calls=%async_computation.2 | async-start | bytes 1835008 | tf_op jit(solution)/shard_map/all_to_all | solution.py:100
  59.8 2.9 %copy-start.2 = (bf16[3202,256]{1,0:T(8,128)(2,1)S(1)}, bf16[3202,256]{1,0:T(8,128)(2,1)}, u32[]{:S(2)}) copy-start(bf16[3202,256]{1,0:T(8,128)(2,1)} %param.8) | copy-start | bytes 4918276
  123.3 45.9 %all-to-all-start.1 = ((bf16[64,8,768]{2,1,0:T(8,128)(2,1)}), bf16[64,8,768]{2,1,0:T(8,128)(2,1)S(1)}, u32[]{:S(2)}, u32[]{:S(2)}) async-start(bf16[64,8,768]{2,1,0:T(8,128)(2,1)} %reshape.97), calls=%async_computation.1 | async-start | bytes 1572864 | tf_op jit(solution)/shard_map/all_to_all | solution.py:104
  166.6 13.0 %copy-start.3 = (bf16[2048]{0:T(1024)(128)(2,1)S(1)}, bf16[2048]{0:T(1024)(128)(2,1)}, u32[]{:S(2)}) copy-start(bf16[2048]{0:T(1024)(128)(2,1)} %param.11) | copy-start | bytes 12292
  169.2 33.3 %all-to-all-start.3 = ((bf16[64,8,768]{2,1,0:T(8,128)(2,1)}), bf16[64,8,768]{2,1,0:T(8,128)(2,1)S(1)}, u32[]{:S(2)}, u32[]{:S(2)}) async-start(bf16[64,8,768]{2,1,0:T(8,128)(2,1)} %reshape.102), calls=%async_computation.3 | async-start | bytes 1572864 | tf_op jit(solution)/shard_map/all_to_all | solution.py:104

commit v6 on v4

--- a/solution.py
+++ b/solution.py
@@ -26,7 +26,7 @@
 
 def attend_kernel(seen_ref, q_ref, k_ref, v_ref, o_ref):
     tm = q_ref.shape[0]
-    tp = k_ref.shape[0]
+    tp = k_ref.shape[1]
     scale = 1.0 / HD**0.5
     limit = seen_ref[...] * IMG_TOK
     allowed = lax.broadcasted_iota(jnp.int32, (tm, tp), 1).astype(jnp.float32) < limit
@@ -34,9 +34,7 @@
     vals = v_ref[...]
     for g in range(GROUP):
         q = q_ref[:, g * HD : (g + 1) * HD]
-        s = lax.dot_general(
-            q, keys, (((1,), (1,)), ((), ())), preferred_element_type=jnp.float32
-        ) * scale
+        s = jnp.dot(q, keys, preferred_element_type=jnp.float32) * scale
         s = jnp.where(allowed, s, jnp.float32(-1e30))
         top = jnp.max(s, axis=1, keepdims=True)
         w = jnp.exp(s - top)
@@ -51,19 +49,25 @@
     padded = -(-tokens // 128) * 128
     kv_local = keys.shape[1] // HD
     kp = jnp.pad(keys, ((0, padded - tokens), (0, 0)))
+    kp = kp.reshape(padded, kv_local, HD).transpose(1, 2, 0)
     vp = jnp.pad(values, ((0, padded - tokens), (0, 0)))
-    tm = math.gcd(rows, 128)
+    tm = math.gcd(rows, 384)
     return pl.pallas_call(
         attend_kernel,
         grid=(kv_local, rows // tm),
         in_specs=[
             pl.BlockSpec((tm, 1), lambda k, i: (i, 0)),
             pl.BlockSpec((tm, GROUP * HD), lambda k, i: (i, k)),
-            pl.BlockSpec((padded, HD), lambda k, i: (0, k)),
+            pl.BlockSpec((None, HD, padded), lambda k, i: (k, 0, 0)),
             pl.BlockSpec((padded, HD), lambda k, i: (0, k)),
         ],
         out_specs=pl.BlockSpec((tm, GROUP * HD), lambda k, i: (i, k)),
         out_shape=jax.ShapeDtypeStruct((rows, width), jnp.bfloat16),
+        cost_estimate=pl.CostEstimate(
+            flops=4 * rows * width * padded,
+            transcendentals=rows * (width // HD) * padded,
+            bytes_accessed=4 * rows * width + 4 * padded * kv_local * HD,
+        ),
     )(seen, q, kp, vp)
 
 

time: 178 us -> 175 us (0.983)
  Pallas kernels: 42.1 us -> 39 us
  waiting for transfers between devices: 78.2 us -> 76.2 us
    unnamed x8 -> x9, local copies, waits for them, and re-layouts: 0.02 us -> 3.46 us
    pallas_call x1, Pallas kernels: 42.1 us -> 39 us  [attend(): pl.pallas_call(attend_kernel, grid=(kv_local, rows // tm), in_specs=[pl.B...]
    all_to_all x1, waiting for transfers between devices: 38.4 us -> 36.5 us  [shards(): lax.all_to_all(sent, 'docs', split_axis=0, concat_axis=0, tiled=True)]
  transfers between devices with their start and end apart: 2 -> 2, of which waited for: 2 -> 2; matrix products, arithmetic and copies ran while one was open for 2% -> 3% of each run, Pallas kernels for 0% -> 0%
where the time goes in v6:
time: 175 us; the launch traced here: 174 us
  waiting for transfers between devices  76.2 us (44%)
  Pallas kernels  39 us (22%)
  local copies, waits for them, and re-layouts  19.9 us (11%)
  starting transfers between devices  19.6 us (11%)
  blocking collectives  8.47 us (5%)
  other arithmetic  6.58 us (4%)
  matrix products  4.18 us (2%)
    all_to_all x1, waiting for transfers between devices, shards(): lax.all_to_all(context.reshape(docs, 8, lanes), 'docs', split_axis=0, con...  39.8 us
    pallas_call x1, Pallas kernels, attend(): pl.pallas_call(attend_kernel, grid=(kv_local, rows // tm), in_specs=[pl.B...  39 us
    all_to_all x1, waiting for transfers between devices, shards(): lax.all_to_all(sent, 'docs', split_axis=0, concat_axis=0, tiled=True)  36.5 us
    all_to_all x1, starting transfers between devices, shards(): lax.all_to_all(sent, 'docs', split_axis=0, concat_axis=0, tiled=True)  13.3 us
    psum x1, blocking collectives, shards(): power = lax.psum(squares(mine), 'mp')  8.47 us
    all_to_all x1, starting transfers between devices, shards(): lax.all_to_all(context.reshape(docs, 8, lanes), 'docs', split_axis=0, con...  6.23 us
    reshape x1, local copies, waits for them, and re-layouts, shards(): context.reshape(docs, 8, lanes)  3.87 us
  transfers between devices with their start and end apart: 2, of which 2 were waited for; matrix products, arithmetic and copies ran while one was open for 3% of the time, Pallas kernels for 0%

profile of v6, /device:TPU:1, one launch (start us, length us, event | category | flops | bytes accessed | tf_op | source)
XLA Modules:
  0.0 174.0 jit_solution(94431463977070750)
XLA Ops:
  0.0 0.8 fusion.11
  1.6 0.8 fusion.10
  2.4 0.7 multiply_add_fusion
  3.1 1.7 convolution_convert_fusion
  4.8 2.9 %reshape.58 = bf16[64,8,1536]{2,1,0:T(8,128)(2,1)S(1)} reshape(bf16[384,2048]{1,0:T(8,128)(2,1)} %convolution_convert_fusion) | data formatting | bytes 3145728 | tf_op jit(solution)/shard_map/reshape | solution.py:90
  8.1 1.4 fusion.4
  9.5 13.3 %all-to-all-start = ((bf16[64,8,1664]{2,1,0:T(8,128)(2,1)}), bf16[64,8,1664]{2,1,0:T(8,128)(2,1)}, u32[]{:S(2)}, u32[]{:S(2)}) async-start(bf16[64,8,1664]{2,1,0:T(8,128)(2,1)} %fusion.4), calls=%async_computation | async-start | bytes 3407872 | tf_op jit(solution)/shard_map/all_to_all | solution.py:93
  22.9 2.7 %copy.18 = bf16[3202,256]{0,1:T(8,128)(2,1)S(1)} copy(bf16[3202,256]{1,0:T(8,128)(2,1)} %param.7) | data formatting | bytes 3278848
  25.6 1.3 pad.12.clone
  26.9 0.7 copy-done.1
  27.6 1.3 pad.13.v_ref
  28.9 36.5 %all-to-all-done = bf16[64,8,1664]{2,1,0:T(8,128)(2,1)} async-done(((bf16[64,8,1664]{2,1,0:T(8,128)(2,1)}), bf16[64,8,1664]{2,1,0:T(8,128)(2,1)}, u32[]{:S(2)}, u32[]{:S(2)}) %all-to-all-start) | async-done | bytes 1703968 | tf_op jit(solution)/shard_map/all_to_all | solution.py:93
  65.4 1.5 slice.18
  66.9 2.2 %reshape.60.q_ref = bf16[384,2048]{1,0:T(8,128)(2,1)} reshape(bf16[64,8,1536]{2,1,0:T(8,128)(2,1)S(1)} %slice.18) | data formatting | bytes 3145728 | tf_op jit(solution)/shard_map/reshape | solution.py:94
  69.1 1.0 fusion.12
  70.1 0.8 reshape.67.seen_ref
  70.9 39.0 %shard_map.64 = bf16[384,2048]{1,0:T(8,128)(2,1)} custom-call(f32[384,1]{1,0:T(8,128)} %reshape.67.seen_ref, bf16[384,2048]{1,0:T(8,128)(2,1)} %reshape.60.q_ref, bf16[2,128,3328]{2,1,0:T(8,128)(2,1)} %bitcast.27, bf16[3328,256]{1,0:T(8,128)(2,1)} %pad.13.v_ref), custom_call_target="tpu_custom_call" | custom-call | flops 10468982784 | bytes 6553600 | tf_op jit(solution)/shard_map/pallas_call | solution.py:55
  109.9 3.9 %reshape.62 = bf16[64,8,1536]{2,1,0:T(8,128)(2,1)} reshape(bf16[384,2048]{1,0:T(8,128)(2,1)} %shard_map.64) | data formatting | bytes 3145728 | tf_op jit(solution)/shard_map/reshape | solution.py:97
  113.7 6.2 %all-to-all-start.1 = ((bf16[64,8,1536]{2,1,0:T(8,128)(2,1)}), bf16[64,8,1536]{2,1,0:T(8,128)(2,1)S(1)}, u32[]{:S(2)}, u32[]{:S(2)}) async-start(bf16[64,8,1536]{2,1,0:T(8,128)(2,1)} %reshape.62), calls=%async_computation.1 | async-start | bytes 3145728 | tf_op jit(solution)/shard_map/all_to_all | solution.py:97
  120.0 39.8 %all-to-all-done.1 = bf16[64,8,1536]{2,1,0:T(8,128)(2,1)S(1)} async-done(((bf16[64,8,1536]{2,1,0:T(8,128)(2,1)}), bf16[64,8,1536]{2,1,0:T(8,128)(2,1)S(1)}, u32[]{:S(2)}, u32[]{:S(2)}) %all-to-all-start.1) | async-done | bytes 1572896 | tf_op jit(solution)/shard_map/all_to_all | solution.py:97
  159.8 2.2 %reshape.63 = bf16[384,2048]{1,0:T(8,128)(2,1)} reshape(bf16[64,8,1536]{2,1,0:T(8,128)(2,1)S(1)} %all-to-all-done.1) | data formatting | bytes 3145728 | tf_op jit(solution)/shard_map/reshape | solution.py:98
  161.9 2.2 %fusion.1 = (f32[256]{0:T(256)S(1)}, bf16[256,2048]{1,0:T(8,128)(2,1)S(1)}) fusion(bf16[384,2048]{1,0:T(8,128)(2,1)} %reshape.63, s32[256]{0:T(256)S(1)} %multiply_add_fusion), kind=kOutput, calls=%fused_computation.6 | convolution fusion | flops 404848384 | bytes 2623488 | tf_op jit(solution)/shard_map/sr,sc->rc/dot_general | solution.py:99
  164.2 8.5 %psum.7 = f32[256]{0:T(256)S(1)} all-reduce(f32[256]{0:T(256)S(1)} %get-tuple-element.5), channel_id=1, replica_groups=mesh['docs'=64,'mp'=4] {'mp'}, use_global_device_ids=true, to_apply=%region_4.5 | all-reduce | flops 256 | bytes 2048 | tf_op jit(solution)/shard_map/psum | solution.py:102
  172.7 1.3 fusion.3
  (17 shorter events, 1.2 us)
Async XLA Ops:
  0.0 3.1 %copy-start = (bf16[256,2048]{1,0:T(8,128)(2,1)S(1)}, bf16[256,2048]{1,0:T(8,128)(2,1)}, u32[]{:S(2)}) copy-start(bf16[256,2048]{1,0:T(8,128)(2,1)} %param.6) | copy-start | bytes 3145732
  4.8 2.9 %copy-start.3 = (s32[256]{0:T(256)S(1)}, s32[256]{0:T(256)}, u32[]{:S(2)}) copy-start(s32[256]{0:T(256)} %param.10) | copy-start | bytes 3076
  9.5 55.9 %all-to-all-start = ((bf16[64,8,1664]{2,1,0:T(8,128)(2,1)}), bf16[64,8,1664]{2,1,0:T(8,128)(2,1)}, u32[]{:S(2)}, u32[]{:S(2)}) async-start(bf16[64,8,1664]{2,1,0:T(8,128)(2,1)} %fusion.4), calls=%async_computation | async-start | bytes 3407872 | tf_op jit(solution)/shard_map/all_to_all | solution.py:93
  25.6 2.0 %copy-start.1 = (bf16[3202,256]{1,0:T(8,128)(2,1)S(1)}, bf16[3202,256]{1,0:T(8,128)(2,1)}, u32[]{:S(2)}) copy-start(bf16[3202,256]{1,0:T(8,128)(2,1)} %param.8) | copy-start | bytes 4918276
  113.7 6.2 %copy-start.2 = (bf16[2048]{0:T(1024)(128)(2,1)S(1)}, bf16[2048]{0:T(1024)(128)(2,1)}, u32[]{:S(2)}) copy-start(bf16[2048]{0:T(1024)(128)(2,1)} %param.11) | copy-start | bytes 12292
  113.7 46.0 %all-to-all-start.1 = ((bf16[64,8,1536]{2,1,0:T(8,128)(2,1)}), bf16[64,8,1536]{2,1,0:T(8,128)(2,1)S(1)}, u32[]{:S(2)}, u32[]{:S(2)}) async-start(bf16[64,8,1536]{2,1,0:T(8,128)(2,1)} %reshape.62), calls=%async_computation.1 | async-start | bytes 3145728 | tf_op jit(solution)/shard_map/all_to_all | solution.py:97

commit v7 on v6

--- a/solution.py
+++ b/solution.py
@@ -71,6 +71,56 @@
     )(seen, q, kp, vp)
 
 
+def power_kernel(x_ref, o_ref, slots, send_sem, recv_sem):
+    doc = lax.axis_index("docs")
+    col = lax.axis_index("mp")
+    n = slots.shape[0]
+    mesh_id = pl.DeviceIdType.MESH
+    barrier = pltpu.get_barrier_semaphore()
+    for d in range(1, n):
+        pl.semaphore_signal(barrier, inc=1, device_id=(doc, lax.rem(col + d, n)), device_id_type=mesh_id)
+    pl.semaphore_wait(barrier, n - 1)
+    slots[col] = x_ref[...]
+    copies = []
+    for d in range(1, n):
+        copy = pltpu.make_async_remote_copy(
+            src_ref=x_ref,
+            dst_ref=slots.at[col],
+            send_sem=send_sem.at[d - 1],
+            recv_sem=recv_sem.at[d - 1],
+            device_id=(doc, lax.rem(col + d, n)),
+            device_id_type=mesh_id,
+        )
+        copy.start()
+        copies.append(copy)
+    for d in range(1, n):
+        copies[d - 1].wait_send()
+        pltpu.make_async_copy(
+            x_ref, slots.at[lax.rem(col + n - d, n)], recv_sem.at[d - 1]
+        ).wait()
+    total = slots[0]
+    for i in range(1, n):
+        total = total + slots[i]
+    o_ref[...] = total
+
+
+def power_sum(part):
+    n = lax.axis_size("mp")
+    row = part.reshape(1, -1)
+    return pl.pallas_call(
+        power_kernel,
+        in_specs=[pl.BlockSpec(memory_space=pltpu.VMEM)],
+        out_specs=pl.BlockSpec(memory_space=pltpu.VMEM),
+        out_shape=jax.ShapeDtypeStruct(row.shape, row.dtype),
+        scratch_shapes=[
+            pltpu.VMEM((n,) + row.shape, row.dtype),
+            pltpu.SemaphoreType.DMA((n - 1,)),
+            pltpu.SemaphoreType.DMA((n - 1,)),
+        ],
+        compiler_params=pltpu.CompilerParams(collective_id=0, has_side_effects=True),
+    )(row).reshape(part.shape)
+
+
 def shards(queries, keys, values, owner_of_row, visible, gain):
     docs = lax.axis_size("docs")
     rows = queries.shape[0]
@@ -99,7 +149,7 @@
     mine = jnp.einsum("sr,sc->rc", place, flat_back, preferred_element_type=jnp.float32).astype(
         jnp.bfloat16
     )
-    power = lax.psum(squares(mine), "mp")
+    power = power_sum(squares(mine))
     return rescale(mine, power, gain)
 
 

time: 175 us -> 173 us (0.989)
  blocking collectives: 8.47 us -> 0 us
  Pallas kernels: 39 us -> 44.9 us
    psum x1 -> x0, blocking collectives: 8.47 us -> none  [shards(): power = lax.psum(squares(mine), 'mp')]
    pallas_call x0 -> x1, Pallas kernels: none -> 5.95 us  [power_sum(): pl.pallas_call(power_kernel, in_specs=[pl.BlockSpec(memory_space=pltpu.VM...]
where the time goes in v7:
time: 173 us
  waiting for transfers between devices  76.2 us (44%)
  Pallas kernels  44.9 us (26%)
  local copies, waits for them, and re-layouts  19.9 us (12%)
  starting transfers between devices  19.6 us (11%)
  other arithmetic  7.25 us (4%)
  matrix products  4.75 us (3%)
    all_to_all x1, waiting for transfers between devices, shards(): lax.all_to_all(context.reshape(docs, 8, lanes), 'docs', split_axis=0, con...  39.8 us
    pallas_call x1, Pallas kernels, attend(): pl.pallas_call(attend_kernel, grid=(kv_local, rows // tm), in_specs=[pl.B...  39 us
    all_to_all x1, waiting for transfers between devices, shards(): lax.all_to_all(sent, 'docs', split_axis=0, concat_axis=0, tiled=True)  36.5 us
    all_to_all x1, starting transfers between devices, shards(): lax.all_to_all(sent, 'docs', split_axis=0, concat_axis=0, tiled=True)  13.3 us
    all_to_all x1, starting transfers between devices, shards(): lax.all_to_all(context.reshape(docs, 8, lanes), 'docs', split_axis=0, con...  6.23 us
    pallas_call x1, Pallas kernels, power_sum(): pl.pallas_call(power_kernel, in_specs=[pl.BlockSpec(memory_space=pltpu.VM...  5.95 us
    reshape x1, local copies, waits for them, and re-layouts, shards(): context.reshape(docs, 8, lanes)  3.87 us
    unnamed x9, local copies, waits for them, and re-layouts  3.46 us
  transfers between devices with their start and end apart: 2, of which 2 were waited for; matrix products, arithmetic and copies ran while one was open for 3% of the time, Pallas kernels for 0%

profile of v7, /device:TPU:1, one launch (start us, length us, event | category | flops | bytes accessed | tf_op | source)
XLA Modules:
  0.0 172.7 jit_solution(17503782837583249414)
XLA Ops:
  0.0 0.8 fusion.11
  1.6 0.8 fusion.10
  3.1 1.7 %convolution_convert_fusion = bf16[384,2048]{1,0:T(8,128)(2,1)} fusion(bf16[256,2048]{1,0:T(8,128)(2,1)S(1)} %copy-done, s32[256]{0:T(256)S(1)} %multiply_add_fusion), kind=kOutput, calls=%fused_computation.2 | convolution fusion | flops 403537920 | bytes 2622464 | tf_op jit(solution)/shard_map/dot_general | solution.py:137
  4.8 2.9 %reshape.73 = bf16[64,8,1536]{2,1,0:T(8,128)(2,1)S(1)} reshape(bf16[384,2048]{1,0:T(8,128)(2,1)} %convolution_convert_fusion) | data formatting | bytes 3145728 | tf_op jit(solution)/shard_map/reshape | solution.py:140
  8.1 1.4 fusion.4
  9.5 13.3 %all-to-all-start = ((bf16[64,8,1664]{2,1,0:T(8,128)(2,1)}), bf16[64,8,1664]{2,1,0:T(8,128)(2,1)}, u32[]{:S(2)}, u32[]{:S(2)}) async-start(bf16[64,8,1664]{2,1,0:T(8,128)(2,1)} %fusion.4), calls=%async_computation | async-start | bytes 3407872 | tf_op jit(solution)/shard_map/all_to_all | solution.py:143
  22.9 2.7 %copy.18 = bf16[3202,256]{0,1:T(8,128)(2,1)S(1)} copy(bf16[3202,256]{1,0:T(8,128)(2,1)} %param.7) | data formatting | bytes 3278848
  25.6 1.3 pad.12.clone
  26.9 0.7 copy-done.1
  27.6 1.3 pad.13.v_ref
  28.9 36.5 %all-to-all-done = bf16[64,8,1664]{2,1,0:T(8,128)(2,1)} async-done(((bf16[64,8,1664]{2,1,0:T(8,128)(2,1)}), bf16[64,8,1664]{2,1,0:T(8,128)(2,1)}, u32[]{:S(2)}, u32[]{:S(2)}) %all-to-all-start) | async-done | bytes 1703968 | tf_op jit(solution)/shard_map/all_to_all | solution.py:143
  65.4 1.5 slice.18
  66.9 2.2 %reshape.75.q_ref = bf16[384,2048]{1,0:T(8,128)(2,1)} reshape(bf16[64,8,1536]{2,1,0:T(8,128)(2,1)S(1)} %slice.18) | data formatting | bytes 3145728 | tf_op jit(solution)/shard_map/reshape | solution.py:144
  69.1 1.0 fusion.12
  70.1 0.8 reshape.83.seen_ref
  70.9 39.0 %shard_map.64 = bf16[384,2048]{1,0:T(8,128)(2,1)} custom-call(f32[384,1]{1,0:T(8,128)} %reshape.83.seen_ref, bf16[384,2048]{1,0:T(8,128)(2,1)} %reshape.75.q_ref, bf16[2,128,3328]{2,1,0:T(8,128)(2,1)} %bitcast.29, bf16[3328,256]{1,0:T(8,128)(2,1)} %pad.13.v_ref), custom_call_target="tpu_custom_call" | custom-call | flops 10468982784 | bytes 6553600 | tf_op jit(solution)/shard_map/pallas_call | solution.py:55
  109.9 3.9 %reshape.77 = bf16[64,8,1536]{2,1,0:T(8,128)(2,1)} reshape(bf16[384,2048]{1,0:T(8,128)(2,1)} %shard_map.64) | data formatting | bytes 3145728 | tf_op jit(solution)/shard_map/reshape | solution.py:147
  113.7 6.2 %all-to-all-start.1 = ((bf16[64,8,1536]{2,1,0:T(8,128)(2,1)}), bf16[64,8,1536]{2,1,0:T(8,128)(2,1)S(1)}, u32[]{:S(2)}, u32[]{:S(2)}) async-start(bf16[64,8,1536]{2,1,0:T(8,128)(2,1)} %reshape.77), calls=%async_computation.1 | async-start | bytes 3145728 | tf_op jit(solution)/shard_map/all_to_all | solution.py:147
  120.0 39.8 %all-to-all-done.1 = bf16[64,8,1536]{2,1,0:T(8,128)(2,1)S(1)} async-done(((bf16[64,8,1536]{2,1,0:T(8,128)(2,1)}), bf16[64,8,1536]{2,1,0:T(8,128)(2,1)S(1)}, u32[]{:S(2)}, u32[]{:S(2)}) %all-to-all-start.1) | async-done | bytes 1572896 | tf_op jit(solution)/shard_map/all_to_all | solution.py:147
  159.8 2.2 %reshape.78 = bf16[384,2048]{1,0:T(8,128)(2,1)} reshape(bf16[64,8,1536]{2,1,0:T(8,128)(2,1)S(1)} %all-to-all-done.1) | data formatting | bytes 3145728 | tf_op jit(solution)/shard_map/reshape | solution.py:148
  161.9 2.8 %fusion.1 = (f32[256]{0:T(256)}, bf16[256,2048]{1,0:T(8,128)(2,1)S(1)}) fusion(bf16[384,2048]{1,0:T(8,128)(2,1)} %reshape.78, s32[256]{0:T(256)S(1)} %multiply_add_fusion), kind=kOutput, calls=%fused_computation.6 | convolution fusion | flops 404848384 | bytes 2623488 | tf_op jit(solution)/shard_map/sr,sc->rc/dot_general | solution.py:149
  164.8 6.0 %shard_map.65 = f32[1,256]{1,0:T(1,128)} custom-call(f32[1,256]{1,0:T(1,128)} %bitcast.34), custom_call_target="tpu_custom_call" | custom-call | tf_op jit(solution)/shard_map/pallas_call | solution.py:110
  170.7 0.7 add_rsqrt_fusion
  171.4 1.3 fusion.3
  (17 shorter events, 1.9 us)
Async XLA Ops:
  0.0 3.1 %copy-start = (bf16[256,2048]{1,0:T(8,128)(2,1)S(1)}, bf16[256,2048]{1,0:T(8,128)(2,1)}, u32[]{:S(2)}) copy-start(bf16[256,2048]{1,0:T(8,128)(2,1)} %param.6) | copy-start | bytes 3145732
  4.8 2.9 %copy-start.3 = (s32[256]{0:T(256)S(1)}, s32[256]{0:T(256)}, u32[]{:S(2)}) copy-start(s32[256]{0:T(256)} %param.10) | copy-start | bytes 3076
  9.5 55.9 %all-to-all-start = ((bf16[64,8,1664]{2,1,0:T(8,128)(2,1)}), bf16[64,8,1664]{2,1,0:T(8,128)(2,1)}, u32[]{:S(2)}, u32[]{:S(2)}) async-start(bf16[64,8,1664]{2,1,0:T(8,128)(2,1)} %fusion.4), calls=%async_computation | async-start | bytes 3407872 | tf_op jit(solution)/shard_map/all_to_all | solution.py:143
  25.6 2.0 %copy-start.1 = (bf16[3202,256]{1,0:T(8,128)(2,1)S(1)}, bf16[3202,256]{1,0:T(8,128)(2,1)}, u32[]{:S(2)}) copy-start(bf16[3202,256]{1,0:T(8,128)(2,1)} %param.8) | copy-start | bytes 4918276
  113.7 6.2 %copy-start.2 = (bf16[2048]{0:T(1024)(128)(2,1)S(1)}, bf16[2048]{0:T(1024)(128)(2,1)}, u32[]{:S(2)}) copy-start(bf16[2048]{0:T(1024)(128)(2,1)} %param.11) | copy-start | bytes 12292
  113.7 46.0 %all-to-all-start.1 = ((bf16[64,8,1536]{2,1,0:T(8,128)(2,1)}), bf16[64,8,1536]{2,1,0:T(8,128)(2,1)S(1)}, u32[]{:S(2)}, u32[]{:S(2)}) async-start(bf16[64,8,1536]{2,1,0:T(8,128)(2,1)} %reshape.77), calls=%async_computation.1 | async-start | bytes 3145728 | tf_op jit(solution)/shard_map/all_to_all | solution.py:147

commit v8 on v7

--- a/solution.py
+++ b/solution.py
@@ -30,17 +30,17 @@
     scale = 1.0 / HD**0.5
     limit = seen_ref[...] * IMG_TOK
     allowed = lax.broadcasted_iota(jnp.int32, (tm, tp), 1).astype(jnp.float32) < limit
+    bias = jnp.where(allowed, jnp.float32(0), jnp.float32(-1e30))
     keys = k_ref[...]
     vals = v_ref[...]
     for g in range(GROUP):
         q = q_ref[:, g * HD : (g + 1) * HD]
-        s = jnp.dot(q, keys, preferred_element_type=jnp.float32) * scale
-        s = jnp.where(allowed, s, jnp.float32(-1e30))
+        s = jnp.dot(q, keys, preferred_element_type=jnp.float32) * scale + bias
         top = jnp.max(s, axis=1, keepdims=True)
         w = jnp.exp(s - top)
-        total = jnp.sum(w, axis=1, keepdims=True)
-        ctx = jnp.dot(w.astype(jnp.bfloat16), vals, preferred_element_type=jnp.float32)
-        o_ref[:, g * HD : (g + 1) * HD] = (ctx / total).astype(o_ref.dtype)
+        both = jnp.dot(w.astype(jnp.bfloat16), vals, preferred_element_type=jnp.float32)
+        ctx = both[:, :HD] / both[:, HD : HD + 1]
+        o_ref[:, g * HD : (g + 1) * HD] = ctx.astype(o_ref.dtype)
 
 
 def attend(q, seen, keys, values):
@@ -51,6 +51,9 @@
     kp = jnp.pad(keys, ((0, padded - tokens), (0, 0)))
     kp = kp.reshape(padded, kv_local, HD).transpose(1, 2, 0)
     vp = jnp.pad(values, ((0, padded - tokens), (0, 0)))
+    vp = vp.reshape(padded, kv_local, HD).transpose(1, 0, 2)
+    ones = jnp.zeros((kv_local, padded, HD), vp.dtype).at[:, :, 0].set(1)
+    vp = jnp.concatenate([vp, ones], axis=2)
     tm = math.gcd(rows, 384)
     return pl.pallas_call(
         attend_kernel,
@@ -59,7 +62,7 @@
             pl.BlockSpec((tm, 1), lambda k, i: (i, 0)),
             pl.BlockSpec((tm, GROUP * HD), lambda k, i: (i, k)),
             pl.BlockSpec((None, HD, padded), lambda k, i: (k, 0, 0)),
-            pl.BlockSpec((padded, HD), lambda k, i: (0, k)),
+            pl.BlockSpec((None, padded, 2 * HD), lambda k, i: (k, 0, 0)),
         ],
         out_specs=pl.BlockSpec((tm, GROUP * HD), lambda k, i: (i, k)),
         out_shape=jax.ShapeDtypeStruct((rows, width), jnp.bfloat16),

time: 173 us -> 168 us (0.971)
  waiting for transfers between devices: 76.2 us -> 67.1 us
  local copies, waits for them, and re-layouts: 19.9 us -> 26.9 us
  Pallas kernels: 44.9 us -> 39.7 us
  other arithmetic: 7.25 us -> 9.34 us
    all_to_all x1, waiting for transfers between devices: 36.5 us -> 27.3 us  [shards(): lax.all_to_all(sent, 'docs', split_axis=0, concat_axis=0, tiled=True)]
    pallas_call x1, Pallas kernels: 39 us -> 33.8 us  [attend(): pl.pallas_call(attend_kernel, grid=(kv_local, rows // tm), in_specs=[pl.B...]
    reshape x0 -> x1, local copies, waits for them, and re-layouts: none -> 3.77 us  [attend(): vp = vp.reshape(padded, kv_local, HD).transpose(1, 0, 2)]
    unnamed x9 -> x12, local copies, waits for them, and re-layouts: 3.46 us -> 6.68 us
    concatenate x0 -> x1, other arithmetic: none -> 2.09 us  [attend(): vp = jnp.concatenate([vp, ones], axis=2)]
  transfers between devices with their start and end apart: 2 -> 2, of which waited for: 2 -> 2; matrix products, arithmetic and copies ran while one was open for 3% -> 8% of each run, Pallas kernels for 0% -> 0%
where the time goes in v8:
time: 168 us; the launch traced here: 167 us
  waiting for transfers between devices  67.1 us (40%)
  Pallas kernels  39.7 us (24%)
  local copies, waits for them, and re-layouts  26.9 us (16%)
  starting transfers between devices  19.6 us (12%)
  other arithmetic  9.34 us (6%)
  matrix products  4.75 us (3%)
    all_to_all x1, waiting for transfers between devices, shards(): lax.all_to_all(context.reshape(docs, 8, lanes), 'docs', split_axis=0, con...  39.8 us
    pallas_call x1, Pallas kernels, attend(): pl.pallas_call(attend_kernel, grid=(kv_local, rows // tm), in_specs=[pl.B...  33.8 us
    all_to_all x1, waiting for transfers between devices, shards(): lax.all_to_all(sent, 'docs', split_axis=0, concat_axis=0, tiled=True)  27.3 us
    all_to_all x1, starting transfers between devices, shards(): lax.all_to_all(sent, 'docs', split_axis=0, concat_axis=0, tiled=True)  13.3 us
    unnamed x12, local copies, waits for them, and re-layouts  6.68 us
    all_to_all x1, starting transfers between devices, shards(): lax.all_to_all(context.reshape(docs, 8, lanes), 'docs', split_axis=0, con...  6.23 us
    pallas_call x1, Pallas kernels, power_sum(): pl.pallas_call(power_kernel, in_specs=[pl.BlockSpec(memory_space=pltpu.VM...  5.96 us
    reshape x1, local copies, waits for them, and re-layouts, shards(): context.reshape(docs, 8, lanes)  3.87 us
  transfers between devices with their start and end apart: 2, of which 2 were waited for; matrix products, arithmetic and copies ran while one was open for 8% of the time, Pallas kernels for 0%

profile of v8, /device:TPU:1, one launch (start us, length us, event | category | flops | bytes accessed | tf_op | source)
XLA Modules:
  0.0 167.5 jit_solution(10816293367168510387)
XLA Ops:
  1.6 0.8 fusion.10
  3.1 1.7 %convolution_convert_fusion = bf16[384,2048]{1,0:T(8,128)(2,1)} fusion(bf16[256,2048]{1,0:T(8,128)(2,1)S(1)} %copy-done, s32[256]{0:T(256)S(1)} %multiply_add_fusion), kind=kOutput, calls=%fused_computation.3 | convolution fusion | flops 403537920 | bytes 2622464 | tf_op jit(solution)/shard_map/dot_general | solution.py:140
  4.8 2.9 %reshape.104 = bf16[64,8,1536]{2,1,0:T(8,128)(2,1)S(1)} reshape(bf16[384,2048]{1,0:T(8,128)(2,1)} %convolution_convert_fusion) | data formatting | bytes 3145728 | tf_op jit(solution)/shard_map/reshape | solution.py:143
  8.1 1.4 fusion.4
  9.5 13.3 %all-to-all-start = ((bf16[64,8,1664]{2,1,0:T(8,128)(2,1)}), bf16[64,8,1664]{2,1,0:T(8,128)(2,1)}, u32[]{:S(2)}, u32[]{:S(2)}) async-start(bf16[64,8,1664]{2,1,0:T(8,128)(2,1)} %fusion.4), calls=%async_computation | async-start | bytes 3407872 | tf_op jit(solution)/shard_map/all_to_all | solution.py:146
  22.9 2.7 %copy.18 = bf16[3202,256]{0,1:T(8,128)(2,1)S(1)} copy(bf16[3202,256]{1,0:T(8,128)(2,1)} %param.10) | data formatting | bytes 3278848 | tf_op args[2]
  25.6 1.3 pad.15
  26.9 3.8 %copy.19 = bf16[3328,2,128]{2,0,1:T(8,128)(2,1)} copy(bf16[3328,2,128]{0,2,1:T(8,128)(2,1)} %bitcast.31) | data formatting | bytes 3407872 | tf_op jit(solution)/shard_map/reshape | solution.py:54
  30.7 2.7 %copy.22 = bf16[3202,256]{0,1:T(8,128)(2,1)S(1)} copy(bf16[3202,256]{1,0:T(8,128)(2,1)} %param.9) | data formatting | bytes 3278848
  33.4 1.3 pad.14.clone
  36.0 2.1 %pad_maximum_fusion.v_ref = bf16[2,3328,256]{2,1,0:T(8,128)(2,1)} fusion(bf16[2,3328,128]{2,1,0:T(8,128)(2,1)S(1)} %copy-done.2, bf16[2,3328,128]{2,1,0:T(8,128)(2,1)S(1)} %bitcast.32), kind=kLoop, calls=%fused_computation.1 | loop fusion | flops 6815744 | bytes 6815744 | tf_op jit(solution)/shard_map/concatenate | solution.py:56
  38.1 27.3 %all-to-all-done = bf16[64,8,1664]{2,1,0:T(8,128)(2,1)} async-done(((bf16[64,8,1664]{2,1,0:T(8,128)(2,1)}), bf16[64,8,1664]{2,1,0:T(8,128)(2,1)}, u32[]{:S(2)}, u32[]{:S(2)}) %all-to-all-start) | async-done | bytes 1703968 | tf_op jit(solution)/shard_map/all_to_all | solution.py:146
  65.4 1.5 slice.37
  66.9 2.2 %reshape.106.q_ref = bf16[384,2048]{1,0:T(8,128)(2,1)} reshape(bf16[64,8,1536]{2,1,0:T(8,128)(2,1)S(1)} %slice.37) | data formatting | bytes 3145728 | tf_op jit(solution)/shard_map/reshape | solution.py:147
  69.1 1.0 fusion.12
  70.1 0.8 reshape.115.seen_ref
  70.9 33.8 %shard_map.64 = bf16[384,2048]{1,0:T(8,128)(2,1)} custom-call(f32[384,1]{1,0:T(8,128)} %reshape.115.seen_ref, bf16[384,2048]{1,0:T(8,128)(2,1)} %reshape.106.q_ref, bf16[2,128,3328]{2,1,0:T(8,128)(2,1)} %bitcast.33, bf16[2,3328,256]{2,1,0:T(8,128)(2,1)} %pad_maximum_fusion.v_ref), custom_call_target="tpu_custom_call" | custom-call | flops 10468982784 | bytes 6553600 | tf_op jit(solution)/shard_map/pallas_call | solution.py:58
  104.7 3.9 %reshape.109 = bf16[64,8,1536]{2,1,0:T(8,128)(2,1)} reshape(bf16[384,2048]{1,0:T(8,128)(2,1)} %shard_map.64) | data formatting | bytes 3145728 | tf_op jit(solution)/shard_map/reshape | solution.py:150
  108.5 6.2 %all-to-all-start.1 = ((bf16[64,8,1536]{2,1,0:T(8,128)(2,1)}), bf16[64,8,1536]{2,1,0:T(8,128)(2,1)S(1)}, u32[]{:S(2)}, u32[]{:S(2)}) async-start(bf16[64,8,1536]{2,1,0:T(8,128)(2,1)} %reshape.109), calls=%async_computation.1 | async-start | bytes 3145728 | tf_op jit(solution)/shard_map/all_to_all | solution.py:150
  114.8 39.8 %all-to-all-done.1 = bf16[64,8,1536]{2,1,0:T(8,128)(2,1)S(1)} async-done(((bf16[64,8,1536]{2,1,0:T(8,128)(2,1)}), bf16[64,8,1536]{2,1,0:T(8,128)(2,1)S(1)}, u32[]{:S(2)}, u32[]{:S(2)}) %all-to-all-start.1) | async-done | bytes 1572896 | tf_op jit(solution)/shard_map/all_to_all | solution.py:150
  154.6 2.2 %reshape.110 = bf16[384,2048]{1,0:T(8,128)(2,1)} reshape(bf16[64,8,1536]{2,1,0:T(8,128)(2,1)S(1)} %all-to-all-done.1) | data formatting | bytes 3145728 | tf_op jit(solution)/shard_map/reshape | solution.py:151
  156.7 2.8 %fusion.1 = (f32[256]{0:T(256)}, bf16[256,2048]{1,0:T(8,128)(2,1)S(1)}) fusion(bf16[384,2048]{1,0:T(8,128)(2,1)} %reshape.110, s32[256]{0:T(256)S(1)} %multiply_add_fusion), kind=kOutput, calls=%fused_computation.7 | convolution fusion | flops 404848384 | bytes 2623488 | tf_op jit(solution)/shard_map/sr,sc->rc/dot_general | solution.py:152
  159.6 6.0 %shard_map.65 = f32[1,256]{1,0:T(1,128)} custom-call(f32[1,256]{1,0:T(1,128)} %bitcast.38), custom_call_target="tpu_custom_call" | custom-call | tf_op jit(solution)/shard_map/pallas_call | solution.py:113
  166.2 1.3 fusion.3
  (22 shorter events, 4.6 us)
Async XLA Ops:
  0.0 3.1 %copy-start = (bf16[256,2048]{1,0:T(8,128)(2,1)S(1)}, bf16[256,2048]{1,0:T(8,128)(2,1)}, u32[]{:S(2)}) copy-start(bf16[256,2048]{1,0:T(8,128)(2,1)} %param.8) | copy-start | bytes 3145732
  4.8 2.9 %copy-start.4 = (s32[256]{0:T(256)S(1)}, s32[256]{0:T(256)}, u32[]{:S(2)}) copy-start(s32[256]{0:T(256)} %param.12) | copy-start | bytes 3076
  9.5 55.9 %all-to-all-start = ((bf16[64,8,1664]{2,1,0:T(8,128)(2,1)}), bf16[64,8,1664]{2,1,0:T(8,128)(2,1)}, u32[]{:S(2)}, u32[]{:S(2)}) async-start(bf16[64,8,1664]{2,1,0:T(8,128)(2,1)} %fusion.4), calls=%async_computation | async-start | bytes 3407872 | tf_op jit(solution)/shard_map/all_to_all | solution.py:146
  33.4 2.1 %copy-start.1 = (bf16[3328,2,128]{2,0,1:T(8,128)(2,1)S(1)}, bf16[3328,2,128]{2,0,1:T(8,128)(2,1)}, u32[]{:S(2)}) copy-start(bf16[3328,2,128]{2,0,1:T(8,128)(2,1)} %copy.19) | copy-start | bytes 5111812
  33.4 2.6 %copy-start.2 = (bf16[2,3328,128]{2,1,0:T(8,128)(2,1)S(1)}, bf16[2,3328,128]{2,1,0:T(8,128)(2,1)}, u32[]{:S(2)}) copy-start(bf16[2,3328,128]{2,1,0:T(8,128)(2,1)} %constant.43.clone.1) | copy-start | bytes 5111812
  108.5 6.2 %copy-start.3 = (bf16[2048]{0:T(1024)(128)(2,1)S(1)}, bf16[2048]{0:T(1024)(128)(2,1)}, u32[]{:S(2)}) copy-start(bf16[2048]{0:T(1024)(128)(2,1)} %param.13) | copy-start | bytes 12292
  108.5 46.0 %all-to-all-start.1 = ((bf16[64,8,1536]{2,1,0:T(8,128)(2,1)}), bf16[64,8,1536]{2,1,0:T(8,128)(2,1)S(1)}, u32[]{:S(2)}, u32[]{:S(2)}) async-start(bf16[64,8,1536]{2,1,0:T(8,128)(2,1)} %reshape.109), calls=%async_computation.1 | async-start | bytes 3145728 | tf_op jit(solution)/shard_map/all_to_all | solution.py:150

commit v9 on v8

--- a/solution.py
+++ b/solution.py
@@ -33,14 +33,17 @@
     bias = jnp.where(allowed, jnp.float32(0), jnp.float32(-1e30))
     keys = k_ref[...]
     vals = v_ref[...]
-    for g in range(GROUP):
-        q = q_ref[:, g * HD : (g + 1) * HD]
-        s = jnp.dot(q, keys, preferred_element_type=jnp.float32) * scale + bias
-        top = jnp.max(s, axis=1, keepdims=True)
-        w = jnp.exp(s - top)
-        both = jnp.dot(w.astype(jnp.bfloat16), vals, preferred_element_type=jnp.float32)
-        ctx = both[:, :HD] / both[:, HD : HD + 1]
-        o_ref[:, g * HD : (g + 1) * HD] = ctx.astype(o_ref.dtype)
+    for pair in range(0, GROUP, 4):
+        scores = []
+        for g in range(pair, pair + 4):
+            q = q_ref[:, g * HD : (g + 1) * HD]
+            scores.append(jnp.dot(q, keys, preferred_element_type=jnp.float32) * scale + bias)
+        for g, s in zip(range(pair, pair + 4), scores):
+            top = jnp.max(s, axis=1, keepdims=True)
+            w = jnp.exp(s - top)
+            both = jnp.dot(w.astype(jnp.bfloat16), vals, preferred_element_type=jnp.float32)
+            ctx = both[:, :HD] / both[:, HD : HD + 1]
+            o_ref[:, g * HD : (g + 1) * HD] = ctx.astype(o_ref.dtype)
 
 
 def attend(q, seen, keys, values):

time: 168 us -> 166 us (0.988)
  Pallas kernels: 39.7 us -> 37.9 us
    pallas_call x1, Pallas kernels: 33.8 us -> 31.9 us  [attend(): pl.pallas_call(attend_kernel, grid=(kv_local, rows // tm), in_specs=[pl.B...]
where the time goes in v9:
time: 166 us
  waiting for transfers between devices  67.1 us (40%)
  Pallas kernels  37.9 us (23%)
  local copies, waits for them, and re-layouts  26.9 us (16%)
  starting transfers between devices  19.6 us (12%)
  other arithmetic  9.34 us (6%)
  matrix products  4.75 us (3%)
    all_to_all x1, waiting for transfers between devices, shards(): lax.all_to_all(context.reshape(docs, 8, lanes), 'docs', split_axis=0, con...  39.8 us
    pallas_call x1, Pallas kernels, attend(): pl.pallas_call(attend_kernel, grid=(kv_local, rows // tm), in_specs=[pl.B...  31.9 us
    all_to_all x1, waiting for transfers between devices, shards(): lax.all_to_all(sent, 'docs', split_axis=0, concat_axis=0, tiled=True)  27.3 us
    all_to_all x1, starting transfers between devices, shards(): lax.all_to_all(sent, 'docs', split_axis=0, concat_axis=0, tiled=True)  13.3 us
    unnamed x12, local copies, waits for them, and re-layouts  6.68 us
    all_to_all x1, starting transfers between devices, shards(): lax.all_to_all(context.reshape(docs, 8, lanes), 'docs', split_axis=0, con...  6.23 us
    pallas_call x1, Pallas kernels, power_sum(): pl.pallas_call(power_kernel, in_specs=[pl.BlockSpec(memory_space=pltpu.VM...  5.96 us
    reshape x1, local copies, waits for them, and re-layouts, shards(): context.reshape(docs, 8, lanes)  3.87 us
  transfers between devices with their start and end apart: 2, of which 2 were waited for; matrix products, arithmetic and copies ran while one was open for 8% of the time, Pallas kernels for 0%

profile of v9, /device:TPU:1, one launch (start us, length us, event | category | flops | bytes accessed | tf_op | source)
XLA Modules:
  0.0 165.7 jit_solution(5738912001992411079)
XLA Ops:
  1.6 0.8 fusion.10
  3.1 1.7 %convolution_convert_fusion = bf16[384,2048]{1,0:T(8,128)(2,1)} fusion(bf16[256,2048]{1,0:T(8,128)(2,1)S(1)} %copy-done, s32[256]{0:T(256)S(1)} %multiply_add_fusion), kind=kOutput, calls=%fused_computation.3 | convolution fusion | flops 403537920 | bytes 2622464 | tf_op jit(solution)/shard_map/dot_general | solution.py:143
  4.8 2.9 %reshape.104 = bf16[64,8,1536]{2,1,0:T(8,128)(2,1)S(1)} reshape(bf16[384,2048]{1,0:T(8,128)(2,1)} %convolution_convert_fusion) | data formatting | bytes 3145728 | tf_op jit(solution)/shard_map/reshape | solution.py:146
  8.1 1.4 fusion.4
  9.5 13.3 %all-to-all-start = ((bf16[64,8,1664]{2,1,0:T(8,128)(2,1)}), bf16[64,8,1664]{2,1,0:T(8,128)(2,1)}, u32[]{:S(2)}, u32[]{:S(2)}) async-start(bf16[64,8,1664]{2,1,0:T(8,128)(2,1)} %fusion.4), calls=%async_computation | async-start | bytes 3407872 | tf_op jit(solution)/shard_map/all_to_all | solution.py:149
  22.9 2.7 %copy.18 = bf16[3202,256]{0,1:T(8,128)(2,1)S(1)} copy(bf16[3202,256]{1,0:T(8,128)(2,1)} %param.10) | data formatting | bytes 3278848 | tf_op args[2]
  25.6 1.3 pad.15
  26.9 3.8 %copy.19 = bf16[3328,2,128]{2,0,1:T(8,128)(2,1)} copy(bf16[3328,2,128]{0,2,1:T(8,128)(2,1)} %bitcast.31) | data formatting | bytes 3407872 | tf_op jit(solution)/shard_map/reshape | solution.py:57
  30.7 2.7 %copy.22 = bf16[3202,256]{0,1:T(8,128)(2,1)S(1)} copy(bf16[3202,256]{1,0:T(8,128)(2,1)} %param.9) | data formatting | bytes 3278848
  33.4 1.3 pad.14.clone
  36.0 2.1 %pad_maximum_fusion.v_ref = bf16[2,3328,256]{2,1,0:T(8,128)(2,1)} fusion(bf16[2,3328,128]{2,1,0:T(8,128)(2,1)S(1)} %copy-done.2, bf16[2,3328,128]{2,1,0:T(8,128)(2,1)S(1)} %bitcast.32), kind=kLoop, calls=%fused_computation.1 | loop fusion | flops 6815744 | bytes 6815744 | tf_op jit(solution)/shard_map/concatenate | solution.py:59
  38.1 27.3 %all-to-all-done = bf16[64,8,1664]{2,1,0:T(8,128)(2,1)} async-done(((bf16[64,8,1664]{2,1,0:T(8,128)(2,1)}), bf16[64,8,1664]{2,1,0:T(8,128)(2,1)}, u32[]{:S(2)}, u32[]{:S(2)}) %all-to-all-start) | async-done | bytes 1703968 | tf_op jit(solution)/shard_map/all_to_all | solution.py:149
  65.4 1.5 slice.37
  66.9 2.2 %reshape.106.q_ref = bf16[384,2048]{1,0:T(8,128)(2,1)} reshape(bf16[64,8,1536]{2,1,0:T(8,128)(2,1)S(1)} %slice.37) | data formatting | bytes 3145728 | tf_op jit(solution)/shard_map/reshape | solution.py:150
  69.1 1.0 fusion.12
  70.1 0.8 reshape.115.seen_ref
  70.9 31.9 %shard_map.64 = bf16[384,2048]{1,0:T(8,128)(2,1)} custom-call(f32[384,1]{1,0:T(8,128)} %reshape.115.seen_ref, bf16[384,2048]{1,0:T(8,128)(2,1)} %reshape.106.q_ref, bf16[2,128,3328]{2,1,0:T(8,128)(2,1)} %bitcast.33, bf16[2,3328,256]{2,1,0:T(8,128)(2,1)} %pad_maximum_fusion.v_ref), custom_call_target="tpu_custom_call" | custom-call | flops 10468982784 | bytes 6553600 | tf_op jit(solution)/shard_map/pallas_call | solution.py:61
  102.8 3.9 %reshape.109 = bf16[64,8,1536]{2,1,0:T(8,128)(2,1)} reshape(bf16[384,2048]{1,0:T(8,128)(2,1)} %shard_map.64) | data formatting | bytes 3145728 | tf_op jit(solution)/shard_map/reshape | solution.py:153
  106.7 6.2 %all-to-all-start.1 = ((bf16[64,8,1536]{2,1,0:T(8,128)(2,1)}), bf16[64,8,1536]{2,1,0:T(8,128)(2,1)S(1)}, u32[]{:S(2)}, u32[]{:S(2)}) async-start(bf16[64,8,1536]{2,1,0:T(8,128)(2,1)} %reshape.109), calls=%async_computation.1 | async-start | bytes 3145728 | tf_op jit(solution)/shard_map/all_to_all | solution.py:153
  113.0 39.8 %all-to-all-done.1 = bf16[64,8,1536]{2,1,0:T(8,128)(2,1)S(1)} async-done(((bf16[64,8,1536]{2,1,0:T(8,128)(2,1)}), bf16[64,8,1536]{2,1,0:T(8,128)(2,1)S(1)}, u32[]{:S(2)}, u32[]{:S(2)}) %all-to-all-start.1) | async-done | bytes 1572896 | tf_op jit(solution)/shard_map/all_to_all | solution.py:153
  152.7 2.2 %reshape.110 = bf16[384,2048]{1,0:T(8,128)(2,1)} reshape(bf16[64,8,1536]{2,1,0:T(8,128)(2,1)S(1)} %all-to-all-done.1) | data formatting | bytes 3145728 | tf_op jit(solution)/shard_map/reshape | solution.py:154
  154.9 2.8 %fusion.1 = (f32[256]{0:T(256)}, bf16[256,2048]{1,0:T(8,128)(2,1)S(1)}) fusion(bf16[384,2048]{1,0:T(8,128)(2,1)} %reshape.110, s32[256]{0:T(256)S(1)} %multiply_add_fusion), kind=kOutput, calls=%fused_computation.7 | convolution fusion | flops 404848384 | bytes 2623488 | tf_op jit(solution)/shard_map/sr,sc->rc/dot_general | solution.py:155
  157.7 6.0 %shard_map.65 = f32[1,256]{1,0:T(1,128)} custom-call(f32[1,256]{1,0:T(1,128)} %bitcast.38), custom_call_target="tpu_custom_call" | custom-call | tf_op jit(solution)/shard_map/pallas_call | solution.py:116
  164.4 1.3 fusion.3
  (22 shorter events, 4.6 us)
Async XLA Ops:
  0.0 3.1 %copy-start = (bf16[256,2048]{1,0:T(8,128)(2,1)S(1)}, bf16[256,2048]{1,0:T(8,128)(2,1)}, u32[]{:S(2)}) copy-start(bf16[256,2048]{1,0:T(8,128)(2,1)} %param.8) | copy-start | bytes 3145732
  4.8 2.9 %copy-start.4 = (s32[256]{0:T(256)S(1)}, s32[256]{0:T(256)}, u32[]{:S(2)}) copy-start(s32[256]{0:T(256)} %param.12) | copy-start | bytes 3076
  9.5 55.9 %all-to-all-start = ((bf16[64,8,1664]{2,1,0:T(8,128)(2,1)}), bf16[64,8,1664]{2,1,0:T(8,128)(2,1)}, u32[]{:S(2)}, u32[]{:S(2)}) async-start(bf16[64,8,1664]{2,1,0:T(8,128)(2,1)} %fusion.4), calls=%async_computation | async-start | bytes 3407872 | tf_op jit(solution)/shard_map/all_to_all | solution.py:149
  33.4 2.1 %copy-start.1 = (bf16[3328,2,128]{2,0,1:T(8,128)(2,1)S(1)}, bf16[3328,2,128]{2,0,1:T(8,128)(2,1)}, u32[]{:S(2)}) copy-start(bf16[3328,2,128]{2,0,1:T(8,128)(2,1)} %copy.19) | copy-start | bytes 5111812
  33.4 2.6 %copy-start.2 = (bf16[2,3328,128]{2,1,0:T(8,128)(2,1)S(1)}, bf16[2,3328,128]{2,1,0:T(8,128)(2,1)}, u32[]{:S(2)}) copy-start(bf16[2,3328,128]{2,1,0:T(8,128)(2,1)} %constant.43.clone.1) | copy-start | bytes 5111812
  106.7 6.2 %copy-start.3 = (bf16[2048]{0:T(1024)(128)(2,1)S(1)}, bf16[2048]{0:T(1024)(128)(2,1)}, u32[]{:S(2)}) copy-start(bf16[2048]{0:T(1024)(128)(2,1)} %param.13) | copy-start | bytes 12292
  106.7 46.0 %all-to-all-start.1 = ((bf16[64,8,1536]{2,1,0:T(8,128)(2,1)}), bf16[64,8,1536]{2,1,0:T(8,128)(2,1)S(1)}, u32[]{:S(2)}, u32[]{:S(2)}) async-start(bf16[64,8,1536]{2,1,0:T(8,128)(2,1)} %reshape.109), calls=%async_computation.1 | async-start | bytes 3145728 | tf_op jit(solution)/shard_map/all_to_all | solution.py:153

commit v10 on v9

--- a/solution.py
+++ b/solution.py
@@ -33,17 +33,22 @@
     bias = jnp.where(allowed, jnp.float32(0), jnp.float32(-1e30))
     keys = k_ref[...]
     vals = v_ref[...]
-    for pair in range(0, GROUP, 4):
+    def batch(b, carry):
         scores = []
-        for g in range(pair, pair + 4):
-            q = q_ref[:, g * HD : (g + 1) * HD]
+        for j in range(4):
+            col = pl.multiple_of((b * 4 + j) * HD, HD)
+            q = q_ref[:, pl.ds(col, HD)]
             scores.append(jnp.dot(q, keys, preferred_element_type=jnp.float32) * scale + bias)
-        for g, s in zip(range(pair, pair + 4), scores):
+        for j, s in enumerate(scores):
+            col = pl.multiple_of((b * 4 + j) * HD, HD)
             top = jnp.max(s, axis=1, keepdims=True)
             w = jnp.exp(s - top)
             both = jnp.dot(w.astype(jnp.bfloat16), vals, preferred_element_type=jnp.float32)
             ctx = both[:, :HD] / both[:, HD : HD + 1]
-            o_ref[:, g * HD : (g + 1) * HD] = ctx.astype(o_ref.dtype)
+            o_ref[:, pl.ds(col, HD)] = ctx.astype(o_ref.dtype)
+        return carry
+
+    lax.fori_loop(0, GROUP // 4, batch, 0)
 
 
 def attend(q, seen, keys, values):

time: 166 us -> 167 us (level)
  no operation moved by 1% of the time
where the time goes in v10:
time: 167 us
  waiting for transfers between devices  67.1 us (40%)
  Pallas kernels  38.8 us (23%)
  local copies, waits for them, and re-layouts  26.9 us (16%)
  starting transfers between devices  19.6 us (12%)
  other arithmetic  9.34 us (6%)
  matrix products  4.75 us (3%)
    all_to_all x1, waiting for transfers between devices, shards(): lax.all_to_all(context.reshape(docs, 8, lanes), 'docs', split_axis=0, con...  39.8 us
    pallas_call x1, Pallas kernels, attend(): pl.pallas_call(attend_kernel, grid=(kv_local, rows // tm), in_specs=[pl.B...  32.8 us
    all_to_all x1, waiting for transfers between devices, shards(): lax.all_to_all(sent, 'docs', split_axis=0, concat_axis=0, tiled=True)  27.3 us
    all_to_all x1, starting transfers between devices, shards(): lax.all_to_all(sent, 'docs', split_axis=0, concat_axis=0, tiled=True)  13.3 us
    unnamed x12, local copies, waits for them, and re-layouts  6.68 us
    all_to_all x1, starting transfers between devices, shards(): lax.all_to_all(context.reshape(docs, 8, lanes), 'docs', split_axis=0, con...  6.23 us
    pallas_call x1, Pallas kernels, power_sum(): pl.pallas_call(power_kernel, in_specs=[pl.BlockSpec(memory_space=pltpu.VM...  5.95 us
    reshape x1, local copies, waits for them, and re-layouts, shards(): context.reshape(docs, 8, lanes)  3.87 us
  transfers between devices with their start and end apart: 2, of which 2 were waited for; matrix products, arithmetic and copies ran while one was open for 8% of the time, Pallas kernels for 0%

profile of v10, /device:TPU:1, one launch (start us, length us, event | category | flops | bytes accessed | tf_op | source)
XLA Modules:
  0.0 166.5 jit_solution(1166503203081642327)
XLA Ops:
  1.6 0.8 fusion.10
  3.1 1.7 %convolution_convert_fusion = bf16[384,2048]{1,0:T(8,128)(2,1)} fusion(bf16[256,2048]{1,0:T(8,128)(2,1)S(1)} %copy-done, s32[256]{0:T(256)S(1)} %multiply_add_fusion), kind=kOutput, calls=%fused_computation.3 | convolution fusion | flops 403537920 | bytes 2622464 | tf_op jit(solution)/shard_map/dot_general | solution.py:148
  4.8 2.9 %reshape.104 = bf16[64,8,1536]{2,1,0:T(8,128)(2,1)S(1)} reshape(bf16[384,2048]{1,0:T(8,128)(2,1)} %convolution_convert_fusion) | data formatting | bytes 3145728 | tf_op jit(solution)/shard_map/reshape | solution.py:151
  8.1 1.4 fusion.4
  9.5 13.3 %all-to-all-start = ((bf16[64,8,1664]{2,1,0:T(8,128)(2,1)}), bf16[64,8,1664]{2,1,0:T(8,128)(2,1)}, u32[]{:S(2)}, u32[]{:S(2)}) async-start(bf16[64,8,1664]{2,1,0:T(8,128)(2,1)} %fusion.4), calls=%async_computation | async-start | bytes 3407872 | tf_op jit(solution)/shard_map/all_to_all | solution.py:154
  22.9 2.7 %copy.18 = bf16[3202,256]{0,1:T(8,128)(2,1)S(1)} copy(bf16[3202,256]{1,0:T(8,128)(2,1)} %param.10) | data formatting | bytes 3278848 | tf_op args[2]
  25.6 1.3 pad.15
  26.9 3.8 %copy.19 = bf16[3328,2,128]{2,0,1:T(8,128)(2,1)} copy(bf16[3328,2,128]{0,2,1:T(8,128)(2,1)} %bitcast.31) | data formatting | bytes 3407872 | tf_op jit(solution)/shard_map/reshape | solution.py:62
  30.7 2.7 %copy.22 = bf16[3202,256]{0,1:T(8,128)(2,1)S(1)} copy(bf16[3202,256]{1,0:T(8,128)(2,1)} %param.9) | data formatting | bytes 3278848
  33.4 1.3 pad.14.clone
  36.0 2.1 %pad_maximum_fusion.v_ref = bf16[2,3328,256]{2,1,0:T(8,128)(2,1)} fusion(bf16[2,3328,128]{2,1,0:T(8,128)(2,1)S(1)} %copy-done.2, bf16[2,3328,128]{2,1,0:T(8,128)(2,1)S(1)} %bitcast.32), kind=kLoop, calls=%fused_computation.1 | loop fusion | flops 6815744 | bytes 6815744 | tf_op jit(solution)/shard_map/concatenate | solution.py:64
  38.1 27.3 %all-to-all-done = bf16[64,8,1664]{2,1,0:T(8,128)(2,1)} async-done(((bf16[64,8,1664]{2,1,0:T(8,128)(2,1)}), bf16[64,8,1664]{2,1,0:T(8,128)(2,1)}, u32[]{:S(2)}, u32[]{:S(2)}) %all-to-all-start) | async-done | bytes 1703968 | tf_op jit(solution)/shard_map/all_to_all | solution.py:154
  65.4 1.5 slice.37
  66.9 2.2 %reshape.106.q_ref = bf16[384,2048]{1,0:T(8,128)(2,1)} reshape(bf16[64,8,1536]{2,1,0:T(8,128)(2,1)S(1)} %slice.37) | data formatting | bytes 3145728 | tf_op jit(solution)/shard_map/reshape | solution.py:155
  69.1 1.0 fusion.12
  70.1 0.8 reshape.115.seen_ref
  70.9 32.8 %shard_map.64 = bf16[384,2048]{1,0:T(8,128)(2,1)} custom-call(f32[384,1]{1,0:T(8,128)} %reshape.115.seen_ref, bf16[384,2048]{1,0:T(8,128)(2,1)} %reshape.106.q_ref, bf16[2,128,3328]{2,1,0:T(8,128)(2,1)} %bitcast.33, bf16[2,3328,256]{2,1,0:T(8,128)(2,1)} %pad_maximum_fusion.v_ref), custom_call_target="tpu_custom_call" | custom-call | flops 10468982784 | bytes 6553600 | tf_op jit(solution)/shard_map/pallas_call | solution.py:66
  103.7 3.9 %reshape.109 = bf16[64,8,1536]{2,1,0:T(8,128)(2,1)} reshape(bf16[384,2048]{1,0:T(8,128)(2,1)} %shard_map.64) | data formatting | bytes 3145728 | tf_op jit(solution)/shard_map/reshape | solution.py:158
  107.6 6.2 %all-to-all-start.1 = ((bf16[64,8,1536]{2,1,0:T(8,128)(2,1)}), bf16[64,8,1536]{2,1,0:T(8,128)(2,1)S(1)}, u32[]{:S(2)}, u32[]{:S(2)}) async-start(bf16[64,8,1536]{2,1,0:T(8,128)(2,1)} %reshape.109), calls=%async_computation.1 | async-start | bytes 3145728 | tf_op jit(solution)/shard_map/all_to_all | solution.py:158
  113.8 39.8 %all-to-all-done.1 = bf16[64,8,1536]{2,1,0:T(8,128)(2,1)S(1)} async-done(((bf16[64,8,1536]{2,1,0:T(8,128)(2,1)}), bf16[64,8,1536]{2,1,0:T(8,128)(2,1)S(1)}, u32[]{:S(2)}, u32[]{:S(2)}) %all-to-all-start.1) | async-done | bytes 1572896 | tf_op jit(solution)/shard_map/all_to_all | solution.py:158
  153.6 2.2 %reshape.110 = bf16[384,2048]{1,0:T(8,128)(2,1)} reshape(bf16[64,8,1536]{2,1,0:T(8,128)(2,1)S(1)} %all-to-all-done.1) | data formatting | bytes 3145728 | tf_op jit(solution)/shard_map/reshape | solution.py:159
  155.8 2.8 %fusion.1 = (f32[256]{0:T(256)}, bf16[256,2048]{1,0:T(8,128)(2,1)S(1)}) fusion(bf16[384,2048]{1,0:T(8,128)(2,1)} %reshape.110, s32[256]{0:T(256)S(1)} %multiply_add_fusion), kind=kOutput, calls=%fused_computation.7 | convolution fusion | flops 404848384 | bytes 2623488 | tf_op jit(solution)/shard_map/sr,sc->rc/dot_general | solution.py:160
  158.6 6.0 %shard_map.65 = f32[1,256]{1,0:T(1,128)} custom-call(f32[1,256]{1,0:T(1,128)} %bitcast.38), custom_call_target="tpu_custom_call" | custom-call | tf_op jit(solution)/shard_map/pallas_call | solution.py:121
  165.3 1.3 fusion.3
  (22 shorter events, 4.6 us)
Async XLA Ops:
  0.0 3.1 %copy-start = (bf16[256,2048]{1,0:T(8,128)(2,1)S(1)}, bf16[256,2048]{1,0:T(8,128)(2,1)}, u32[]{:S(2)}) copy-start(bf16[256,2048]{1,0:T(8,128)(2,1)} %param.8) | copy-start | bytes 3145732
  4.8 2.9 %copy-start.4 = (s32[256]{0:T(256)S(1)}, s32[256]{0:T(256)}, u32[]{:S(2)}) copy-start(s32[256]{0:T(256)} %param.12) | copy-start | bytes 3076
  9.5 55.9 %all-to-all-start = ((bf16[64,8,1664]{2,1,0:T(8,128)(2,1)}), bf16[64,8,1664]{2,1,0:T(8,128)(2,1)}, u32[]{:S(2)}, u32[]{:S(2)}) async-start(bf16[64,8,1664]{2,1,0:T(8,128)(2,1)} %fusion.4), calls=%async_computation | async-start | bytes 3407872 | tf_op jit(solution)/shard_map/all_to_all | solution.py:154
  33.4 2.1 %copy-start.1 = (bf16[3328,2,128]{2,0,1:T(8,128)(2,1)S(1)}, bf16[3328,2,128]{2,0,1:T(8,128)(2,1)}, u32[]{:S(2)}) copy-start(bf16[3328,2,128]{2,0,1:T(8,128)(2,1)} %copy.19) | copy-start | bytes 5111812
  33.4 2.6 %copy-start.2 = (bf16[2,3328,128]{2,1,0:T(8,128)(2,1)S(1)}, bf16[2,3328,128]{2,1,0:T(8,128)(2,1)}, u32[]{:S(2)}) copy-start(bf16[2,3328,128]{2,1,0:T(8,128)(2,1)} %constant.43.clone.1) | copy-start | bytes 5111812
  107.6 6.2 %copy-start.3 = (bf16[2048]{0:T(1024)(128)(2,1)S(1)}, bf16[2048]{0:T(1024)(128)(2,1)}, u32[]{:S(2)}) copy-start(bf16[2048]{0:T(1024)(128)(2,1)} %param.13) | copy-start | bytes 12292
  107.6 46.0 %all-to-all-start.1 = ((bf16[64,8,1536]{2,1,0:T(8,128)(2,1)}), bf16[64,8,1536]{2,1,0:T(8,128)(2,1)S(1)}, u32[]{:S(2)}, u32[]{:S(2)}) async-start(bf16[64,8,1536]{2,1,0:T(8,128)(2,1)} %reshape.109), calls=%async_computation.1 | async-start | bytes 3145728 | tf_op jit(solution)/shard_map/all_to_all | solution.py:158

commit v11 on v9

--- a/solution.py
+++ b/solution.py
@@ -127,6 +127,20 @@
     )(row).reshape(part.shape)
 
 
+def to_slabs(x, docs, cap):
+    width = x.shape[1]
+    lanes = cap * width // 8
+    x3 = x.reshape(docs, cap, width)
+    tail = x3[:, :, lanes:].reshape(docs, 8 - cap, lanes)
+    return jnp.concatenate([x3[:, :, :lanes], tail], axis=1)
+
+
+def from_slabs(y, cap, width):
+    docs, _, lanes = y.shape
+    tail = y[:, cap:, :].reshape(docs, cap, width - lanes)
+    return jnp.concatenate([y[:, :cap, :], tail], axis=2).reshape(docs * cap, width)
+
+
 def shards(queries, keys, values, owner_of_row, visible, gain):
     docs = lax.axis_size("docs")
     rows = queries.shape[0]
@@ -143,15 +157,15 @@
     packed = jnp.dot(place, queries, preferred_element_type=jnp.float32).astype(jnp.bfloat16)
     seen = jnp.dot(place, visible.astype(jnp.bfloat16), preferred_element_type=jnp.float32)
     lanes = cap * width // 8
-    slabs = packed.reshape(docs, 8, lanes)
+    slabs = to_slabs(packed, docs, cap)
     seen_tile = jnp.pad(seen.astype(jnp.bfloat16).reshape(docs, 1, cap), ((0, 0), (0, 7), (0, 128 - cap)))
     sent = jnp.concatenate([slabs, seen_tile], axis=2)
     arrived = lax.all_to_all(sent, "docs", split_axis=0, concat_axis=0, tiled=True)
-    arrived_q = arrived[:, :, :lanes].reshape(docs * cap, width)
+    arrived_q = from_slabs(arrived[:, :, :lanes], cap, width)
     arrived_seen = arrived[:, 0, lanes : lanes + cap].astype(jnp.float32).reshape(docs * cap, 1)
     context = attend(arrived_q, arrived_seen, keys, values)
-    returned = lax.all_to_all(context.reshape(docs, 8, lanes), "docs", split_axis=0, concat_axis=0, tiled=True)
-    flat_back = returned.reshape(docs * cap, width)
+    returned = lax.all_to_all(to_slabs(context, docs, cap), "docs", split_axis=0, concat_axis=0, tiled=True)
+    flat_back = from_slabs(returned, cap, width)
     mine = jnp.einsum("sr,sc->rc", place, flat_back, preferred_element_type=jnp.float32).astype(
         jnp.bfloat16
     )

time: 166 us -> 179 us (1.078)
  local copies, waits for them, and re-layouts: 26.9 us -> 36.9 us
  other arithmetic: 9.34 us -> 16.5 us
  waiting for transfers between devices: 67.1 us -> 63.2 us
    concatenate x0 -> x2, other arithmetic: none -> 5.96 us  [the longest x1 3.32 us: to_slabs(): return jnp.concatenate([x3[:, :, :lanes], tail], axis=1)]
    slice x1 -> x7, local copies, waits for them, and re-layouts: 1.51 us -> 6.29 us  [the longest x2 2.55 us: to_slabs(): return jnp.concatenate([x3[:, :, :lanes], tail], axis=1)]
    concatenate x0 -> x4, local copies, waits for them, and re-layouts: none -> 4.77 us  [from_slabs(): jnp.concatenate([y[:, :cap, :], tail], axis=2).reshape(docs * cap, width)]
    all_to_all x1, waiting for transfers between devices: 27.3 us -> 23.5 us  [shards(): lax.all_to_all(sent, 'docs', split_axis=0, concat_axis=0, tiled=True)]
    reshape x4, local copies, waits for them, and re-layouts: 11.2 us -> 7.61 us  [the longest x2 4.97 us: to_slabs(): x3 = x.reshape(docs, cap, width)]
    concatenate x1, other arithmetic: 1.4 us -> 3.45 us  [shards(): sent = jnp.concatenate([slabs, seen_tile], axis=2)]
  transfers between devices with their start and end apart: 2 -> 2, of which waited for: 2 -> 2; matrix products, arithmetic and copies ran while one was open for 8% -> 11% of each run, Pallas kernels for 0% -> 0%
where the time goes in v11:
time: 179 us
  waiting for transfers between devices  63.2 us (35%)
  Pallas kernels  37.8 us (21%)
  local copies, waits for them, and re-layouts  36.9 us (21%)
  starting transfers between devices  19.4 us (11%)
  other arithmetic  16.5 us (9%)
  matrix products  4.61 us (3%)
    all_to_all x1, waiting for transfers between devices, shards(): lax.all_to_all(to_slabs(context, docs, cap), 'docs', split_axis=0, concat...  39.8 us
    pallas_call x1, Pallas kernels, attend(): pl.pallas_call(attend_kernel, grid=(kv_local, rows // tm), in_specs=[pl.B...  31.9 us
    all_to_all x1, waiting for transfers between devices, shards(): lax.all_to_all(sent, 'docs', split_axis=0, concat_axis=0, tiled=True)  23.5 us
    all_to_all x1, starting transfers between devices, shards(): lax.all_to_all(sent, 'docs', split_axis=0, concat_axis=0, tiled=True)  13.2 us
    unnamed x12, local copies, waits for them, and re-layouts  7.54 us
    all_to_all x1, starting transfers between devices, shards(): lax.all_to_all(to_slabs(context, docs, cap), 'docs', split_axis=0, concat...  6.23 us
    pallas_call x1, Pallas kernels, power_sum(): pl.pallas_call(power_kernel, in_specs=[pl.BlockSpec(memory_space=pltpu.VM...  5.96 us
    reshape x2, local copies, waits for them, and re-layouts, to_slabs(): x3 = x.reshape(docs, cap, width)  4.97 us
  transfers between devices with their start and end apart: 2, of which 2 were waited for; matrix products, arithmetic and copies ran while one was open for 11% of the time, Pallas kernels for 0%

profile of v11, /device:TPU:1, one launch (start us, length us, event | category | flops | bytes accessed | tf_op | source)
XLA Modules:
  0.0 178.5 jit_solution(13783620788699317800)
XLA Ops:
  3.1 1.7 convolution_convert_fusion
  4.8 2.5 %reshape.114 = bf16[64,6,2048]{2,1,0:T(8,128)(2,1)S(1)} reshape(bf16[384,2048]{1,0:T(8,128)(2,1)} %convolution_convert_fusion) | data formatting | bytes 3145728 | tf_op jit(solution)/shard_map/reshape | solution.py:133
  9.4 1.3 reshape.115
  11.1 3.4 %fusion.4 = bf16[64,8,1664]{2,1,0:T(8,128)(2,1)} fusion(bf16[64,1,6]{2,1,0:T(2,128)(2,1)S(1)} %reshape.125, bf16[64,2,1536]{2,1,0:T(2,128)(2,1)S(1)} %reshape.115, bf16[64,6,1536]{2,1,0:T(8,128)(2,1)} %slice.67), kind=kLoop, calls=%fused_computation.10 | loop fusion | flops 6815744 | bytes 3277568 | tf_op jit(solution)/shard_map/concatenate | solution.py:162
  14.6 13.2 %all-to-all-start = ((bf16[64,8,1664]{2,1,0:T(8,128)(2,1)}), bf16[64,8,1664]{2,1,0:T(8,128)(2,1)S(1)}, u32[]{:S(2)}, u32[]{:S(2)}) async-start(bf16[64,8,1664]{2,1,0:T(8,128)(2,1)} %fusion.4), calls=%async_computation | async-start | bytes 3407872 | tf_op jit(solution)/shard_map/all_to_all | solution.py:163
  27.8 3.8 %copy.11 = bf16[3202,256]{0,1:T(8,128)(2,1)} copy(bf16[3202,256]{1,0:T(8,128)(2,1)} %param.10) | data formatting | bytes 3278848 | tf_op args[2]
  31.5 2.7 %pad.15 = bf16[3328,256]{0,1:T(8,128)(2,1)} pad(bf16[3202,256]{0,1:T(8,128)(2,1)} %copy.11, bf16[]{:T(256)} %constant.42.clone.1), padding=0_126x0_0 | pad | bytes 3343362 | tf_op jit(solution)/shard_map/jit(_pad)/pad | solution.py:56
  34.3 3.8 %copy.12 = bf16[3328,2,128]{2,0,1:T(8,128)(2,1)} copy(bf16[3328,2,128]{0,2,1:T(8,128)(2,1)} %bitcast.32) | data formatting | bytes 3407872 | tf_op jit(solution)/shard_map/reshape | solution.py:57
  38.0 3.8 %copy.14 = bf16[3202,256]{0,1:T(8,128)(2,1)} copy(bf16[3202,256]{1,0:T(8,128)(2,1)} %param.9) | data formatting | bytes 3278848
  41.8 3.0 %pad.14.clone = bf16[3328,256]{0,1:T(8,128)(2,1)} pad(bf16[3202,256]{0,1:T(8,128)(2,1)} %copy.14, bf16[]{:T(256)} %constant.42.clone.1), padding=0_126x0_0 | pad | bytes 3343362 | tf_op jit(solution)/shard_map/jit(_pad)/pad | solution.py:54
  44.8 2.1 %pad_maximum_fusion.v_ref = bf16[2,3328,256]{2,1,0:T(8,128)(2,1)} fusion(bf16[2,3328,128]{2,1,0:T(8,128)(2,1)S(1)} %copy-done.2, bf16[2,3328,128]{2,1,0:T(8,128)(2,1)S(1)} %bitcast.33), kind=kLoop, calls=%fused_computation.1 | loop fusion | flops 6815744 | bytes 6815744 | tf_op jit(solution)/shard_map/concatenate | solution.py:59
  46.9 23.5 %all-to-all-done = bf16[64,8,1664]{2,1,0:T(8,128)(2,1)S(1)} async-done(((bf16[64,8,1664]{2,1,0:T(8,128)(2,1)}), bf16[64,8,1664]{2,1,0:T(8,128)(2,1)S(1)}, u32[]{:S(2)}, u32[]{:S(2)}) %all-to-all-start) | async-done | bytes 1703968 | tf_op jit(solution)/shard_map/all_to_all | solution.py:163
  71.6 3.1 %concatenate.32 = bf16[384,1536]{1,0:T(8,128)(2,1)} reshape(bf16[64,6,1536]{2,1,0:T(8,128)(2,1)} %slice.70) | data formatting | bytes 2359296 | tf_op jit(solution)/shard_map/concatenate | solution.py:141
  76.2 2.6 %pad_maximum_fusion.1.q_ref = bf16[384,2048]{1,0:T(8,128)(2,1)} fusion(bf16[384,512]{1,0:T(8,128)(2,1)S(1)} %concatenate.33, bf16[384,1536]{1,0:T(8,128)(2,1)} %concatenate.32), kind=kLoop, calls=%fused_computation.11 | loop fusion | flops 3145728 | bytes 3145728 | tf_op jit(solution)/shard_map/concatenate | solution.py:141
  78.9 31.9 %shard_map.64 = bf16[384,2048]{1,0:T(8,128)(2,1)} custom-call(f32[384,1]{1,0:T(8,128)} %reshape.126.seen_ref, bf16[384,2048]{1,0:T(8,128)(2,1)} %pad_maximum_fusion.1.q_ref, bf16[2,128,3328]{2,1,0:T(8,128)(2,1)} %bitcast.34, bf16[2,3328,256]{2,1,0:T(8,128)(2,1)} %pad_maximum_fusion.v_ref), custom_call_target="tpu_custom_call" | custom-call | flops 10468982784 | bytes 6553600 | tf_op jit(solution)/shard_map/pallas_call | solution.py:61
  110.7 2.5 %reshape.119 = bf16[64,6,2048]{2,1,0:T(8,128)(2,1)S(1)} reshape(bf16[384,2048]{1,0:T(8,128)(2,1)} %shard_map.64) | data formatting | bytes 3145728 | tf_op jit(solution)/shard_map/reshape | solution.py:133
  113.2 1.3 slice.72
  115.3 1.3 reshape.120
  116.7 3.3 %pad_maximum_fusion.2 = bf16[64,8,1536]{2,1,0:T(8,128)(2,1)} fusion(bf16[64,2,1536]{2,1,0:T(2,128)(2,1)S(1)} %reshape.120, bf16[64,6,1536]{2,1,0:T(8,128)(2,1)} %slice.72), kind=kLoop, calls=%fused_computation.12 | loop fusion | flops 3145728 | bytes 3145728 | tf_op jit(solution)/shard_map/concatenate | solution.py:135
  120.0 6.2 %all-to-all-start.1 = ((bf16[64,8,1536]{2,1,0:T(8,128)(2,1)}), bf16[64,8,1536]{2,1,0:T(8,128)(2,1)S(1)}, u32[]{:S(2)}, u32[]{:S(2)}) async-start(bf16[64,8,1536]{2,1,0:T(8,128)(2,1)} %pad_maximum_fusion.2), calls=%async_computation.1 | async-start | bytes 3145728 | tf_op jit(solution)/shard_map/all_to_all | solution.py:167
  126.3 39.8 %all-to-all-done.1 = bf16[64,8,1536]{2,1,0:T(8,128)(2,1)S(1)} async-done(((bf16[64,8,1536]{2,1,0:T(8,128)(2,1)}), bf16[64,8,1536]{2,1,0:T(8,128)(2,1)S(1)}, u32[]{:S(2)}, u32[]{:S(2)}) %all-to-all-start.1) | async-done | bytes 1572896 | tf_op jit(solution)/shard_map/all_to_all | solution.py:167
  167.9 2.7 %fusion.1 = (f32[256]{0:T(256)}, bf16[256,2048]{1,0:T(8,128)(2,1)S(1)}) fusion(bf16[384,512]{1,0:T(8,128)(2,1)S(1)} %concatenate.38, bf16[384,1536]{1,0:T(8,128)(2,1)} %concatenate.37, s32[256]{0:T(256)S(1)} %multiply_add_fusion), kind=kOutput, calls=%fused_computation.7 | convolution fusion | flops 407994112 | bytes 2623488 | tf_op jit(solution)/shard_map/sr,sc->rc/dot_general | solution.py:169
  170.6 6.0 %shard_map.65 = f32[1,256]{1,0:T(1,128)} custom-call(f32[1,256]{1,0:T(1,128)} %bitcast.39), custom_call_target="tpu_custom_call" | custom-call | tf_op jit(solution)/shard_map/pallas_call | solution.py:116
  177.2 1.3 fusion.3
  (34 shorter events, 11.8 us)
Async XLA Ops:
  0.0 3.1 %copy-start = (bf16[256,2048]{1,0:T(8,128)(2,1)S(1)}, bf16[256,2048]{1,0:T(8,128)(2,1)}, u32[]{:S(2)}) copy-start(bf16[256,2048]{1,0:T(8,128)(2,1)} %param.8) | copy-start | bytes 3145732
  8.6 2.2 %copy-start.4 = (s32[256]{0:T(256)S(1)}, s32[256]{0:T(256)}, u32[]{:S(2)}) copy-start(s32[256]{0:T(256)} %param.12) | copy-start | bytes 3076
  14.6 55.8 %all-to-all-start = ((bf16[64,8,1664]{2,1,0:T(8,128)(2,1)}), bf16[64,8,1664]{2,1,0:T(8,128)(2,1)S(1)}, u32[]{:S(2)}, u32[]{:S(2)}) async-start(bf16[64,8,1664]{2,1,0:T(8,128)(2,1)} %fusion.4), calls=%async_computation | async-start | bytes 3407872 | tf_op jit(solution)/shard_map/all_to_all | solution.py:163
  41.8 3.0 %copy-start.1 = (bf16[3328,2,128]{2,0,1:T(8,128)(2,1)S(1)}, bf16[3328,2,128]{2,0,1:T(8,128)(2,1)}, u32[]{:S(2)}) copy-start(bf16[3328,2,128]{2,0,1:T(8,128)(2,1)} %copy.12) | copy-start | bytes 5111812
  41.8 3.0 %copy-start.2 = (bf16[2,3328,128]{2,1,0:T(8,128)(2,1)S(1)}, bf16[2,3328,128]{2,1,0:T(8,128)(2,1)}, u32[]{:S(2)}) copy-start(bf16[2,3328,128]{2,1,0:T(8,128)(2,1)} %constant.43.clone.1) | copy-start | bytes 5111812
  120.0 6.2 %copy-start.3 = (bf16[2048]{0:T(1024)(128)(2,1)S(1)}, bf16[2048]{0:T(1024)(128)(2,1)}, u32[]{:S(2)}) copy-start(bf16[2048]{0:T(1024)(128)(2,1)} %param.13) | copy-start | bytes 12292
  120.0 46.0 %all-to-all-start.1 = ((bf16[64,8,1536]{2,1,0:T(8,128)(2,1)}), bf16[64,8,1536]{2,1,0:T(8,128)(2,1)S(1)}, u32[]{:S(2)}, u32[]{:S(2)}) async-start(bf16[64,8,1536]{2,1,0:T(8,128)(2,1)} %pad_maximum_fusion.2), calls=%async_computation.1 | async-start | bytes 3145728 | tf_op jit(solution)/shard_map/all_to_all | solution.py:167

commit v12 on v9

--- a/solution.py
+++ b/solution.py
@@ -24,13 +24,18 @@
     return jnp.sum(wide * wide, axis=-1)
 
 
-def attend_kernel(seen_ref, q_ref, k_ref, v_ref, o_ref):
+def attend_kernel(seen_ref, q_ref, k_ref, v_ref, o_ref, bias_ref):
     tm = q_ref.shape[0]
     tp = k_ref.shape[1]
     scale = 1.0 / HD**0.5
-    limit = seen_ref[...] * IMG_TOK
-    allowed = lax.broadcasted_iota(jnp.int32, (tm, tp), 1).astype(jnp.float32) < limit
-    bias = jnp.where(allowed, jnp.float32(0), jnp.float32(-1e30))
+
+    @pl.when(pl.program_id(1) == 0)
+    def _():
+        limit = seen_ref[...] * IMG_TOK
+        allowed = lax.broadcasted_iota(jnp.int32, (tm, tp), 1).astype(jnp.float32) < limit
+        bias_ref[...] = jnp.where(allowed, jnp.float32(0), jnp.float32(-1e30))
+
+    bias = bias_ref[...]
     keys = k_ref[...]
     vals = v_ref[...]
     for pair in range(0, GROUP, 4):
@@ -60,14 +65,15 @@
     tm = math.gcd(rows, 384)
     return pl.pallas_call(
         attend_kernel,
-        grid=(kv_local, rows // tm),
+        grid=(rows // tm, kv_local),
         in_specs=[
-            pl.BlockSpec((tm, 1), lambda k, i: (i, 0)),
-            pl.BlockSpec((tm, GROUP * HD), lambda k, i: (i, k)),
-            pl.BlockSpec((None, HD, padded), lambda k, i: (k, 0, 0)),
-            pl.BlockSpec((None, padded, 2 * HD), lambda k, i: (k, 0, 0)),
+            pl.BlockSpec((tm, 1), lambda i, k: (i, 0)),
+            pl.BlockSpec((tm, GROUP * HD), lambda i, k: (i, k)),
+            pl.BlockSpec((None, HD, padded), lambda i, k: (k, 0, 0)),
+            pl.BlockSpec((None, padded, 2 * HD), lambda i, k: (k, 0, 0)),
         ],
-        out_specs=pl.BlockSpec((tm, GROUP * HD), lambda k, i: (i, k)),
+        out_specs=pl.BlockSpec((tm, GROUP * HD), lambda i, k: (i, k)),
+        scratch_shapes=[pltpu.VMEM((tm, padded), jnp.float32)],
         out_shape=jax.ShapeDtypeStruct((rows, width), jnp.bfloat16),
         cost_estimate=pl.CostEstimate(
             flops=4 * rows * width * padded,

time: 166 us -> 166 us (level)
  no operation moved by 1% of the time
where the time goes in v12:
time: 166 us; the launch traced here: 165 us
  waiting for transfers between devices  67.1 us (40%)
  Pallas kernels  37.6 us (23%)
  local copies, waits for them, and re-layouts  26.9 us (16%)
  starting transfers between devices  19.5 us (12%)
  other arithmetic  9.34 us (6%)
  matrix products  4.75 us (3%)
    all_to_all x1, waiting for transfers between devices, shards(): lax.all_to_all(context.reshape(docs, 8, lanes), 'docs', split_axis=0, con...  39.8 us
    pallas_call x1, Pallas kernels, attend(): pl.pallas_call(attend_kernel, grid=(rows // tm, kv_local), in_specs=[pl.B...  31.7 us
    all_to_all x1, waiting for transfers between devices, shards(): lax.all_to_all(sent, 'docs', split_axis=0, concat_axis=0, tiled=True)  27.3 us
    all_to_all x1, starting transfers between devices, shards(): lax.all_to_all(sent, 'docs', split_axis=0, concat_axis=0, tiled=True)  13.3 us
    unnamed x12, local copies, waits for them, and re-layouts  6.68 us
    all_to_all x1, starting transfers between devices, shards(): lax.all_to_all(context.reshape(docs, 8, lanes), 'docs', split_axis=0, con...  6.22 us
    pallas_call x1, Pallas kernels, power_sum(): pl.pallas_call(power_kernel, in_specs=[pl.BlockSpec(memory_space=pltpu.VM...  5.96 us
    reshape x1, local copies, waits for them, and re-layouts, shards(): context.reshape(docs, 8, lanes)  3.87 us
  transfers between devices with their start and end apart: 2, of which 2 were waited for; matrix products, arithmetic and copies ran while one was open for 8% of the time, Pallas kernels for 0%

profile of v12, /device:TPU:1, one launch (start us, length us, event | category | flops | bytes accessed | tf_op | source)
XLA Modules:
  0.0 165.4 jit_solution(16113063263843267274)
XLA Ops:
  1.6 0.8 fusion.10
  3.1 1.7 %convolution_convert_fusion = bf16[384,2048]{1,0:T(8,128)(2,1)} fusion(bf16[256,2048]{1,0:T(8,128)(2,1)S(1)} %copy-done, s32[256]{0:T(256)S(1)} %multiply_add_fusion), kind=kOutput, calls=%fused_computation.3 | convolution fusion | flops 403537920 | bytes 2622464 | tf_op jit(solution)/shard_map/dot_general | solution.py:149
  4.8 2.9 %reshape.104 = bf16[64,8,1536]{2,1,0:T(8,128)(2,1)S(1)} reshape(bf16[384,2048]{1,0:T(8,128)(2,1)} %convolution_convert_fusion) | data formatting | bytes 3145728 | tf_op jit(solution)/shard_map/reshape | solution.py:152
  8.1 1.4 fusion.4
  9.5 13.3 %all-to-all-start = ((bf16[64,8,1664]{2,1,0:T(8,128)(2,1)}), bf16[64,8,1664]{2,1,0:T(8,128)(2,1)}, u32[]{:S(2)}, u32[]{:S(2)}) async-start(bf16[64,8,1664]{2,1,0:T(8,128)(2,1)} %fusion.4), calls=%async_computation | async-start | bytes 3407872 | tf_op jit(solution)/shard_map/all_to_all | solution.py:155
  22.9 2.7 %copy.18 = bf16[3202,256]{0,1:T(8,128)(2,1)S(1)} copy(bf16[3202,256]{1,0:T(8,128)(2,1)} %param.10) | data formatting | bytes 3278848 | tf_op args[2]
  25.6 1.3 pad.15
  26.9 3.8 %copy.19 = bf16[3328,2,128]{2,0,1:T(8,128)(2,1)} copy(bf16[3328,2,128]{0,2,1:T(8,128)(2,1)} %bitcast.31) | data formatting | bytes 3407872 | tf_op jit(solution)/shard_map/reshape | solution.py:62
  30.7 2.7 %copy.22 = bf16[3202,256]{0,1:T(8,128)(2,1)S(1)} copy(bf16[3202,256]{1,0:T(8,128)(2,1)} %param.9) | data formatting | bytes 3278848
  33.4 1.3 pad.14.clone
  36.0 2.1 %pad_maximum_fusion.v_ref = bf16[2,3328,256]{2,1,0:T(8,128)(2,1)} fusion(bf16[2,3328,128]{2,1,0:T(8,128)(2,1)S(1)} %copy-done.2, bf16[2,3328,128]{2,1,0:T(8,128)(2,1)S(1)} %bitcast.32), kind=kLoop, calls=%fused_computation.1 | loop fusion | flops 6815744 | bytes 6815744 | tf_op jit(solution)/shard_map/concatenate | solution.py:64
  38.1 27.3 %all-to-all-done = bf16[64,8,1664]{2,1,0:T(8,128)(2,1)} async-done(((bf16[64,8,1664]{2,1,0:T(8,128)(2,1)}), bf16[64,8,1664]{2,1,0:T(8,128)(2,1)}, u32[]{:S(2)}, u32[]{:S(2)}) %all-to-all-start) | async-done | bytes 1703968 | tf_op jit(solution)/shard_map/all_to_all | solution.py:155
  65.4 1.5 slice.37
  66.9 2.2 %reshape.106.q_ref = bf16[384,2048]{1,0:T(8,128)(2,1)} reshape(bf16[64,8,1536]{2,1,0:T(8,128)(2,1)S(1)} %slice.37) | data formatting | bytes 3145728 | tf_op jit(solution)/shard_map/reshape | solution.py:156
  69.1 1.0 fusion.12
  70.1 0.8 reshape.115.seen_ref
  70.9 31.7 %shard_map.64 = bf16[384,2048]{1,0:T(8,128)(2,1)} custom-call(f32[384,1]{1,0:T(8,128)} %reshape.115.seen_ref, bf16[384,2048]{1,0:T(8,128)(2,1)} %reshape.106.q_ref, bf16[2,128,3328]{2,1,0:T(8,128)(2,1)} %bitcast.33, bf16[2,3328,256]{2,1,0:T(8,128)(2,1)} %pad_maximum_fusion.v_ref), custom_call_target="tpu_custom_call" | custom-call | flops 10468982784 | bytes 6553600 | tf_op jit(solution)/shard_map/pallas_call | solution.py:66
  102.6 3.9 %reshape.109 = bf16[64,8,1536]{2,1,0:T(8,128)(2,1)} reshape(bf16[384,2048]{1,0:T(8,128)(2,1)} %shard_map.64) | data formatting | bytes 3145728 | tf_op jit(solution)/shard_map/reshape | solution.py:159
  106.4 6.2 %all-to-all-start.1 = ((bf16[64,8,1536]{2,1,0:T(8,128)(2,1)}), bf16[64,8,1536]{2,1,0:T(8,128)(2,1)S(1)}, u32[]{:S(2)}, u32[]{:S(2)}) async-start(bf16[64,8,1536]{2,1,0:T(8,128)(2,1)} %reshape.109), calls=%async_computation.1 | async-start | bytes 3145728 | tf_op jit(solution)/shard_map/all_to_all | solution.py:159
  112.7 39.8 %all-to-all-done.1 = bf16[64,8,1536]{2,1,0:T(8,128)(2,1)S(1)} async-done(((bf16[64,8,1536]{2,1,0:T(8,128)(2,1)}), bf16[64,8,1536]{2,1,0:T(8,128)(2,1)S(1)}, u32[]{:S(2)}, u32[]{:S(2)}) %all-to-all-start.1) | async-done | bytes 1572896 | tf_op jit(solution)/shard_map/all_to_all | solution.py:159
  152.5 2.2 %reshape.110 = bf16[384,2048]{1,0:T(8,128)(2,1)} reshape(bf16[64,8,1536]{2,1,0:T(8,128)(2,1)S(1)} %all-to-all-done.1) | data formatting | bytes 3145728 | tf_op jit(solution)/shard_map/reshape | solution.py:160
  154.7 2.8 %fusion.1 = (f32[256]{0:T(256)}, bf16[256,2048]{1,0:T(8,128)(2,1)S(1)}) fusion(bf16[384,2048]{1,0:T(8,128)(2,1)} %reshape.110, s32[256]{0:T(256)S(1)} %multiply_add_fusion), kind=kOutput, calls=%fused_computation.7 | convolution fusion | flops 404848384 | bytes 2623488 | tf_op jit(solution)/shard_map/sr,sc->rc/dot_general | solution.py:161
  157.5 6.0 %shard_map.65 = f32[1,256]{1,0:T(1,128)} custom-call(f32[1,256]{1,0:T(1,128)} %bitcast.38), custom_call_target="tpu_custom_call" | custom-call | tf_op jit(solution)/shard_map/pallas_call | solution.py:122
  164.1 1.3 fusion.3
  (22 shorter events, 4.6 us)
Async XLA Ops:
  0.0 3.1 %copy-start = (bf16[256,2048]{1,0:T(8,128)(2,1)S(1)}, bf16[256,2048]{1,0:T(8,128)(2,1)}, u32[]{:S(2)}) copy-start(bf16[256,2048]{1,0:T(8,128)(2,1)} %param.8) | copy-start | bytes 3145732
  4.8 2.9 %copy-start.4 = (s32[256]{0:T(256)S(1)}, s32[256]{0:T(256)}, u32[]{:S(2)}) copy-start(s32[256]{0:T(256)} %param.12) | copy-start | bytes 3076
  9.5 55.9 %all-to-all-start = ((bf16[64,8,1664]{2,1,0:T(8,128)(2,1)}), bf16[64,8,1664]{2,1,0:T(8,128)(2,1)}, u32[]{:S(2)}, u32[]{:S(2)}) async-start(bf16[64,8,1664]{2,1,0:T(8,128)(2,1)} %fusion.4), calls=%async_computation | async-start | bytes 3407872 | tf_op jit(solution)/shard_map/all_to_all | solution.py:155
  33.4 2.1 %copy-start.1 = (bf16[3328,2,128]{2,0,1:T(8,128)(2,1)S(1)}, bf16[3328,2,128]{2,0,1:T(8,128)(2,1)}, u32[]{:S(2)}) copy-start(bf16[3328,2,128]{2,0,1:T(8,128)(2,1)} %copy.19) | copy-start | bytes 5111812
  33.4 2.6 %copy-start.2 = (bf16[2,3328,128]{2,1,0:T(8,128)(2,1)S(1)}, bf16[2,3328,128]{2,1,0:T(8,128)(2,1)}, u32[]{:S(2)}) copy-start(bf16[2,3328,128]{2,1,0:T(8,128)(2,1)} %constant.43.clone.1) | copy-start | bytes 5111812
  106.4 6.2 %copy-start.3 = (bf16[2048]{0:T(1024)(128)(2,1)S(1)}, bf16[2048]{0:T(1024)(128)(2,1)}, u32[]{:S(2)}) copy-start(bf16[2048]{0:T(1024)(128)(2,1)} %param.13) | copy-start | bytes 12292
  106.4 46.0 %all-to-all-start.1 = ((bf16[64,8,1536]{2,1,0:T(8,128)(2,1)}), bf16[64,8,1536]{2,1,0:T(8,128)(2,1)S(1)}, u32[]{:S(2)}, u32[]{:S(2)}) async-start(bf16[64,8,1536]{2,1,0:T(8,128)(2,1)} %reshape.109), calls=%async_computation.1 | async-start | bytes 3145728 | tf_op jit(solution)/shard_map/all_to_all | solution.py:159

commit v13 on v12

--- a/solution.py
+++ b/solution.py
@@ -31,9 +31,10 @@
 
     @pl.when(pl.program_id(1) == 0)
     def _():
-        limit = seen_ref[...] * IMG_TOK
-        allowed = lax.broadcasted_iota(jnp.int32, (tm, tp), 1).astype(jnp.float32) < limit
-        bias_ref[...] = jnp.where(allowed, jnp.float32(0), jnp.float32(-1e30))
+        token = lax.broadcasted_iota(jnp.int32, (1, tp), 1)
+        rows_of = [jnp.where(token < n * IMG_TOK, jnp.float32(0), jnp.float32(-1e30)) for n in range(3)]
+        seen = seen_ref[...]
+        bias_ref[...] = jnp.where(seen > 1.5, rows_of[2], jnp.where(seen > 0.5, rows_of[1], rows_of[0]))
 
     bias = bias_ref[...]
     keys = k_ref[...]

time: 166 us -> 166 us (level)
  no operation moved by 1% of the time
where the time goes in v13:
time: 166 us; the launch traced here: 165 us
  waiting for transfers between devices  67.1 us (40%)
  Pallas kernels  37.7 us (23%)
  local copies, waits for them, and re-layouts  26.9 us (16%)
  starting transfers between devices  19.6 us (12%)
  other arithmetic  9.34 us (6%)
  matrix products  4.75 us (3%)
    all_to_all x1, waiting for transfers between devices, shards(): lax.all_to_all(context.reshape(docs, 8, lanes), 'docs', split_axis=0, con...  39.8 us
    pallas_call x1, Pallas kernels, attend(): pl.pallas_call(attend_kernel, grid=(rows // tm, kv_local), in_specs=[pl.B...  31.7 us
    all_to_all x1, waiting for transfers between devices, shards(): lax.all_to_all(sent, 'docs', split_axis=0, concat_axis=0, tiled=True)  27.3 us
    all_to_all x1, starting transfers between devices, shards(): lax.all_to_all(sent, 'docs', split_axis=0, concat_axis=0, tiled=True)  13.3 us
    unnamed x12, local copies, waits for them, and re-layouts  6.68 us
    all_to_all x1, starting transfers between devices, shards(): lax.all_to_all(context.reshape(docs, 8, lanes), 'docs', split_axis=0, con...  6.24 us
    pallas_call x1, Pallas kernels, power_sum(): pl.pallas_call(power_kernel, in_specs=[pl.BlockSpec(memory_space=pltpu.VM...  5.96 us
    reshape x1, local copies, waits for them, and re-layouts, shards(): context.reshape(docs, 8, lanes)  3.87 us
  transfers between devices with their start and end apart: 2, of which 2 were waited for; matrix products, arithmetic and copies ran while one was open for 8% of the time, Pallas kernels for 0%

profile of v13, /device:TPU:1, one launch (start us, length us, event | category | flops | bytes accessed | tf_op | source)
XLA Modules:
  0.0 165.5 jit_solution(1860578824640133421)
XLA Ops:
  1.6 0.8 fusion.10
  3.1 1.7 %convolution_convert_fusion = bf16[384,2048]{1,0:T(8,128)(2,1)} fusion(bf16[256,2048]{1,0:T(8,128)(2,1)S(1)} %copy-done, s32[256]{0:T(256)S(1)} %multiply_add_fusion), kind=kOutput, calls=%fused_computation.3 | convolution fusion | flops 403537920 | bytes 2622464 | tf_op jit(solution)/shard_map/dot_general | solution.py:150
  4.8 2.9 %reshape.104 = bf16[64,8,1536]{2,1,0:T(8,128)(2,1)S(1)} reshape(bf16[384,2048]{1,0:T(8,128)(2,1)} %convolution_convert_fusion) | data formatting | bytes 3145728 | tf_op jit(solution)/shard_map/reshape | solution.py:153
  8.1 1.4 fusion.4
  9.5 13.3 %all-to-all-start = ((bf16[64,8,1664]{2,1,0:T(8,128)(2,1)}), bf16[64,8,1664]{2,1,0:T(8,128)(2,1)}, u32[]{:S(2)}, u32[]{:S(2)}) async-start(bf16[64,8,1664]{2,1,0:T(8,128)(2,1)} %fusion.4), calls=%async_computation | async-start | bytes 3407872 | tf_op jit(solution)/shard_map/all_to_all | solution.py:156
  22.9 2.7 %copy.18 = bf16[3202,256]{0,1:T(8,128)(2,1)S(1)} copy(bf16[3202,256]{1,0:T(8,128)(2,1)} %param.10) | data formatting | bytes 3278848 | tf_op args[2]
  25.6 1.3 pad.15
  26.9 3.8 %copy.19 = bf16[3328,2,128]{2,0,1:T(8,128)(2,1)} copy(bf16[3328,2,128]{0,2,1:T(8,128)(2,1)} %bitcast.31) | data formatting | bytes 3407872 | tf_op jit(solution)/shard_map/reshape | solution.py:63
  30.7 2.7 %copy.22 = bf16[3202,256]{0,1:T(8,128)(2,1)S(1)} copy(bf16[3202,256]{1,0:T(8,128)(2,1)} %param.9) | data formatting | bytes 3278848
  33.4 1.3 pad.14.clone
  36.0 2.1 %pad_maximum_fusion.v_ref = bf16[2,3328,256]{2,1,0:T(8,128)(2,1)} fusion(bf16[2,3328,128]{2,1,0:T(8,128)(2,1)S(1)} %copy-done.2, bf16[2,3328,128]{2,1,0:T(8,128)(2,1)S(1)} %bitcast.32), kind=kLoop, calls=%fused_computation.1 | loop fusion | flops 6815744 | bytes 6815744 | tf_op jit(solution)/shard_map/concatenate | solution.py:65
  38.1 27.3 %all-to-all-done = bf16[64,8,1664]{2,1,0:T(8,128)(2,1)} async-done(((bf16[64,8,1664]{2,1,0:T(8,128)(2,1)}), bf16[64,8,1664]{2,1,0:T(8,128)(2,1)}, u32[]{:S(2)}, u32[]{:S(2)}) %all-to-all-start) | async-done | bytes 1703968 | tf_op jit(solution)/shard_map/all_to_all | solution.py:156
  65.4 1.5 slice.37
  66.9 2.2 %reshape.106.q_ref = bf16[384,2048]{1,0:T(8,128)(2,1)} reshape(bf16[64,8,1536]{2,1,0:T(8,128)(2,1)S(1)} %slice.37) | data formatting | bytes 3145728 | tf_op jit(solution)/shard_map/reshape | solution.py:157
  69.1 1.0 fusion.12
  70.1 0.8 reshape.115.seen_ref
  70.9 31.7 %shard_map.64 = bf16[384,2048]{1,0:T(8,128)(2,1)} custom-call(f32[384,1]{1,0:T(8,128)} %reshape.115.seen_ref, bf16[384,2048]{1,0:T(8,128)(2,1)} %reshape.106.q_ref, bf16[2,128,3328]{2,1,0:T(8,128)(2,1)} %bitcast.33, bf16[2,3328,256]{2,1,0:T(8,128)(2,1)} %pad_maximum_fusion.v_ref), custom_call_target="tpu_custom_call" | custom-call | flops 10468982784 | bytes 6553600 | tf_op jit(solution)/shard_map/pallas_call | solution.py:67
  102.6 3.9 %reshape.109 = bf16[64,8,1536]{2,1,0:T(8,128)(2,1)} reshape(bf16[384,2048]{1,0:T(8,128)(2,1)} %shard_map.64) | data formatting | bytes 3145728 | tf_op jit(solution)/shard_map/reshape | solution.py:160
  106.5 6.2 %all-to-all-start.1 = ((bf16[64,8,1536]{2,1,0:T(8,128)(2,1)}), bf16[64,8,1536]{2,1,0:T(8,128)(2,1)S(1)}, u32[]{:S(2)}, u32[]{:S(2)}) async-start(bf16[64,8,1536]{2,1,0:T(8,128)(2,1)} %reshape.109), calls=%async_computation.1 | async-start | bytes 3145728 | tf_op jit(solution)/shard_map/all_to_all | solution.py:160
  112.8 39.8 %all-to-all-done.1 = bf16[64,8,1536]{2,1,0:T(8,128)(2,1)S(1)} async-done(((bf16[64,8,1536]{2,1,0:T(8,128)(2,1)}), bf16[64,8,1536]{2,1,0:T(8,128)(2,1)S(1)}, u32[]{:S(2)}, u32[]{:S(2)}) %all-to-all-start.1) | async-done | bytes 1572896 | tf_op jit(solution)/shard_map/all_to_all | solution.py:160
  152.5 2.2 %reshape.110 = bf16[384,2048]{1,0:T(8,128)(2,1)} reshape(bf16[64,8,1536]{2,1,0:T(8,128)(2,1)S(1)} %all-to-all-done.1) | data formatting | bytes 3145728 | tf_op jit(solution)/shard_map/reshape | solution.py:161
  154.7 2.8 %fusion.1 = (f32[256]{0:T(256)}, bf16[256,2048]{1,0:T(8,128)(2,1)S(1)}) fusion(bf16[384,2048]{1,0:T(8,128)(2,1)} %reshape.110, s32[256]{0:T(256)S(1)} %multiply_add_fusion), kind=kOutput, calls=%fused_computation.7 | convolution fusion | flops 404848384 | bytes 2623488 | tf_op jit(solution)/shard_map/sr,sc->rc/dot_general | solution.py:162
  157.5 6.0 %shard_map.65 = f32[1,256]{1,0:T(1,128)} custom-call(f32[1,256]{1,0:T(1,128)} %bitcast.38), custom_call_target="tpu_custom_call" | custom-call | tf_op jit(solution)/shard_map/pallas_call | solution.py:123
  164.2 1.3 fusion.3
  (22 shorter events, 4.6 us)
Async XLA Ops:
  0.0 3.1 %copy-start = (bf16[256,2048]{1,0:T(8,128)(2,1)S(1)}, bf16[256,2048]{1,0:T(8,128)(2,1)}, u32[]{:S(2)}) copy-start(bf16[256,2048]{1,0:T(8,128)(2,1)} %param.8) | copy-start | bytes 3145732
  4.8 2.9 %copy-start.4 = (s32[256]{0:T(256)S(1)}, s32[256]{0:T(256)}, u32[]{:S(2)}) copy-start(s32[256]{0:T(256)} %param.12) | copy-start | bytes 3076
  9.5 55.9 %all-to-all-start = ((bf16[64,8,1664]{2,1,0:T(8,128)(2,1)}), bf16[64,8,1664]{2,1,0:T(8,128)(2,1)}, u32[]{:S(2)}, u32[]{:S(2)}) async-start(bf16[64,8,1664]{2,1,0:T(8,128)(2,1)} %fusion.4), calls=%async_computation | async-start | bytes 3407872 | tf_op jit(solution)/shard_map/all_to_all | solution.py:156
  33.4 2.1 %copy-start.1 = (bf16[3328,2,128]{2,0,1:T(8,128)(2,1)S(1)}, bf16[3328,2,128]{2,0,1:T(8,128)(2,1)}, u32[]{:S(2)}) copy-start(bf16[3328,2,128]{2,0,1:T(8,128)(2,1)} %copy.19) | copy-start | bytes 5111812
  33.4 2.6 %copy-start.2 = (bf16[2,3328,128]{2,1,0:T(8,128)(2,1)S(1)}, bf16[2,3328,128]{2,1,0:T(8,128)(2,1)}, u32[]{:S(2)}) copy-start(bf16[2,3328,128]{2,1,0:T(8,128)(2,1)} %constant.43.clone.1) | copy-start | bytes 5111812
  106.5 6.3 %copy-start.3 = (bf16[2048]{0:T(1024)(128)(2,1)S(1)}, bf16[2048]{0:T(1024)(128)(2,1)}, u32[]{:S(2)}) copy-start(bf16[2048]{0:T(1024)(128)(2,1)} %param.13) | copy-start | bytes 12292
  106.5 46.0 %all-to-all-start.1 = ((bf16[64,8,1536]{2,1,0:T(8,128)(2,1)}), bf16[64,8,1536]{2,1,0:T(8,128)(2,1)S(1)}, u32[]{:S(2)}, u32[]{:S(2)}) async-start(bf16[64,8,1536]{2,1,0:T(8,128)(2,1)} %reshape.109), calls=%async_computation.1 | async-start | bytes 3145728 | tf_op jit(solution)/shard_map/all_to_all | solution.py:160

commit v14 on v12

--- a/solution.py
+++ b/solution.py
@@ -62,7 +62,7 @@
     vp = vp.reshape(padded, kv_local, HD).transpose(1, 0, 2)
     ones = jnp.zeros((kv_local, padded, HD), vp.dtype).at[:, :, 0].set(1)
     vp = jnp.concatenate([vp, ones], axis=2)
-    tm = math.gcd(rows, 384)
+    tm = math.gcd(rows, 192)
     return pl.pallas_call(
         attend_kernel,
         grid=(rows // tm, kv_local),

time: 166 us -> 166 us (level)
  no operation moved by 1% of the time
where the time goes in v14:
time: 166 us; the launch traced here: 165 us
  waiting for transfers between devices  67.1 us (40%)
  Pallas kernels  37.6 us (23%)
  local copies, waits for them, and re-layouts  26.9 us (16%)
  starting transfers between devices  19.6 us (12%)
  other arithmetic  9.34 us (6%)
  matrix products  4.75 us (3%)
    all_to_all x1, waiting for transfers between devices, shards(): lax.all_to_all(context.reshape(docs, 8, lanes), 'docs', split_axis=0, con...  39.8 us
    pallas_call x1, Pallas kernels, attend(): pl.pallas_call(attend_kernel, grid=(rows // tm, kv_local), in_specs=[pl.B...  31.7 us
    all_to_all x1, waiting for transfers between devices, shards(): lax.all_to_all(sent, 'docs', split_axis=0, concat_axis=0, tiled=True)  27.3 us
    all_to_all x1, starting transfers between devices, shards(): lax.all_to_all(sent, 'docs', split_axis=0, concat_axis=0, tiled=True)  13.3 us
    unnamed x12, local copies, waits for them, and re-layouts  6.68 us
    all_to_all x1, starting transfers between devices, shards(): lax.all_to_all(context.reshape(docs, 8, lanes), 'docs', split_axis=0, con...  6.22 us
    pallas_call x1, Pallas kernels, power_sum(): pl.pallas_call(power_kernel, in_specs=[pl.BlockSpec(memory_space=pltpu.VM...  5.97 us
    reshape x1, local copies, waits for them, and re-layouts, shards(): context.reshape(docs, 8, lanes)  3.87 us
  transfers between devices with their start and end apart: 2, of which 2 were waited for; matrix products, arithmetic and copies ran while one was open for 8% of the time, Pallas kernels for 0%

profile of v14, /device:TPU:1, one launch (start us, length us, event | category | flops | bytes accessed | tf_op | source)
XLA Modules:
  0.0 165.4 jit_solution(10179646810224243912)
XLA Ops:
  1.6 0.8 fusion.10
  3.1 1.7 %convolution_convert_fusion = bf16[384,2048]{1,0:T(8,128)(2,1)} fusion(bf16[256,2048]{1,0:T(8,128)(2,1)S(1)} %copy-done, s32[256]{0:T(256)S(1)} %multiply_add_fusion), kind=kOutput, calls=%fused_computation.3 | convolution fusion | flops 403537920 | bytes 2622464 | tf_op jit(solution)/shard_map/dot_general | solution.py:149
  4.8 2.9 %reshape.104 = bf16[64,8,1536]{2,1,0:T(8,128)(2,1)S(1)} reshape(bf16[384,2048]{1,0:T(8,128)(2,1)} %convolution_convert_fusion) | data formatting | bytes 3145728 | tf_op jit(solution)/shard_map/reshape | solution.py:152
  8.1 1.4 fusion.4
  9.5 13.3 %all-to-all-start = ((bf16[64,8,1664]{2,1,0:T(8,128)(2,1)}), bf16[64,8,1664]{2,1,0:T(8,128)(2,1)}, u32[]{:S(2)}, u32[]{:S(2)}) async-start(bf16[64,8,1664]{2,1,0:T(8,128)(2,1)} %fusion.4), calls=%async_computation | async-start | bytes 3407872 | tf_op jit(solution)/shard_map/all_to_all | solution.py:155
  22.9 2.7 %copy.18 = bf16[3202,256]{0,1:T(8,128)(2,1)S(1)} copy(bf16[3202,256]{1,0:T(8,128)(2,1)} %param.10) | data formatting | bytes 3278848 | tf_op args[2]
  25.6 1.3 pad.15
  26.9 3.8 %copy.19 = bf16[3328,2,128]{2,0,1:T(8,128)(2,1)} copy(bf16[3328,2,128]{0,2,1:T(8,128)(2,1)} %bitcast.31) | data formatting | bytes 3407872 | tf_op jit(solution)/shard_map/reshape | solution.py:62
  30.7 2.7 %copy.22 = bf16[3202,256]{0,1:T(8,128)(2,1)S(1)} copy(bf16[3202,256]{1,0:T(8,128)(2,1)} %param.9) | data formatting | bytes 3278848
  33.4 1.3 pad.14.clone
  36.0 2.1 %pad_maximum_fusion.v_ref = bf16[2,3328,256]{2,1,0:T(8,128)(2,1)} fusion(bf16[2,3328,128]{2,1,0:T(8,128)(2,1)S(1)} %copy-done.2, bf16[2,3328,128]{2,1,0:T(8,128)(2,1)S(1)} %bitcast.32), kind=kLoop, calls=%fused_computation.1 | loop fusion | flops 6815744 | bytes 6815744 | tf_op jit(solution)/shard_map/concatenate | solution.py:64
  38.1 27.3 %all-to-all-done = bf16[64,8,1664]{2,1,0:T(8,128)(2,1)} async-done(((bf16[64,8,1664]{2,1,0:T(8,128)(2,1)}), bf16[64,8,1664]{2,1,0:T(8,128)(2,1)}, u32[]{:S(2)}, u32[]{:S(2)}) %all-to-all-start) | async-done | bytes 1703968 | tf_op jit(solution)/shard_map/all_to_all | solution.py:155
  65.4 1.5 slice.37
  66.9 2.2 %reshape.106.q_ref = bf16[384,2048]{1,0:T(8,128)(2,1)} reshape(bf16[64,8,1536]{2,1,0:T(8,128)(2,1)S(1)} %slice.37) | data formatting | bytes 3145728 | tf_op jit(solution)/shard_map/reshape | solution.py:156
  69.1 1.0 fusion.12
  70.1 0.8 reshape.115.seen_ref
  70.9 31.7 %shard_map.64 = bf16[384,2048]{1,0:T(8,128)(2,1)} custom-call(f32[384,1]{1,0:T(8,128)} %reshape.115.seen_ref, bf16[384,2048]{1,0:T(8,128)(2,1)} %reshape.106.q_ref, bf16[2,128,3328]{2,1,0:T(8,128)(2,1)} %bitcast.33, bf16[2,3328,256]{2,1,0:T(8,128)(2,1)} %pad_maximum_fusion.v_ref), custom_call_target="tpu_custom_call" | custom-call | flops 10468982784 | bytes 6553600 | tf_op jit(solution)/shard_map/pallas_call | solution.py:66
  102.6 3.9 %reshape.109 = bf16[64,8,1536]{2,1,0:T(8,128)(2,1)} reshape(bf16[384,2048]{1,0:T(8,128)(2,1)} %shard_map.64) | data formatting | bytes 3145728 | tf_op jit(solution)/shard_map/reshape | solution.py:159
  106.4 6.2 %all-to-all-start.1 = ((bf16[64,8,1536]{2,1,0:T(8,128)(2,1)}), bf16[64,8,1536]{2,1,0:T(8,128)(2,1)S(1)}, u32[]{:S(2)}, u32[]{:S(2)}) async-start(bf16[64,8,1536]{2,1,0:T(8,128)(2,1)} %reshape.109), calls=%async_computation.1 | async-start | bytes 3145728 | tf_op jit(solution)/shard_map/all_to_all | solution.py:159
  112.7 39.8 %all-to-all-done.1 = bf16[64,8,1536]{2,1,0:T(8,128)(2,1)S(1)} async-done(((bf16[64,8,1536]{2,1,0:T(8,128)(2,1)}), bf16[64,8,1536]{2,1,0:T(8,128)(2,1)S(1)}, u32[]{:S(2)}, u32[]{:S(2)}) %all-to-all-start.1) | async-done | bytes 1572896 | tf_op jit(solution)/shard_map/all_to_all | solution.py:159
  152.5 2.2 %reshape.110 = bf16[384,2048]{1,0:T(8,128)(2,1)} reshape(bf16[64,8,1536]{2,1,0:T(8,128)(2,1)S(1)} %all-to-all-done.1) | data formatting | bytes 3145728 | tf_op jit(solution)/shard_map/reshape | solution.py:160
  154.7 2.8 %fusion.1 = (f32[256]{0:T(256)}, bf16[256,2048]{1,0:T(8,128)(2,1)S(1)}) fusion(bf16[384,2048]{1,0:T(8,128)(2,1)} %reshape.110, s32[256]{0:T(256)S(1)} %multiply_add_fusion), kind=kOutput, calls=%fused_computation.7 | convolution fusion | flops 404848384 | bytes 2623488 | tf_op jit(solution)/shard_map/sr,sc->rc/dot_general | solution.py:161
  157.5 6.0 %shard_map.65 = f32[1,256]{1,0:T(1,128)} custom-call(f32[1,256]{1,0:T(1,128)} %bitcast.38), custom_call_target="tpu_custom_call" | custom-call | tf_op jit(solution)/shard_map/pallas_call | solution.py:122
  164.1 1.3 fusion.3
  (22 shorter events, 4.6 us)
Async XLA Ops:
  0.0 3.1 %copy-start = (bf16[256,2048]{1,0:T(8,128)(2,1)S(1)}, bf16[256,2048]{1,0:T(8,128)(2,1)}, u32[]{:S(2)}) copy-start(bf16[256,2048]{1,0:T(8,128)(2,1)} %param.8) | copy-start | bytes 3145732
  4.8 2.9 %copy-start.4 = (s32[256]{0:T(256)S(1)}, s32[256]{0:T(256)}, u32[]{:S(2)}) copy-start(s32[256]{0:T(256)} %param.12) | copy-start | bytes 3076
  9.5 55.9 %all-to-all-start = ((bf16[64,8,1664]{2,1,0:T(8,128)(2,1)}), bf16[64,8,1664]{2,1,0:T(8,128)(2,1)}, u32[]{:S(2)}, u32[]{:S(2)}) async-start(bf16[64,8,1664]{2,1,0:T(8,128)(2,1)} %fusion.4), calls=%async_computation | async-start | bytes 3407872 | tf_op jit(solution)/shard_map/all_to_all | solution.py:155
  33.4 2.1 %copy-start.1 = (bf16[3328,2,128]{2,0,1:T(8,128)(2,1)S(1)}, bf16[3328,2,128]{2,0,1:T(8,128)(2,1)}, u32[]{:S(2)}) copy-start(bf16[3328,2,128]{2,0,1:T(8,128)(2,1)} %copy.19) | copy-start | bytes 5111812
  33.4 2.6 %copy-start.2 = (bf16[2,3328,128]{2,1,0:T(8,128)(2,1)S(1)}, bf16[2,3328,128]{2,1,0:T(8,128)(2,1)}, u32[]{:S(2)}) copy-start(bf16[2,3328,128]{2,1,0:T(8,128)(2,1)} %constant.43.clone.1) | copy-start | bytes 5111812
  106.4 6.2 %copy-start.3 = (bf16[2048]{0:T(1024)(128)(2,1)S(1)}, bf16[2048]{0:T(1024)(128)(2,1)}, u32[]{:S(2)}) copy-start(bf16[2048]{0:T(1024)(128)(2,1)} %param.13) | copy-start | bytes 12292
  106.4 46.0 %all-to-all-start.1 = ((bf16[64,8,1536]{2,1,0:T(8,128)(2,1)}), bf16[64,8,1536]{2,1,0:T(8,128)(2,1)S(1)}, u32[]{:S(2)}, u32[]{:S(2)}) async-start(bf16[64,8,1536]{2,1,0:T(8,128)(2,1)} %reshape.109), calls=%async_computation.1 | async-start | bytes 3145728 | tf_op jit(solution)/shard_map/all_to_all | solution.py:159
